TPU v7x, 32 devices: a whole 2x2x4 slice. The times are simulated.
32 devices in a mesh: dp: 2 (over x), ctx: 16 (over z, y, core).
Axes of the slice: x: 2, y: 2, z: 4, core: 2. Of those that a mesh axis runs over, the one named last changes fastest.
Arguments:
- token_ids: int32 [2, 2048], P('dp', 'ctx'), may hold values from 0 to 7
- queries: bfloat16 [2, 2048, 4096], P('dp', 'ctx'), may hold values from -6 to 6
- gated_values: bfloat16 [2, 2048, 4096], P('dp', 'ctx'), may hold values from -6 to 6
- out_grad: bfloat16 [2, 2048, 4096], P('dp', 'ctx'), may hold values from -6 to 6
- filters: bfloat16 [4096, 128], P('ctx'), may hold values from -0.5 to 0.5
Outputs:
- value_grad: bfloat16 [2, 2048, 4096], P('dp', 'ctx')
- filter_grad: float32 [4096, 128], P('ctx')
Inputs may be any that keep to these rules, and one draw needn't show every extreme that they name: `token_ids`: ids 0 to 3 are upper-case bases, 4 to 7 lower-case bases.
All inputs are finite; a program needn't handle non-finite values.
Results may differ from a plain program's by a relative error of at most 0.0049.
Values may be sent and summed in bfloat16 or wider, within the bound.
No kernel may reach another device: no remote copies, remote signals or barrier semaphores. Data moves between devices by JAX's collectives and lax.ppermute only.
A program may use at most 64 MiB of HBM per device.

v0:
```python
import jax
import jax.numpy as jnp
from jax import lax
from jax.sharding import PartitionSpec as P


def shifted(x, axis, by):
    length = lax.axis_size(axis)
    pairs = [(i, i + by) for i in range(length) if 0 <= i + by < length]
    return lax.ppermute(x, axis, pairs)


def correlate(signal, kernel):
    channels = signal.shape[2]
    return lax.conv_general_dilated(
        signal,
        kernel[:, None, :],
        (1,),
        "VALID",
        dimension_numbers=("NWC", "WIO", "NWC"),
        feature_group_count=channels,
        preferred_element_type=jnp.float32,
    )


def body(token_ids, queries, gated_values, out_grad, filters):
    weight = jnp.where(token_ids < 4, 1.0, 0.1).astype(jnp.float32)
    cotangent = (
        weight[:, :, None] * out_grad.astype(jnp.float32) * queries.astype(jnp.float32)
    ).astype(jnp.bfloat16)
    tap_count = filters.shape[1]
    token_total = lax.axis_size("dp") * lax.axis_size("ctx") * queries.shape[1]
    factor_tok = float(token_total) ** (-0.5)
    next_part = shifted(cotangent[:, : tap_count - 1], "ctx", -1)
    signal = jnp.concatenate([cotangent, next_part], axis=1)
    all_filters = lax.all_gather(filters, "ctx", axis=0, tiled=True)
    value_grad = correlate(signal, all_filters.T).astype(jnp.bfloat16)
    values_wide = gated_values[0]
    local_taps = lax.psum_scatter(
        correlate(signal, values_wide)[0].T * factor_tok, "ctx", scatter_dimension=0, tiled=True
    )
    filter_grad = lax.psum(local_taps, "dp")
    return (value_grad, filter_grad)


def solution(mesh):
    return jax.shard_map(
        body,
        mesh=mesh,
        in_specs=(
            P("dp", "ctx"),
            P("dp", "ctx", None),
            P("dp", "ctx", None),
            P("dp", "ctx", None),
            P("ctx", None),
        ),
        out_specs=(P("dp", "ctx", None), P("ctx", None)),
        check_vma=False,
    )
```

profile of v0, /device:TPU:0, one launch (start us, length us, event | category | flops | bytes accessed | tf_op | source)
XLA Modules:
  0.0 201.7 jit_solution(6966847847205426817)
XLA Ops:
  7.2 0.0 copy-start
  7.2 0.0 reduce-scatter.2.cloned.1.call-start
  7.2 0.7 fusion.4
  8.0 2.0 multiply_convert_fusion
  10.0 1.3 collective-permute-start
  11.3 3.3 %collective-permute-done = bf16[1,127,4096]{2,1,0:T(8,128)(2,1)S(1)} collective-permute-done((bf16[1,127,4096]{2,1,0:T(8,128)(2,1)S(1)}, bf16[1,127,4096]{2,1,0:T(8,128)(2,1)S(1)}, u32[]{:S(2)}, u32[]{:S(2)}) %collective-permute-start) | collective-permute-done | bytes 1040416 | tf_op jit(solution)/shard_map/ppermute | solution.py:10
  14.5 0.2 pad_maximum_fusion
  14.7 0.0 copy-done
  14.7 30.5 %convolution_multiply_fusion = f32[1,128,4096]{2,0,1:T(1,128)S(1)} fusion(bf16[1,255,4096]{2,1,0:T(8,128)(2,1)S(1)} %pad_maximum_fusion, bf16[128,1,4096]{2,0,1:T(8,128)(2,1)S(1)} %bitcast.12), kind=kOutput, calls=%fused_computation.1 | convolution fusion | flops 134742016 | bytes 5234688 | tf_op jit(solution)/shard_map/conv_general_dilated | solution.py:15
  45.3 3.0 %copy.46 = f32[1,128,4096]{2,1,0:T(8,128)} copy(f32[1,128,4096]{2,0,1:T(1,128)S(1)} %convolution_multiply_fusion) | data formatting | bytes 4194304
  48.3 0.0 copy-start.1
  48.3 0.0 reduce-scatter.2.cloned.1.call-update
  48.3 0.0 all-gather.2.cloned.1.call-start
  48.4 0.8 copy-done.1
  49.1 0.7 copy.29
  49.9 0.0 all-gather.2.cloned.1.call-update
  49.9 0.0 all-reduce.2.cloned.1.call-start
  49.9 74.0 %reduce-scatter.2.cloned.1.call-done = f32[256,128]{0,1:T(8,128)} async-done(((f32[4096,128]{0,1:T(8,128)}), f32[256,128]{0,1:T(8,128)}) %reduce-scatter.2.cloned.1.call-update) | async-done | bytes 131088 | tf_op jit(solution)/shard_map/reduce_scatter | solution.py:39
  124.0 0.0 all-reduce.2.cloned.1.call-update
  124.0 38.3 %all-gather.2.cloned.1.call-done = bf16[4096,128]{0,1:T(8,128)(2,1)} async-done(((bf16[256,128]{0,1:T(8,128)(2,1)}), bf16[4096,128]{0,1:T(8,128)(2,1)}) %all-gather.2.cloned.1.call-update) | async-done | bytes 1048592 | tf_op jit(solution)/shard_map/all_gather | solution.py:36
  162.3 29.1 %convolution_convert_fusion = bf16[1,128,4096]{2,0,1:T(2,128)(2,1)S(1)} fusion(bf16[1,255,4096]{2,1,0:T(8,128)(2,1)S(1)} %pad_maximum_fusion, bf16[128,1,4096]{2,0,1:T(8,128)(2,1)} %bitcast.15), kind=kOutput, calls=%fused_computation | convolution fusion | flops 134742016 | bytes 4186112 | tf_op jit(solution)/shard_map/conv_general_dilated | solution.py:15
  191.4 2.1 %copy.34 = bf16[1,128,4096]{2,1,0:T(8,128)(2,1)} copy(bf16[1,128,4096]{2,0,1:T(2,128)(2,1)S(1)} %convolution_convert_fusion) | data formatting | bytes 2097152
  193.5 0.0 all-reduce.2.cloned.1.call-done
  193.5 1.7 copy.35
Async XLA Ops:
  7.2 7.6 %copy-start = (bf16[1,128,4096]{2,1,0:T(8,128)(2,1)S(1)}, bf16[1,128,4096]{2,1,0:T(8,128)(2,1)}, u32[]{:S(2)}) copy-start(bf16[1,128,4096]{2,1,0:T(8,128)(2,1)} %param.7) | copy-start | bytes 3145732
  7.2 116.8 %reduce-scatter.2.cloned.1.call-start = ((), (), s32[]{:S(2)}) async-start(), calls=%async_computation.2 | async-start | bytes 2228224 | tf_op jit(solution)/shard_map/reduce_scatter | solution.py:39
  10.0 4.6 %collective-permute-start = (bf16[1,127,4096]{2,1,0:T(8,128)(2,1)S(1)}, bf16[1,127,4096]{2,1,0:T(8,128)(2,1)S(1)}, u32[]{:S(2)}, u32[]{:S(2)}) collective-permute-start(bf16[1,127,4096]{2,1,0:T(8,128)(2,1)S(1)} %bitcast.14), channel_id=1, source_target_pairs={{1,0},{2,1},{3,2},{4,3},{5,4},{6,5},{7,6},{8,7},{9,8},{10,9},{11,1... | collective-permute-start | bytes 3121160 | tf_op jit(solution)/shard_map/ppermute | solution.py:10
  48.3 0.8 copy-start.1
  48.3 114.0 %all-gather.2.cloned.1.call-start = ((), (), s32[]{:S(2)}) async-start(), calls=%async_computation.1 | async-start | bytes 1114112 | tf_op jit(solution)/shard_map/all_gather | solution.py:36
  49.9 143.6 %all-reduce.2.cloned.1.call-start = ((), (), s32[]{:S(2)}) async-start(), calls=%async_computation.3 | async-start | bytes 262144 | tf_op jit(solution)/shard_map/psum | solution.py:42
Sparse Core Ops, SparseCore 0:
  48.4 75.4 reduce-scatter.1
  126.7 35.5 all-gather.1
  164.6 21.1 all-reduce.1
where the time goes:
time: 202 us
  waiting for transfers between devices  116 us (57%)
  matrix products  59.6 us (30%)
  between operations  13.8 us (7%)
  local copies, waits for them, and re-layouts  8.28 us (4%)
  other arithmetic  2.94 us (1%)
    reduce_scatter x1, waiting for transfers between devices, body(): lax.psum_scatter(correlate(signal, values_wide)[0].T * factor_tok, 'ctx',...  74 us
    conv_general_dilated x2, matrix products, correlate(): lax.conv_general_dilated(signal, kernel[:, None, :], (1,), 'VALID', dimen...  59.6 us
    all_gather x1, waiting for transfers between devices, body(): all_filters = lax.all_gather(filters, 'ctx', axis=0, tiled=True)  38.3 us
    unnamed x8, local copies, waits for them, and re-layouts  8.28 us
  transfers between devices with their start and end apart: 4, of which 3 were waited for; matrix products, arithmetic and copies ran while one was open for 16% of the time, Pallas kernels for 0%

commit v1 on v0

v1 whole, which is shorter than its diff:
```python
import functools

import jax
import jax.numpy as jnp
import numpy as np
from jax import lax
from jax.experimental import pallas as pl
from jax.experimental.pallas import tpu as pltpu
from jax.sharding import PartitionSpec as P

BF16 = jnp.bfloat16
F32 = jnp.float32
AXES = ("dp", "ctx")
LANES = 128


def split_bf16(matrix):
    high = matrix.astype(BF16)
    low = (matrix - high.astype(np.float64)).astype(BF16)
    return np.asarray(high), np.asarray(low)


@functools.lru_cache(None)
def transforms(positions, taps):
    window = positions + taps
    half = window // 2
    angle = 2.0 * np.pi * np.outer(np.arange(half) + 0.5, np.arange(window)) / window
    forward = np.concatenate([np.cos(angle), np.sin(angle)], axis=0)
    high, low = split_bf16(forward)
    of_window = np.concatenate([high, low], axis=0)
    of_values = np.concatenate([high[:, :positions], low[:, :positions]], axis=1)
    of_taps = np.concatenate([high[:, :taps], low[:, :taps]], axis=1)
    inverse = forward.T / half
    inv_high, inv_low = split_bf16(inverse)
    to_taps = np.concatenate([inv_high[:taps], inv_low[:taps]], axis=0)
    to_positions = np.concatenate([inv_high[:positions], inv_low[:positions]], axis=0)
    return of_window, of_values, of_taps, to_taps, to_positions


def mul(a, b):
    return jnp.dot(a, b, preferred_element_type=F32)


def spectrum_of_window(matrix, own, after):
    both = mul(matrix, jnp.concatenate([own, after], axis=0))
    rows = both.shape[0] // 2
    return both[:rows] + both[rows:]


def correlate(x, y, inverse):
    half = x.shape[0] // 2
    a, b, c, d = x[:half], x[half:], y[:half], y[half:]
    product = jnp.concatenate([a * c + b * d, b * c - a * d], axis=0)
    high = product.astype(BF16)
    low = (product - high.astype(F32)).astype(BF16)
    rows = inverse.shape[0] // 2
    both = mul(inverse, high)
    return both[:rows] + both[rows:] + mul(inverse[:rows], low)


def cotangent_kernel(ids_ref, q_ref, g_ref, o_ref):
    positions = ids_ref.shape[1]
    weight = jnp.where(ids_ref[...] < 4, 1.0, 0.1).astype(F32)
    weight = jnp.broadcast_to(weight, (LANES, positions)).T
    for at in range(0, o_ref.shape[1], LANES):
        cols = pl.ds(at, LANES)
        o_ref[:, cols] = (
            weight * g_ref[:, cols].astype(F32) * q_ref[:, cols].astype(F32)
        ).astype(BF16)


def cotangent_of(token_ids, queries, out_grad, tile):
    positions, channels = queries.shape
    block = pl.BlockSpec((positions, tile), lambda i: (0, i))
    return pl.pallas_call(
        cotangent_kernel,
        grid=(channels // tile,),
        in_specs=[pl.BlockSpec((1, positions), lambda i: (0, 0)), block, block],
        out_specs=block,
        out_shape=jax.ShapeDtypeStruct((positions, channels), BF16),
        cost_estimate=pl.CostEstimate(
            flops=2 * positions * channels,
            bytes_accessed=6 * positions * channels,
            transcendentals=0,
        ),
        name="cotangent",
    )(token_ids, queries, out_grad)


def tap_grad_tile(cot_ref, after_ref, val_ref, wx_ref, wv_ref, wi_ref):
    x = spectrum_of_window(wx_ref[...], cot_ref[...], after_ref[...])
    values = val_ref[...]
    y = mul(wv_ref[...], jnp.concatenate([values, values], axis=0))
    return correlate(x, y, wi_ref[...])


def tap_grad_slots_kernel(
    me_ref, cot_ref, after_ref, val_ref, wx_ref, wv_ref, wi_ref, keep_ref, send_ref, tmp_ref
):
    out = tap_grad_tile(cot_ref, after_ref, val_ref, wx_ref, wv_ref, wi_ref)
    low = me_ref[0] % 4
    for block in range(4):
        tmp_ref[block ^ low] = out[:, block * LANES : (block + 1) * LANES]
    for half in range(2):
        keep_ref[half, 0, 0] = tmp_ref[half]
        send_ref[half, 0, 0] = tmp_ref[2 + half].astype(BF16)


def tap_grad_slots(me, cotangent, after, values, taps):
    positions, channels = cotangent.shape
    tile = 4 * LANES
    tiles = channels // tile
    wx, wv, _, wi, _ = transforms(positions, taps)
    data = pl.BlockSpec((positions, tile), lambda t, me: (0, t ^ (me[0] // 4)))
    whole = lambda w: pl.BlockSpec(w.shape, lambda t, me: (0, 0))
    shape = (2, 2, tiles // 2, taps, LANES)
    slot = pl.BlockSpec((2, 1, 1, taps, LANES), lambda t, me: (0, t % 2, t // 2, 0, 0))
    return pl.pallas_call(
        tap_grad_slots_kernel,
        grid_spec=pltpu.PrefetchScalarGridSpec(
            num_scalar_prefetch=1,
            grid=(tiles,),
            in_specs=[data, data, data, whole(wx), whole(wv), whole(wi)],
            out_specs=[slot, slot],
            scratch_shapes=[pltpu.VMEM((4, taps, LANES), F32)],
        ),
        out_shape=[jax.ShapeDtypeStruct(shape, F32), jax.ShapeDtypeStruct(shape, BF16)],
        cost_estimate=pl.CostEstimate(
            flops=2 * 9 * 128 * 256 * channels,
            bytes_accessed=9 * positions * channels,
            transcendentals=0,
        ),
        name="tap_grad_slots",
    )(me, cotangent, after, values, wx, wv, wi)


def tap_grad_plain_kernel(cot_ref, after_ref, val_ref, wx_ref, wv_ref, wi_ref, o_ref):
    o_ref[...] = tap_grad_tile(cot_ref, after_ref, val_ref, wx_ref, wv_ref, wi_ref)


def tap_grad_plain(cotangent, after, values, taps, tile):
    positions, channels = cotangent.shape
    wx, wv, _, wi, _ = transforms(positions, taps)
    data = pl.BlockSpec((positions, tile), lambda t: (0, t))
    whole = lambda w: pl.BlockSpec(w.shape, lambda t: (0, 0))
    return pl.pallas_call(
        tap_grad_plain_kernel,
        grid=(channels // tile,),
        in_specs=[data, data, data, whole(wx), whole(wv), whole(wi)],
        out_specs=pl.BlockSpec((taps, tile), lambda t: (0, t)),
        out_shape=jax.ShapeDtypeStruct((taps, channels), F32),
        name="tap_grad_plain",
    )(cotangent, after, values, wx, wv, wi)


def value_grad_tile(cot_ref, after_ref, filters, wx_ref, wf_ref, wi_ref):
    x = spectrum_of_window(wx_ref[...], cot_ref[...], after_ref[...])
    y = lax.dot_general(
        wf_ref[...],
        jnp.concatenate([filters, filters], axis=1),
        (((1,), (1,)), ((), ())),
        preferred_element_type=F32,
    )
    return correlate(x, y, wi_ref[...]).astype(BF16)


def value_grad_slots_kernel(
    me_ref, cot_ref, after_ref, mine_ref, other_ref, wx_ref, wf_ref, wi_ref, o_ref
):
    even = (me_ref[0] // 2) % 2 == 0
    mine, other = mine_ref[0, 0], other_ref[0, 0]
    filters = jnp.concatenate(
        [jnp.where(even, mine, other), jnp.where(even, other, mine)], axis=0
    )
    o_ref[...] = value_grad_tile(cot_ref, after_ref, filters, wx_ref, wf_ref, wi_ref)


def value_grad_slots(me, cotangent, after, mine, other):
    positions, channels = cotangent.shape
    _, _, shard, taps = mine.shape
    tile = 2 * shard
    tiles = channels // tile
    wx, _, wf, _, wi = transforms(positions, taps)
    data = pl.BlockSpec((positions, tile), lambda t, me: (0, t ^ (me[0] // 4)))
    part = pl.BlockSpec((1, 1, shard, taps), lambda t, me: (t % 2, t // 2, 0, 0))
    whole = lambda w: pl.BlockSpec(w.shape, lambda t, me: (0, 0))
    return pl.pallas_call(
        value_grad_slots_kernel,
        grid_spec=pltpu.PrefetchScalarGridSpec(
            num_scalar_prefetch=1,
            grid=(tiles,),
            in_specs=[data, data, part, part, whole(wx), whole(wf), whole(wi)],
            out_specs=data,
        ),
        out_shape=jax.ShapeDtypeStruct((positions, channels), BF16),
        cost_estimate=pl.CostEstimate(
            flops=2 * 9 * 128 * 256 * channels,
            bytes_accessed=8 * positions * channels,
            transcendentals=0,
        ),
        name="value_grad_slots",
    )(me, cotangent, after, mine, other, wx, wf, wi)


def value_grad_plain_kernel(cot_ref, after_ref, f_ref, wx_ref, wf_ref, wi_ref, o_ref):
    o_ref[...] = value_grad_tile(cot_ref, after_ref, f_ref[...], wx_ref, wf_ref, wi_ref)


def value_grad_plain(cotangent, after, filters, tile):
    positions, channels = cotangent.shape
    taps = filters.shape[1]
    wx, _, wf, _, wi = transforms(positions, taps)
    data = pl.BlockSpec((positions, tile), lambda t: (0, t))
    whole = lambda w: pl.BlockSpec(w.shape, lambda t: (0, 0))
    return pl.pallas_call(
        value_grad_plain_kernel,
        grid=(channels // tile,),
        in_specs=[data, data, pl.BlockSpec((tile, taps), lambda t: (t, 0)), whole(wx), whole(wf), whole(wi)],
        out_specs=data,
        out_shape=jax.ShapeDtypeStruct((positions, channels), BF16),
        name="value_grad_plain",
    )(cotangent, after, filters, wx, wf, wi)


def body(token_ids, queries, gated_values, out_grad, filters):
    queries, gated_values, out_grad = queries[0], gated_values[0], out_grad[0]
    positions, channels = queries.shape
    shard, taps = filters.shape
    seqs, parts = lax.axis_size("dp"), lax.axis_size("ctx")
    factor = float(seqs * parts * positions) ** -0.5

    cotangent = cotangent_of(token_ids, queries, out_grad, 1024)
    after = lax.ppermute(cotangent, "ctx", [(i, i - 1) for i in range(1, parts)])

    staged = seqs == 2 and parts >= 4 and parts & (parts - 1) == 0 and shard == 2 * LANES
    if not staged:
        all_filters = lax.all_gather(filters, "ctx", axis=0, tiled=True)
        value_grad = value_grad_plain(cotangent, after, all_filters, 512)
        share = tap_grad_plain(cotangent, after, gated_values, taps, 512)
        share = lax.psum_scatter(share.T * factor, "ctx", scatter_dimension=0, tiled=True)
        return value_grad[None], lax.psum(share, "dp")

    devices = seqs * parts
    rank = lax.axis_index("dp")
    place = lax.axis_index("ctx")
    me = (place * 2 + rank).astype(jnp.int32).reshape(1)

    def swap(x, bits):
        return lax.ppermute(x, AXES, [(i, i ^ bits) for i in range(devices)])

    line = jnp.stack([filters] + [swap(filters, 4 * k) for k in range(1, parts // 4)])
    mine = jnp.stack([line, swap(line, 2)])
    other = swap(mine, 1)

    keep, send = tap_grad_slots(me, cotangent, after, gated_values, taps)
    keep = keep + swap(send, 1).astype(F32)
    total = keep[0, 0]
    for x, y in ((1, 0), (0, 1), (1, 1)):
        total = total + swap(keep[x, y].astype(BF16), parts * x + 2 * y).astype(F32)
    block = total[0]
    for k in range(1, parts // 4):
        block = block + swap(total[k].astype(BF16), 4 * k).astype(F32)
    block = block * factor
    across = swap(block, parts)
    first = jnp.where(rank == 0, block, across)
    second = jnp.where(rank == 0, across, block)
    filter_grad = jnp.concatenate([first, second], axis=1).T

    value_grad = value_grad_slots(me, cotangent, after, mine, other)
    return value_grad[None], filter_grad


def solution(mesh):
    return jax.shard_map(
        body,
        mesh=mesh,
        in_specs=(
            P("dp", "ctx"),
            P("dp", "ctx", None),
            P("dp", "ctx", None),
            P("dp", "ctx", None),
            P("ctx", None),
        ),
        out_specs=(P("dp", "ctx", None), P("ctx", None)),
        check_vma=False,
    )
```

time: 202 us -> 76.5 us (0.38)
  waiting for transfers between devices: 116 us -> 20.2 us
  matrix products: 59.6 us -> 0 us
  starting transfers between devices: 1.41 us -> 29.4 us
  Pallas kernels: 0 us -> 21.4 us
  between operations: 13.8 us -> 0.76 us
  local copies, waits for them, and re-layouts: 8.28 us -> 2.57 us
    reduce_scatter x1 -> x0, waiting for transfers between devices: 74 us -> none  [body(): lax.psum_scatter(correlate(signal, values_wide)[0].T * factor_tok, 'ctx',...]
    conv_general_dilated x2 -> x0, matrix products: 59.6 us -> none  [correlate(): lax.conv_general_dilated(signal, kernel[:, None, :], (1,), 'VALID', dimen...]
    all_gather x1 -> x0, waiting for transfers between devices: 38.3 us -> none  [body(): all_filters = lax.all_gather(filters, 'ctx', axis=0, tiled=True)]
    ppermute x1 -> x14, starting transfers between devices: 1.29 us -> 29.4 us  [the longest x13 28.1 us: swap(): return lax.ppermute(x, AXES, [(i, i ^ bits) for i in range(devices)])]
    pallas_call x0 -> x3, Pallas kernels: none -> 21.4 us  [the longest x1 8.97 us: tap_grad_slots(): pl.pallas_call(tap_grad_slots_kernel, grid_spec=pltpu.PrefetchScalarGridS...]
    ppermute x1 -> x14, waiting for transfers between devices: 3.25 us -> 20.2 us  [the longest x13 16.7 us: swap(): return lax.ppermute(x, AXES, [(i, i ^ bits) for i in range(devices)])]
    unnamed x8 -> x9, local copies, waits for them, and re-layouts: 8.28 us -> 2.53 us
  transfers between devices with their start and end apart: 4 -> 14, of which waited for: 3 -> 9; matrix products, arithmetic and copies ran while one was open for 16% -> 2% of each run, Pallas kernels for 0% -> 11%
where the time goes in v1:
time: 76.5 us; the launch traced here: 76 us
  starting transfers between devices  29.4 us (38%)
  Pallas kernels  21.4 us (28%)
  waiting for transfers between devices  20.2 us (26%)
  local copies, waits for them, and re-layouts  2.57 us (3%)
  other arithmetic  1.61 us (2%)
    ppermute x13, starting transfers between devices, swap(): return lax.ppermute(x, AXES, [(i, i ^ bits) for i in range(devices)])  28.1 us
    ppermute x13, waiting for transfers between devices, swap(): return lax.ppermute(x, AXES, [(i, i ^ bits) for i in range(devices)])  16.7 us
    pallas_call x1, Pallas kernels, tap_grad_slots(): pl.pallas_call(tap_grad_slots_kernel, grid_spec=pltpu.PrefetchScalarGridS...  8.97 us
    pallas_call x1, Pallas kernels, value_grad_slots(): pl.pallas_call(value_grad_slots_kernel, grid_spec=pltpu.PrefetchScalarGri...  8.57 us
    pallas_call x1, Pallas kernels, cotangent_of(): pl.pallas_call(cotangent_kernel, grid=(channels // tile,), in_specs=[pl.B...  3.85 us
    ppermute x1, waiting for transfers between devices, body(): lax.ppermute(cotangent, 'ctx', [(i, i - 1) for i in range(1, parts)])  3.46 us
    unnamed x9, local copies, waits for them, and re-layouts  2.53 us
  transfers between devices with their start and end apart: 14, of which 9 were waited for; matrix products, arithmetic and copies ran while one was open for 2% of the time, Pallas kernels for 11%

profile of v1, /device:TPU:0, one launch (start us, length us, event | category | flops | bytes accessed | tf_op | source)
XLA Modules:
  0.0 76.0 jit_solution(7576357370370995698)
XLA Ops:
  0.6 3.9 %cotangent.1.cot_ref = bf16[128,4096]{1,0:T(8,128)(2,1)} custom-call(s32[1,128]{1,0:T(1,128)} %ids_ref.1, bf16[128,4096]{1,0:T(8,128)(2,1)} %bitcast.45, bf16[128,4096]{1,0:T(8,128)(2,1)} %bitcast.46), custom_call_target="tpu_custom_call" | custom-call | flops 1048576 | bytes 3145728 | tf_op jit(solution)/shard_map/cotangent/pallas_call | solution.py:75
  4.5 1.3 %collective-permute-start = (bf16[128,4096]{1,0:T(8,128)(2,1)}, bf16[128,4096]{1,0:T(8,128)(2,1)S(1)}, u32[]{:S(2)}, u32[]{:S(2)}) collective-permute-start(bf16[128,4096]{1,0:T(8,128)(2,1)} %cotangent.1.cot_ref), channel_id=1, source_target_pairs={{1,0},{2,1},{3,2},{4,3},{5,4},{6,5},{7,6},{8,7},{9,8},{10,9},{11,1... | collective-permute-start | bytes 3145736 | tf_op jit(solution)/shard_map/ppermute | solution.py:233
  5.8 3.5 %collective-permute-done.after_ref = bf16[128,4096]{1,0:T(8,128)(2,1)S(1)} collective-permute-done((bf16[128,4096]{1,0:T(8,128)(2,1)}, bf16[128,4096]{1,0:T(8,128)(2,1)S(1)}, u32[]{:S(2)}, u32[]{:S(2)}) %collective-permute-start) | collective-permute-done | bytes 1048608 | tf_op jit(solution)/shard_map/ppermute | solution.py:233
  9.2 0.0 copy-start.2
  9.2 1.0 %copy-done.2 = bf16[128,4096]{1,0:T(8,128)(2,1)} copy-done((bf16[128,4096]{1,0:T(8,128)(2,1)}, bf16[128,4096]{1,0:T(8,128)(2,1)S(1)}, u32[]{:S(2)}) %copy-start.2) | copy-done | bytes 1048600
  10.2 0.0 copy-start.1
  10.2 9.0 %tap_grad_slots.1 = (f32[2,2,4,128,128]{4,3,2,1,0:T(8,128)}, bf16[2,2,4,128,128]{4,3,2,1,0:T(8,128)(2,1)}) custom-call(s32[1]{0:T(128)} %bitcast.me_ref, bf16[128,4096]{1,0:T(8,128)(2,1)} %cotangent.1.cot_ref, bf16[128,4096]{1,0:T(8,128)(2,1)} %copy-done.2, bf16[128,4096]{1,0:T(8,128)(2,1)} %bitcast.52, bf16[512,256]{1,0:T(8,128)(2,1)} %constant.21.clone.wx_ref, ...), custom_call_target="tpu_custom_call" | custom-call | flops 2415919104 | bytes 4718592 | tf_op jit(solution)/shard_map/tap_grad_slots/pallas_call | solution.py:118
  19.2 12.9 %collective-permute-start.6 = (bf16[2,2,4,128,128]{4,3,2,1,0:T(8,128)(2,1)}, bf16[2,2,4,128,128]{4,3,2,1,0:T(8,128)(2,1)S(1)}, u32[]{:S(2)}, u32[]{:S(2)}) collective-permute-start(bf16[2,2,4,128,128]{4,3,2,1,0:T(8,128)(2,1)} %get-tuple-element.5), channel_id=1, source_target_pairs={{0,1},{1,0},{2,3},{3,2},{4,5},{5,4},{6,7},{7,6},{8,9},{9,8},{10,11... | collective-permute-start | bytes 1572872 | tf_op jit(solution)/shard_map/ppermute | solution.py:249
  32.1 0.0 copy-done.1
  32.1 1.6 %collective-permute-start.1 = (bf16[256,128]{1,0:T(8,128)(2,1)S(1)}, bf16[256,128]{1,0:T(8,128)(2,1)S(1)}, u32[]{:S(2)}, u32[]{:S(2)}) collective-permute-start(bf16[256,128]{1,0:T(8,128)(2,1)S(1)} %copy-done.1), channel_id=1, source_target_pairs={{0,4},{1,5},{2,6},{3,7},{4,0},{5,1},{6,2},{7,3},{8,12},{9,13},{10,... | collective-permute-start | bytes 196616 | tf_op jit(solution)/shard_map/ppermute | solution.py:249
  33.7 2.5 %collective-permute-start.3 = (bf16[256,128]{1,0:T(8,128)(2,1)S(1)}, bf16[256,128]{1,0:T(8,128)(2,1)S(1)}, u32[]{:S(2)}, u32[]{:S(2)}) collective-permute-start(bf16[256,128]{1,0:T(8,128)(2,1)S(1)} %copy-done.1), channel_id=1, source_target_pairs={{0,12},{1,13},{2,14},{3,15},{4,8},{5,9},{6,10},{7,11},{8,4},{9,5},... | collective-permute-start | bytes 196616 | tf_op jit(solution)/shard_map/ppermute | solution.py:249
  36.2 0.1 collective-permute-start.2
  36.3 0.1 collective-permute-done.1
  36.4 4.1 %collective-permute-done.3 = bf16[256,128]{1,0:T(8,128)(2,1)S(1)} collective-permute-done((bf16[256,128]{1,0:T(8,128)(2,1)S(1)}, bf16[256,128]{1,0:T(8,128)(2,1)S(1)}, u32[]{:S(2)}, u32[]{:S(2)}) %collective-permute-start.3) | collective-permute-done | bytes 65568 | tf_op jit(solution)/shard_map/ppermute | solution.py:249
  40.5 2.3 %collective-permute-done.2 = bf16[256,128]{1,0:T(8,128)(2,1)S(1)} collective-permute-done((bf16[256,128]{1,0:T(8,128)(2,1)S(1)}, bf16[256,128]{1,0:T(8,128)(2,1)S(1)}, u32[]{:S(2)}, u32[]{:S(2)}) %collective-permute-start.2) | collective-permute-done | bytes 65568 | tf_op jit(solution)/shard_map/ppermute | solution.py:249
  42.8 2.3 %collective-permute-start.4 = (bf16[4,256,128]{2,1,0:T(8,128)(2,1)S(1)}, bf16[4,256,128]{2,1,0:T(8,128)(2,1)S(1)}, u32[]{:S(2)}, u32[]{:S(2)}) collective-permute-start(bf16[4,256,128]{2,1,0:T(8,128)(2,1)S(1)} %get-tuple-element.16), channel_id=1, source_target_pairs={{0,2},{1,3},{2,0},{3,1},{4,6},{5,7},{6,4},{7,5},{8,10},{9,11},{10,... | collective-permute-start | bytes 786440 | tf_op jit(solution)/shard_map/ppermute | solution.py:249
  45.1 0.0 collective-permute-done.6
  45.1 1.4 %fusion.10 = (bf16[2,2,4,128,128]{4,3,2,1,0:T(8,128)(2,1)S(1)}, f32[2,2,4,128,128]{4,3,2,1,0:T(8,128)S(1)}) fusion(f32[2,2,4,128,128]{4,3,2,1,0:T(8,128)} %get-tuple-element.4, bf16[2,2,4,128,128]{4,3,2,1,0:T(8,128)(2,1)S(1)} %collective-permute-done.6), kind=kLoop, calls=%fused_computation.23 | loop fusion | flops 786432 | bytes 3145728 | tf_op jit(solution)/shard_map/convert.5
  46.6 1.6 %collective-permute-start.7 = (bf16[4,128,128]{2,1,0:T(8,128)(2,1)S(1)}, bf16[4,128,128]{2,1,0:T(8,128)(2,1)S(1)}, u32[]{:S(2)}, u32[]{:S(2)}) collective-permute-start(bf16[4,128,128]{2,1,0:T(8,128)(2,1)S(1)} %get-tuple-element.12), channel_id=1, source_target_pairs={{0,16},{1,17},{2,18},{3,19},{4,20},{5,21},{6,22},{7,23},{8,24},{9,... | collective-permute-start | bytes 393224 | tf_op jit(solution)/shard_map/ppermute | solution.py:249
  48.1 0.0 collective-permute-start.9
  48.1 2.0 %collective-permute-start.8 = (bf16[4,128,128]{2,1,0:T(8,128)(2,1)S(1)}, bf16[4,128,128]{2,1,0:T(8,128)(2,1)S(1)}, u32[]{:S(2)}, u32[]{:S(2)}) collective-permute-start(bf16[4,128,128]{2,1,0:T(8,128)(2,1)S(1)} %get-tuple-element.14), channel_id=1, source_target_pairs={{0,2},{1,3},{2,0},{3,1},{4,6},{5,7},{6,4},{7,5},{8,10},{9,11},{10,... | collective-permute-start | bytes 393224 | tf_op jit(solution)/shard_map/ppermute | solution.py:249
  50.1 5.0 %collective-permute-done.4 = bf16[4,256,128]{2,1,0:T(8,128)(2,1)S(1)} collective-permute-done((bf16[4,256,128]{2,1,0:T(8,128)(2,1)S(1)}, bf16[4,256,128]{2,1,0:T(8,128)(2,1)S(1)}, u32[]{:S(2)}, u32[]{:S(2)}) %collective-permute-start.4) | collective-permute-done | bytes 262176 | tf_op jit(solution)/shard_map/ppermute | solution.py:249
  55.1 0.1 pad_maximum_fusion.mine_ref
  55.1 0.0 copy-start
  55.1 0.1 collective-permute-start.5
  55.2 0.0 collective-permute-done.7
  55.2 0.0 collective-permute-done.9
  55.2 2.0 %collective-permute-done.8 = bf16[4,128,128]{2,1,0:T(8,128)(2,1)S(1)} collective-permute-done((bf16[4,128,128]{2,1,0:T(8,128)(2,1)S(1)}, bf16[4,128,128]{2,1,0:T(8,128)(2,1)S(1)}, u32[]{:S(2)}, u32[]{:S(2)}) %collective-permute-start.8) | collective-permute-done | bytes 131104 | tf_op jit(solution)/shard_map/ppermute | solution.py:249
  57.2 0.1 fusion.8
  57.3 0.0 copy-done
  57.3 0.1 collective-permute-start.10
  57.4 2.0 %collective-permute-start.12 = (bf16[128,128]{1,0:T(8,128)(2,1)S(1)}, bf16[128,128]{1,0:T(8,128)(2,1)S(1)}, u32[]{:S(2)}, u32[]{:S(2)}) collective-permute-start(bf16[128,128]{1,0:T(8,128)(2,1)S(1)} %get-tuple-element.20), channel_id=1, source_target_pairs={{0,12},{1,13},{2,14},{3,15},{4,8},{5,9},{6,10},{7,11},{8,4},{9,5},... | collective-permute-start | bytes 98312 | tf_op jit(solution)/shard_map/ppermute | solution.py:249
  59.4 1.5 %collective-permute-start.11 = (bf16[128,128]{1,0:T(8,128)(2,1)S(1)}, bf16[128,128]{1,0:T(8,128)(2,1)S(1)}, u32[]{:S(2)}, u32[]{:S(2)}) collective-permute-start(bf16[128,128]{1,0:T(8,128)(2,1)S(1)} %get-tuple-element.21), channel_id=1, source_target_pairs={{0,8},{1,9},{2,10},{3,11},{4,12},{5,13},{6,14},{7,15},{8,0},{9,1},... | collective-permute-start | bytes 98312 | tf_op jit(solution)/shard_map/ppermute | solution.py:249
  60.9 0.4 collective-permute-done.10
  61.3 1.9 %collective-permute-done.12 = bf16[128,128]{1,0:T(8,128)(2,1)S(1)} collective-permute-done((bf16[128,128]{1,0:T(8,128)(2,1)S(1)}, bf16[128,128]{1,0:T(8,128)(2,1)S(1)}, u32[]{:S(2)}, u32[]{:S(2)}) %collective-permute-start.12) | collective-permute-done | bytes 32800 | tf_op jit(solution)/shard_map/ppermute | solution.py:249
  63.2 1.0 %collective-permute-done.11 = bf16[128,128]{1,0:T(8,128)(2,1)S(1)} collective-permute-done((bf16[128,128]{1,0:T(8,128)(2,1)S(1)}, bf16[128,128]{1,0:T(8,128)(2,1)S(1)}, u32[]{:S(2)}, u32[]{:S(2)}) %collective-permute-start.11) | collective-permute-done | bytes 32800 | tf_op jit(solution)/shard_map/ppermute | solution.py:249
  64.2 1.6 %collective-permute-start.13 = (f32[128,128]{1,0:T(8,128)S(1)}, f32[128,128]{1,0:T(8,128)S(1)}, u32[]{:S(2)}, u32[]{:S(2)}) collective-permute-start(f32[128,128]{1,0:T(8,128)S(1)} %fusion.6), channel_id=1, source_target_pairs={{0,16},{1,17},{2,18},{3,19},{4,20},{5,21},{6,22},{7,23},{8,24},{9,... | collective-permute-start | bytes 196616 | tf_op jit(solution)/shard_map/ppermute | solution.py:249
  65.8 0.0 collective-permute-done.5.other_ref
  65.8 0.0 copy-start.3
  65.8 0.8 %copy-done.3 = bf16[2,4,256,128]{3,2,1,0:T(8,128)(2,1)} copy-done((bf16[2,4,256,128]{3,2,1,0:T(8,128)(2,1)}, bf16[2,4,256,128]{3,2,1,0:T(8,128)(2,1)S(1)}, u32[]{:S(2)}) %copy-start.3) | copy-done | bytes 524312
  66.6 8.6 %value_grad_slots.1 = bf16[128,4096]{1,0:T(8,128)(2,1)} custom-call(s32[1]{0:T(128)} %bitcast.me_ref, bf16[128,4096]{1,0:T(8,128)(2,1)} %cotangent.1.cot_ref, bf16[128,4096]{1,0:T(8,128)(2,1)} %copy-done.2, bf16[2,4,256,128]{3,2,1,0:T(8,128)(2,1)} %copy-done, bf16[2,4,256,128]{3,2,1,0:T(8,128)(2,1)} %copy-done.3, bf16[512,256]{1,0:T(8,128)(2,1)} %constant.21.clone.wx_ref, ...), custom_call_target="tpu_custom_call" | custom-call | flops 2415919104 | bytes 4194304 | tf_op jit(solution)/shard_map/value_grad_slots/pallas_call | solution.py:187
  75.2 0.0 collective-permute-done.13
  75.2 0.8 copy.12
  (6 shorter events, 0.1 us)
Async XLA Ops:
  4.5 4.8 %collective-permute-start = (bf16[128,4096]{1,0:T(8,128)(2,1)}, bf16[128,4096]{1,0:T(8,128)(2,1)S(1)}, u32[]{:S(2)}, u32[]{:S(2)}) collective-permute-start(bf16[128,4096]{1,0:T(8,128)(2,1)} %cotangent.1.cot_ref), channel_id=1, source_target_pairs={{1,0},{2,1},{3,2},{4,3},{5,4},{6,5},{7,6},{8,7},{9,8},{10,9},{11,1... | collective-permute-start | bytes 3145736 | tf_op jit(solution)/shard_map/ppermute | solution.py:233
  9.2 1.0 %copy-start.2 = (bf16[128,4096]{1,0:T(8,128)(2,1)}, bf16[128,4096]{1,0:T(8,128)(2,1)S(1)}, u32[]{:S(2)}) copy-start(bf16[128,4096]{1,0:T(8,128)(2,1)S(1)} %collective-permute-done.after_ref) | copy-start | bytes 3145732
  10.2 21.9 %copy-start.1 = (bf16[256,128]{1,0:T(8,128)(2,1)S(1)}, bf16[256,128]{1,0:T(8,128)(2,1)}, u32[]{:S(2)}) copy-start(bf16[256,128]{1,0:T(8,128)(2,1)} %param.14) | copy-start | bytes 196612
  19.2 25.9 %collective-permute-start.6 = (bf16[2,2,4,128,128]{4,3,2,1,0:T(8,128)(2,1)}, bf16[2,2,4,128,128]{4,3,2,1,0:T(8,128)(2,1)S(1)}, u32[]{:S(2)}, u32[]{:S(2)}) collective-permute-start(bf16[2,2,4,128,128]{4,3,2,1,0:T(8,128)(2,1)} %get-tuple-element.5), channel_id=1, source_target_pairs={{0,1},{1,0},{2,3},{3,2},{4,5},{5,4},{6,7},{7,6},{8,9},{9,8},{10,11... | collective-permute-start | bytes 1572872 | tf_op jit(solution)/shard_map/ppermute | solution.py:249
  32.1 4.3 %collective-permute-start.1 = (bf16[256,128]{1,0:T(8,128)(2,1)S(1)}, bf16[256,128]{1,0:T(8,128)(2,1)S(1)}, u32[]{:S(2)}, u32[]{:S(2)}) collective-permute-start(bf16[256,128]{1,0:T(8,128)(2,1)S(1)} %copy-done.1), channel_id=1, source_target_pairs={{0,4},{1,5},{2,6},{3,7},{4,0},{5,1},{6,2},{7,3},{8,12},{9,13},{10,... | collective-permute-start | bytes 196616 | tf_op jit(solution)/shard_map/ppermute | solution.py:249
  33.7 6.8 %collective-permute-start.3 = (bf16[256,128]{1,0:T(8,128)(2,1)S(1)}, bf16[256,128]{1,0:T(8,128)(2,1)S(1)}, u32[]{:S(2)}, u32[]{:S(2)}) collective-permute-start(bf16[256,128]{1,0:T(8,128)(2,1)S(1)} %copy-done.1), channel_id=1, source_target_pairs={{0,12},{1,13},{2,14},{3,15},{4,8},{5,9},{6,10},{7,11},{8,4},{9,5},... | collective-permute-start | bytes 196616 | tf_op jit(solution)/shard_map/ppermute | solution.py:249
  36.2 6.6 %collective-permute-start.2 = (bf16[256,128]{1,0:T(8,128)(2,1)S(1)}, bf16[256,128]{1,0:T(8,128)(2,1)S(1)}, u32[]{:S(2)}, u32[]{:S(2)}) collective-permute-start(bf16[256,128]{1,0:T(8,128)(2,1)S(1)} %copy-done.1), channel_id=1, source_target_pairs={{0,8},{1,9},{2,10},{3,11},{4,12},{5,13},{6,14},{7,15},{8,0},{9,1},... | collective-permute-start | bytes 196616 | tf_op jit(solution)/shard_map/ppermute | solution.py:249
  42.8 12.3 %collective-permute-start.4 = (bf16[4,256,128]{2,1,0:T(8,128)(2,1)S(1)}, bf16[4,256,128]{2,1,0:T(8,128)(2,1)S(1)}, u32[]{:S(2)}, u32[]{:S(2)}) collective-permute-start(bf16[4,256,128]{2,1,0:T(8,128)(2,1)S(1)} %get-tuple-element.16), channel_id=1, source_target_pairs={{0,2},{1,3},{2,0},{3,1},{4,6},{5,7},{6,4},{7,5},{8,10},{9,11},{10,... | collective-permute-start | bytes 786440 | tf_op jit(solution)/shard_map/ppermute | solution.py:249
  46.6 8.7 %collective-permute-start.7 = (bf16[4,128,128]{2,1,0:T(8,128)(2,1)S(1)}, bf16[4,128,128]{2,1,0:T(8,128)(2,1)S(1)}, u32[]{:S(2)}, u32[]{:S(2)}) collective-permute-start(bf16[4,128,128]{2,1,0:T(8,128)(2,1)S(1)} %get-tuple-element.12), channel_id=1, source_target_pairs={{0,16},{1,17},{2,18},{3,19},{4,20},{5,21},{6,22},{7,23},{8,24},{9,... | collective-permute-start | bytes 393224 | tf_op jit(solution)/shard_map/ppermute | solution.py:249
  48.1 7.1 %collective-permute-start.9 = (bf16[4,128,128]{2,1,0:T(8,128)(2,1)S(1)}, bf16[4,128,128]{2,1,0:T(8,128)(2,1)S(1)}, u32[]{:S(2)}, u32[]{:S(2)}) collective-permute-start(bf16[4,128,128]{2,1,0:T(8,128)(2,1)S(1)} %get-tuple-element.13), channel_id=1, source_target_pairs={{0,18},{1,19},{2,16},{3,17},{4,22},{5,23},{6,20},{7,21},{8,26},{9,... | collective-permute-start | bytes 393224 | tf_op jit(solution)/shard_map/ppermute | solution.py:249
  48.1 9.1 %collective-permute-start.8 = (bf16[4,128,128]{2,1,0:T(8,128)(2,1)S(1)}, bf16[4,128,128]{2,1,0:T(8,128)(2,1)S(1)}, u32[]{:S(2)}, u32[]{:S(2)}) collective-permute-start(bf16[4,128,128]{2,1,0:T(8,128)(2,1)S(1)} %get-tuple-element.14), channel_id=1, source_target_pairs={{0,2},{1,3},{2,0},{3,1},{4,6},{5,7},{6,4},{7,5},{8,10},{9,11},{10,... | collective-permute-start | bytes 393224 | tf_op jit(solution)/shard_map/ppermute | solution.py:249
  55.1 2.2 %copy-start = (bf16[2,4,256,128]{3,2,1,0:T(8,128)(2,1)}, bf16[2,4,256,128]{3,2,1,0:T(8,128)(2,1)S(1)}, u32[]{:S(2)}) copy-start(bf16[2,4,256,128]{3,2,1,0:T(8,128)(2,1)S(1)} %pad_maximum_fusion.mine_ref) | copy-start | bytes 1572868
  55.1 10.7 %collective-permute-start.5 = (bf16[2,4,256,128]{3,2,1,0:T(8,128)(2,1)S(1)}, bf16[2,4,256,128]{3,2,1,0:T(8,128)(2,1)S(1)}, u32[]{:S(2)}, u32[]{:S(2)}) collective-permute-start(bf16[2,4,256,128]{3,2,1,0:T(8,128)(2,1)S(1)} %pad_maximum_fusion.mine_ref), channel_id=1, source_target_pairs={{0,1},{1,0},{2,3},{3,2},{4,5},{5,4},{6,7},{7,6},{8,9},{9,8},{10,11... | collective-permute-start | bytes 1572872 | tf_op jit(solution)/shard_map/ppermute | solution.py:249
  57.3 4.0 %collective-permute-start.10 = (bf16[128,128]{1,0:T(8,128)(2,1)S(1)}, bf16[128,128]{1,0:T(8,128)(2,1)S(1)}, u32[]{:S(2)}, u32[]{:S(2)}) collective-permute-start(bf16[128,128]{1,0:T(8,128)(2,1)S(1)} %get-tuple-element.19), channel_id=1, source_target_pairs={{0,4},{1,5},{2,6},{3,7},{4,0},{5,1},{6,2},{7,3},{8,12},{9,13},{10,... | collective-permute-start | bytes 98312 | tf_op jit(solution)/shard_map/ppermute | solution.py:249
  57.4 5.8 %collective-permute-start.12 = (bf16[128,128]{1,0:T(8,128)(2,1)S(1)}, bf16[128,128]{1,0:T(8,128)(2,1)S(1)}, u32[]{:S(2)}, u32[]{:S(2)}) collective-permute-start(bf16[128,128]{1,0:T(8,128)(2,1)S(1)} %get-tuple-element.20), channel_id=1, source_target_pairs={{0,12},{1,13},{2,14},{3,15},{4,8},{5,9},{6,10},{7,11},{8,4},{9,5},... | collective-permute-start | bytes 98312 | tf_op jit(solution)/shard_map/ppermute | solution.py:249
  59.4 4.8 %collective-permute-start.11 = (bf16[128,128]{1,0:T(8,128)(2,1)S(1)}, bf16[128,128]{1,0:T(8,128)(2,1)S(1)}, u32[]{:S(2)}, u32[]{:S(2)}) collective-permute-start(bf16[128,128]{1,0:T(8,128)(2,1)S(1)} %get-tuple-element.21), channel_id=1, source_target_pairs={{0,8},{1,9},{2,10},{3,11},{4,12},{5,13},{6,14},{7,15},{8,0},{9,1},... | collective-permute-start | bytes 98312 | tf_op jit(solution)/shard_map/ppermute | solution.py:249
  64.2 10.9 %collective-permute-start.13 = (f32[128,128]{1,0:T(8,128)S(1)}, f32[128,128]{1,0:T(8,128)S(1)}, u32[]{:S(2)}, u32[]{:S(2)}) collective-permute-start(f32[128,128]{1,0:T(8,128)S(1)} %fusion.6), channel_id=1, source_target_pairs={{0,16},{1,17},{2,18},{3,19},{4,20},{5,21},{6,22},{7,23},{8,24},{9,... | collective-permute-start | bytes 196616 | tf_op jit(solution)/shard_map/ppermute | solution.py:249
  65.8 0.8 %copy-start.3 = (bf16[2,4,256,128]{3,2,1,0:T(8,128)(2,1)}, bf16[2,4,256,128]{3,2,1,0:T(8,128)(2,1)S(1)}, u32[]{:S(2)}) copy-start(bf16[2,4,256,128]{3,2,1,0:T(8,128)(2,1)S(1)} %collective-permute-done.5.other_ref) | copy-start | bytes 1572868

commit v2 on v1

v2 whole, which is shorter than its diff:
```python
import functools

import jax
import jax.numpy as jnp
import numpy as np
from jax import lax
from jax.experimental import pallas as pl
from jax.experimental.pallas import tpu as pltpu
from jax.sharding import PartitionSpec as P


BF16 = jnp.bfloat16
F32 = jnp.float32
AXES = ("dp", "ctx")
LANES = 128


def split_bf16(matrix):
    high = matrix.astype(BF16)
    low = (matrix - high.astype(np.float64)).astype(BF16)
    return np.asarray(high), np.asarray(low)


@functools.lru_cache(None)
def transforms(positions, taps):
    window = positions + taps
    half = window // 2
    angle = 2.0 * np.pi * np.outer(np.arange(half) + 0.5, np.arange(window)) / window
    forward = np.concatenate([np.cos(angle), np.sin(angle)], axis=0)
    high, low = split_bf16(forward)
    of_window = np.concatenate([high, low], axis=0)
    of_values = np.concatenate([high[:, :positions], low[:, :positions]], axis=1)
    of_taps = np.concatenate([high[:, :taps], low[:, :taps]], axis=1)
    inverse = forward.T / half
    inv_high, inv_low = split_bf16(inverse)
    to_taps = np.concatenate([inv_high[:taps], inv_low[:taps]], axis=0)
    to_positions = np.concatenate([inv_high[:positions], inv_low[:positions]], axis=0)
    return of_window, of_values, of_taps, to_taps, to_positions


def mul(a, b):
    return jnp.dot(a, b, preferred_element_type=F32)


def spectrum_of_window(matrix, own, after):
    both = mul(matrix, jnp.concatenate([own, after], axis=0))
    rows = both.shape[0] // 2
    return both[:rows] + both[rows:]


def correlate(x, y, inverse):
    half = x.shape[0] // 2
    a, b, c, d = x[:half], x[half:], y[:half], y[half:]
    product = jnp.concatenate([a * c + b * d, b * c - a * d], axis=0)
    high = product.astype(BF16)
    low = (product - high.astype(F32)).astype(BF16)
    rows = inverse.shape[0] // 2
    both = mul(inverse, high)
    return both[:rows] + both[rows:] + mul(inverse[:rows], low)


VMEM_SPEC = pl.BlockSpec(memory_space=pltpu.VMEM)
SMEM_SPEC = pl.BlockSpec(memory_space=pltpu.SMEM)
HBM_SPEC = pl.BlockSpec(memory_space=pltpu.HBM)


def params(mib):
    return pltpu.CompilerParams(vmem_limit_bytes=mib << 20)


def cost(flops, nbytes):
    return pl.CostEstimate(flops=flops, bytes_accessed=nbytes, transcendentals=0)


def cotangent_kernel(ids_ref, q_hbm, g_hbm, *refs):
    *outs, q_ref, g_ref, sems = refs
    width = outs[0].shape[1]
    copies = []
    for i in range(len(outs)):
        cols = pl.ds(i * width, width)
        copies.append(
            [
                pltpu.make_async_copy(src.at[:, cols], dst.at[:, cols], sems.at[n, i])
                for n, (src, dst) in enumerate(((q_hbm, q_ref), (g_hbm, g_ref)))
            ]
        )
        for copy in copies[-1]:
            copy.start()
    positions = ids_ref.shape[1]
    weight = jnp.where(ids_ref[...] < 4, 1.0, 0.1).astype(F32)
    weight = jnp.broadcast_to(weight, (LANES, positions)).T
    for i, out in enumerate(outs):
        for copy in copies[i]:
            copy.wait()
        for at in range(0, width, LANES):
            cols = pl.ds(i * width + at, LANES)
            out[:, at : at + LANES] = (
                weight * g_ref[:, cols].astype(F32) * q_ref[:, cols].astype(F32)
            ).astype(BF16)


def cotangent_of(token_ids, queries, out_grad, pieces):
    positions, channels = queries.shape
    piece = jax.ShapeDtypeStruct((positions, channels // pieces), BF16)
    return pl.pallas_call(
        cotangent_kernel,
        in_specs=[VMEM_SPEC, HBM_SPEC, HBM_SPEC],
        out_specs=[VMEM_SPEC] * pieces,
        out_shape=[piece] * pieces,
        scratch_shapes=[pltpu.VMEM((positions, channels), BF16)] * 2
        + [pltpu.SemaphoreType.DMA((2, pieces))],
        compiler_params=params(8),
        cost_estimate=cost(2 * positions * channels, 6 * positions * channels),
        name="cotangent",
    )(token_ids, *(pltpu.with_memory_space_constraint(x, pltpu.HBM) for x in (queries, out_grad)))


def tap_grad_tile(cot_ref, after_ref, val_ref, wx_ref, wv_ref, wi_ref):
    x = spectrum_of_window(wx_ref[...], cot_ref[...], after_ref[...])
    values = val_ref[...]
    y = mul(wv_ref[...], jnp.concatenate([values, values], axis=0))
    return correlate(x, y, wi_ref[...])


def tap_grad_slots_kernel(
    first, me_ref, cot_ref, after_ref, val_ref, wx_ref, wv_ref, wi_ref, keep_ref, send_ref, tmp_ref
):
    width = cot_ref.shape[1]
    x = spectrum_of_window(wx_ref[...], cot_ref[...], after_ref[...])
    values = val_ref[:, first * width : (first + 1) * width]
    y = mul(wv_ref[...], jnp.concatenate([values, values], axis=0))
    out = correlate(x, y, wi_ref[...])
    low, row = me_ref[0] % 4, me_ref[0] // 4 % 2
    for tile in range(width // (4 * LANES)):
        for block in range(4):
            at = (tile * 4 + block) * LANES
            tmp_ref[tile, block ^ low] = out[:, at : at + LANES]
        for half in range(2):
            keep_ref[half, tile % 2 ^ row, tile // 2] = tmp_ref[tile, half]
            send_ref[half, tile % 2 ^ row, tile // 2] = tmp_ref[tile, 2 + half].astype(BF16)


def tap_grad_slots(me, cotangent, after, values, first, taps):
    positions, width = cotangent.shape
    wx, wv, _, wi, _ = transforms(positions, taps)
    tiles = width // (4 * LANES)
    shape = (2, 2, tiles // 2, taps, LANES)
    return pl.pallas_call(
        functools.partial(tap_grad_slots_kernel, first),
        in_specs=[SMEM_SPEC] + [VMEM_SPEC] * 6,
        out_specs=[VMEM_SPEC, VMEM_SPEC],
        out_shape=[jax.ShapeDtypeStruct(shape, F32), jax.ShapeDtypeStruct(shape, BF16)],
        scratch_shapes=[pltpu.VMEM((tiles, 4, taps, LANES), F32)],
        compiler_params=params(24),
        cost_estimate=cost(2 * 9 * 128 * 256 * width, 9 * positions * width),
        name="tap_grad_slots",
    )(me, cotangent, after, values, wx, wv, wi)


def spread_kernel(keep_ref, got_ref, mine_ref, *out_refs):
    mine_ref[...] = keep_ref[0, 0] + got_ref[0, 0].astype(F32)
    for (x, y), out_ref in zip(((1, 0), (0, 1), (1, 1)), out_refs):
        out_ref[...] = (keep_ref[x, y] + got_ref[x, y].astype(F32)).astype(BF16)


def spread(keep, got):
    block = keep.shape[2:]
    return pl.pallas_call(
        spread_kernel,
        in_specs=[VMEM_SPEC] * 2,
        out_specs=[VMEM_SPEC] * 4,
        out_shape=[jax.ShapeDtypeStruct(block, F32)] + [jax.ShapeDtypeStruct(block, BF16)] * 3,
        compiler_params=params(8),
        cost_estimate=cost(keep.size, 8 * keep.size),
        name="spread",
    )(keep, got)


def line_kernel(pieces, me_ref, *refs):
    ins, (mine_ref, *send_refs) = refs[: 4 * pieces], refs[4 * pieces : -1]
    sum_ref = refs[-1]
    depth = ins[0].shape[0]
    for piece in range(pieces):
        own, *got = ins[4 * piece : 4 * piece + 4]
        for z in range(depth):
            total = own[z]
            for ref in got:
                total = total + ref[z].astype(F32)
            sum_ref[piece * depth + z] = total
    at = me_ref[0] // 8
    mine_ref[...] = sum_ref[at]
    for k, send_ref in enumerate(send_refs, 1):
        send_ref[...] = sum_ref[at ^ k].astype(BF16)


def along_line(me, pieces):
    depth, taps, lanes = pieces[0][0].shape
    count = len(pieces) * depth
    flat = [array for piece in pieces for array in piece]
    return pl.pallas_call(
        functools.partial(line_kernel, len(pieces)),
        in_specs=[SMEM_SPEC] + [VMEM_SPEC] * len(flat),
        out_specs=[VMEM_SPEC] * count,
        out_shape=[jax.ShapeDtypeStruct((taps, lanes), F32)]
        + [jax.ShapeDtypeStruct((taps, lanes), BF16)] * (count - 1),
        scratch_shapes=[pltpu.VMEM((count, taps, lanes), F32)],
        compiler_params=params(8),
        cost_estimate=cost(4 * count * taps * lanes, 16 * count * taps * lanes),
        name="along_line",
    )(me, *flat)


def finish_kernel(factor, mine_ref, *refs):
    *got, out_ref = refs
    total = mine_ref[...]
    for ref in got:
        total = total + ref[...].astype(F32)
    out_ref[...] = (total * factor).T


def finish(mine, got, factor):
    taps, lanes = mine.shape
    return pl.pallas_call(
        functools.partial(finish_kernel, factor),
        in_specs=[VMEM_SPEC] * (1 + len(got)),
        out_specs=VMEM_SPEC,
        out_shape=jax.ShapeDtypeStruct((lanes, taps), F32),
        compiler_params=params(8),
        cost_estimate=cost(4 * taps * lanes, 16 * taps * lanes),
        name="finish",
    )(mine, *got)


def join_kernel(me_ref, mine_ref, other_ref, out_ref):
    rank = me_ref[0] % 2
    rows = mine_ref.shape[0]
    out_ref[pl.ds(pl.multiple_of(rank * rows, rows), rows), :] = mine_ref[...]
    out_ref[pl.ds(pl.multiple_of((1 - rank) * rows, rows), rows), :] = other_ref[...]


def join(me, mine, other):
    rows, taps = mine.shape
    return pl.pallas_call(
        join_kernel,
        in_specs=[SMEM_SPEC, VMEM_SPEC, VMEM_SPEC],
        out_specs=VMEM_SPEC,
        out_shape=jax.ShapeDtypeStruct((2 * rows, taps), F32),
        compiler_params=params(8),
        cost_estimate=cost(1, 16 * rows * taps),
        name="join",
    )(me, mine, other)


def tap_grad_plain_kernel(cot_ref, after_ref, val_ref, wx_ref, wv_ref, wi_ref, o_ref):
    o_ref[...] = tap_grad_tile(cot_ref, after_ref, val_ref, wx_ref, wv_ref, wi_ref)


def tap_grad_plain(cotangent, after, values, taps, tile):
    positions, channels = cotangent.shape
    wx, wv, _, wi, _ = transforms(positions, taps)
    data = pl.BlockSpec((positions, tile), lambda t: (0, t))
    whole = lambda w: pl.BlockSpec(w.shape, lambda t: (0, 0))
    return pl.pallas_call(
        tap_grad_plain_kernel,
        grid=(channels // tile,),
        in_specs=[data, data, data, whole(wx), whole(wv), whole(wi)],
        out_specs=pl.BlockSpec((taps, tile), lambda t: (0, t)),
        out_shape=jax.ShapeDtypeStruct((taps, channels), F32),
        name="tap_grad_plain",
    )(cotangent, after, values, wx, wv, wi)


def value_grad_tile(own, after, filters, wx_ref, wf_ref, wi_ref):
    x = spectrum_of_window(wx_ref[...], own, after)
    y = lax.dot_general(
        wf_ref[...],
        jnp.concatenate([filters, filters], axis=1),
        (((1,), (1,)), ((), ())),
        preferred_element_type=F32,
    )
    return correlate(x, y, wi_ref[...]).astype(BF16)


def value_grad_slots_kernel(count, me_ref, *refs):
    cots, afters = refs[:count], refs[count : 2 * count]
    mine_ref, other_ref, wx_ref, wf_ref, wi_ref, out_hbm, out_ref, sems = refs[2 * count :]
    _, depth, _, _ = mine_ref.shape
    me = me_ref[0]
    even, row, at = me // 2 % 2 == 0, me // 4 % 2, me // 8
    width = cots[0].shape[1]
    copies = []
    for piece in range(count):
        filters = []
        for z in range(piece * depth // count, (piece + 1) * depth // count):
            for y in range(2):
                mine, other = mine_ref[y ^ row, z ^ at], other_ref[y ^ row, z ^ at]
                filters += [jnp.where(even, mine, other), jnp.where(even, other, mine)]
        cols = pl.ds(piece * width, width)
        out_ref[:, cols] = value_grad_tile(
            cots[piece][...], afters[piece][...], jnp.concatenate(filters, axis=0), wx_ref, wf_ref, wi_ref
        )
        copies.append(pltpu.make_async_copy(out_ref.at[:, cols], out_hbm.at[:, cols], sems.at[piece]))
        copies[-1].start()
    for copy in copies:
        copy.wait()


def value_grad_slots(me, cotangents, afters, mine, other):
    count = len(cotangents)
    positions, width = cotangents[0].shape
    taps = mine.shape[-1]
    channels = count * width
    wx, _, wf, _, wi = transforms(positions, taps)
    return pl.pallas_call(
        functools.partial(value_grad_slots_kernel, count),
        in_specs=[SMEM_SPEC] + [VMEM_SPEC] * (2 * count + 5),
        out_specs=HBM_SPEC,
        out_shape=jax.ShapeDtypeStruct((positions, channels), BF16),
        scratch_shapes=[pltpu.VMEM((positions, channels), BF16), pltpu.SemaphoreType.DMA((count,))],
        compiler_params=params(24),
        cost_estimate=cost(2 * 9 * 128 * 256 * channels, 8 * positions * channels),
        name="value_grad_slots",
    )(me, *cotangents, *afters, mine, other, wx, wf, wi)


def value_grad_plain_kernel(cot_ref, after_ref, f_ref, wx_ref, wf_ref, wi_ref, o_ref):
    o_ref[...] = value_grad_tile(
        cot_ref[...], after_ref[...], f_ref[...], wx_ref, wf_ref, wi_ref
    )


def value_grad_plain(cotangent, after, filters, tile):
    positions, channels = cotangent.shape
    taps = filters.shape[1]
    wx, _, wf, _, wi = transforms(positions, taps)
    data = pl.BlockSpec((positions, tile), lambda t: (0, t))
    whole = lambda w: pl.BlockSpec(w.shape, lambda t: (0, 0))
    return pl.pallas_call(
        value_grad_plain_kernel,
        grid=(channels // tile,),
        in_specs=[data, data, pl.BlockSpec((tile, taps), lambda t: (t, 0)), whole(wx), whole(wf), whole(wi)],
        out_specs=data,
        out_shape=jax.ShapeDtypeStruct((positions, channels), BF16),
        name="value_grad_plain",
    )(cotangent, after, filters, wx, wf, wi)


def body(token_ids, queries, gated_values, out_grad, filters):
    queries, gated_values, out_grad = queries[0], gated_values[0], out_grad[0]
    positions, _ = queries.shape
    shard, taps = filters.shape
    seqs, parts = lax.axis_size("dp"), lax.axis_size("ctx")
    factor = float(seqs * parts * positions) ** -0.5

    staged = seqs == 2 and parts >= 8 and parts & (parts - 1) == 0 and shard == 2 * LANES
    back = [(i, i - 1) for i in range(1, parts)]
    if not staged:
        (cotangent,) = cotangent_of(token_ids, queries, out_grad, 1)
        after = lax.ppermute(cotangent, "ctx", back)
        all_filters = lax.all_gather(filters, "ctx", axis=0, tiled=True)
        value_grad = value_grad_plain(cotangent, after, all_filters, 512)
        share = tap_grad_plain(cotangent, after, gated_values, taps, 512)
        share = lax.psum_scatter(share.T * factor, "ctx", scatter_dimension=0, tiled=True)
        return value_grad[None], lax.psum(share, "dp")

    devices = seqs * parts
    depth = parts // 4
    rank = lax.axis_index("dp")
    place = lax.axis_index("ctx")
    me = (place * 2 + rank).astype(jnp.int32).reshape(1)

    def swap(x, bits):
        return lax.ppermute(x, AXES, [(i, i ^ bits) for i in range(devices)])

    def after_both(x, *others):
        return lax.optimization_barrier((x, *others))[0]

    hops = (parts, 2, parts + 2)
    cots = cotangent_of(token_ids, queries, out_grad, 2)
    afters = []
    for cot in cots:
        afters.append(lax.ppermute(cot, "ctx", back))

    filters = after_both(filters, cots[0])
    line = jnp.stack([filters] + [swap(filters, 4 * k) for k in range(1, depth)])
    afters[0] = after_both(afters[0], line)

    keep, send = tap_grad_slots(me, cots[0], afters[0], gated_values, 0, taps)
    own, *sends = spread(keep, swap(send, 1))
    sums = [[own] + [swap(x, bits) for x, bits in zip(sends, hops)]]

    afters[1], own = lax.optimization_barrier((afters[1], own))
    line_y = swap(after_both(line, afters[1]), 2)
    keep, send = tap_grad_slots(me, cots[1], afters[1], gated_values, 1, taps)
    mine = jnp.stack([line, after_both(line_y, send)])
    own, *sends = spread(keep, swap(send, 1))
    sums.append([own] + [swap(x, bits) for x, bits in zip(sends, hops)])
    other = swap(mine, 1)

    block, *sends = along_line(me, sums)
    got = [swap(x, 4 * k) for k, x in enumerate(sends, 1)]
    block = finish(block, got, factor)
    filter_grad = join(me, block, swap(block, parts))

    value_grad = value_grad_slots(me, cots, afters, mine, other)
    return value_grad[None], filter_grad


def solution(mesh):
    return jax.shard_map(
        body,
        mesh=mesh,
        in_specs=(
            P("dp", "ctx"),
            P("dp", "ctx", None),
            P("dp", "ctx", None),
            P("dp", "ctx", None),
            P("ctx", None),
        ),
        out_specs=(P("dp", "ctx", None), P("ctx", None)),
        check_vma=False,
    )
```

time: 76.5 us -> 63.7 us (0.83)
  Pallas kernels: 21.4 us -> 10.1 us
  waiting for transfers between devices: 20.2 us -> 28.8 us
  starting transfers between devices: 29.4 us -> 22.1 us
  other arithmetic: 1.61 us -> 0.1 us
  local copies, waits for them, and re-layouts: 2.57 us -> 1.62 us
    ppermute x13 -> x17, waiting for transfers between devices: 16.7 us -> 28.8 us  [swap(): return lax.ppermute(x, AXES, [(i, i ^ bits) for i in range(devices)])]
    pallas_call x3 -> x9, Pallas kernels: 21.4 us -> 10.1 us  [the longest x1 3.99 us: value_grad_slots(): pl.pallas_call(functools.partial(value_grad_slots_kernel, count), in_spec...]
    ppermute x13 -> x17, starting transfers between devices: 28.1 us -> 19.5 us  [swap(): return lax.ppermute(x, AXES, [(i, i ^ bits) for i in range(devices)])]
    ppermute x1 -> x2, waiting for transfers between devices: 3.46 us -> 0.01 us  [body(): afters.append(lax.ppermute(cot, 'ctx', back))]
    another operation x4 -> x2, other arithmetic: 1.56 us -> 0.1 us  [body(): mine = jnp.stack([line, after_both(line_y, send)])]
    ppermute x1 -> x2, starting transfers between devices: 1.28 us -> 2.57 us  [body(): afters.append(lax.ppermute(cot, 'ctx', back))]
    unnamed x9 -> x12, local copies, waits for them, and re-layouts: 2.53 us -> 1.62 us
  transfers between devices with their start and end apart: 14 -> 19, of which waited for: 9 -> 11; matrix products, arithmetic and copies ran while one was open for 2% -> 0% of each run, Pallas kernels for 11% -> 7%
where the time goes in v2:
time: 63.7 us; the launch traced here: 63.5 us
  waiting for transfers between devices  28.8 us (45%)
  starting transfers between devices  22.1 us (35%)
  Pallas kernels  10.1 us (16%)
  local copies, waits for them, and re-layouts  1.62 us (3%)
  between operations  0.8 us (1%)
    ppermute x17, waiting for transfers between devices, swap(): return lax.ppermute(x, AXES, [(i, i ^ bits) for i in range(devices)])  28.8 us
    ppermute x17, starting transfers between devices, swap(): return lax.ppermute(x, AXES, [(i, i ^ bits) for i in range(devices)])  19.5 us
    pallas_call x1, Pallas kernels, value_grad_slots(): pl.pallas_call(functools.partial(value_grad_slots_kernel, count), in_spec...  3.99 us
    pallas_call x2, Pallas kernels, tap_grad_slots(): pl.pallas_call(functools.partial(tap_grad_slots_kernel, first), in_specs=...  3.3 us
    ppermute x2, starting transfers between devices, body(): afters.append(lax.ppermute(cot, 'ctx', back))  2.57 us
    pallas_call x1, Pallas kernels, cotangent_of(): pl.pallas_call(cotangent_kernel, in_specs=[VMEM_SPEC, HBM_SPEC, HBM_SPEC]...  1.82 us
    unnamed x12, local copies, waits for them, and re-layouts  1.62 us
  transfers between devices with their start and end apart: 19, of which 11 were waited for; matrix products, arithmetic and copies ran while one was open for 0% of the time, Pallas kernels for 7%

profile of v2, /device:TPU:0, one launch (start us, length us, event | category | flops | bytes accessed | tf_op | source)
XLA Modules:
  0.0 63.5 jit_solution(13550764525772016073)
XLA Ops:
  0.6 0.6 %copy-done = s32[1,128]{1,0:T(1,128)S(1)} copy-done((s32[1,128]{1,0:T(1,128)S(1)}, s32[1,128]{1,0:T(1,128)}, u32[]{:S(2)}) %copy-start) | copy-done | bytes 536
  1.3 1.8 %cotangent.1 = (bf16[128,2048]{1,0:T(8,128)(2,1)S(1)}, bf16[128,2048]{1,0:T(8,128)(2,1)S(1)}) custom-call(s32[1,128]{1,0:T(1,128)S(1)} %copy-done, bf16[128,4096]{1,0:T(8,128)(2,1)} %bitcast.14, bf16[128,4096]{1,0:T(8,128)(2,1)} %bitcast.15), custom_call_target="tpu_custom_call" | custom-call | flops 1048576 | bytes 3145728 | tf_op jit(solution)/shard_map/cotangent/pallas_call | solution.py:105
  3.1 1.3 %collective-permute-start = (bf16[128,2048]{1,0:T(8,128)(2,1)S(1)}, bf16[128,2048]{1,0:T(8,128)(2,1)S(1)}, u32[]{:S(2)}, u32[]{:S(2)}) collective-permute-start(bf16[128,2048]{1,0:T(8,128)(2,1)S(1)} %get-tuple-element.25.cot_ref.refs_0_), channel_id=1, source_target_pairs={{1,0},{2,1},{3,2},{4,3},{5,4},{6,5},{7,6},{8,7},{9,8},{10,9},{11,1... | collective-permute-start | bytes 1572872 | tf_op jit(solution)/shard_map/ppermute | solution.py:382
  4.4 6.6 %collective-permute-start.3 = (bf16[256,128]{1,0:T(8,128)(2,1)S(1)}, bf16[256,128]{1,0:T(8,128)(2,1)S(1)}, u32[]{:S(2)}, u32[]{:S(2)}) collective-permute-start(bf16[256,128]{1,0:T(8,128)(2,1)S(1)} %copy-done.5), channel_id=1, source_target_pairs={{0,12},{1,13},{2,14},{3,15},{4,8},{5,9},{6,10},{7,11},{8,4},{9,5},... | collective-permute-start | bytes 196616 | tf_op jit(solution)/shard_map/ppermute | solution.py:373
  11.0 0.0 collective-permute-start.2
  11.0 0.6 %collective-permute-start.1 = (bf16[256,128]{1,0:T(8,128)(2,1)S(1)}, bf16[256,128]{1,0:T(8,128)(2,1)S(1)}, u32[]{:S(2)}, u32[]{:S(2)}) collective-permute-start(bf16[256,128]{1,0:T(8,128)(2,1)S(1)} %copy-done.5), channel_id=1, source_target_pairs={{0,4},{1,5},{2,6},{3,7},{4,0},{5,1},{6,2},{7,3},{8,12},{9,13},{10,... | collective-permute-start | bytes 196616 | tf_op jit(solution)/shard_map/ppermute | solution.py:373
  11.7 1.3 %collective-permute-start.4 = (bf16[128,2048]{1,0:T(8,128)(2,1)S(1)}, bf16[128,2048]{1,0:T(8,128)(2,1)S(1)}, u32[]{:S(2)}, u32[]{:S(2)}) collective-permute-start(bf16[128,2048]{1,0:T(8,128)(2,1)S(1)} %get-tuple-element.26.cot_ref.refs_1_), channel_id=1, source_target_pairs={{1,0},{2,1},{3,2},{4,3},{5,4},{6,5},{7,6},{8,7},{9,8},{10,9},{11,1... | collective-permute-start | bytes 1572872 | tf_op jit(solution)/shard_map/ppermute | solution.py:382
  13.0 7.3 %collective-permute-done.3 = bf16[256,128]{1,0:T(8,128)(2,1)S(1)} collective-permute-done((bf16[256,128]{1,0:T(8,128)(2,1)S(1)}, bf16[256,128]{1,0:T(8,128)(2,1)S(1)}, u32[]{:S(2)}, u32[]{:S(2)}) %collective-permute-start.3) | collective-permute-done | bytes 65568 | tf_op jit(solution)/shard_map/ppermute | solution.py:373
  20.3 1.8 %collective-permute-done.2 = bf16[256,128]{1,0:T(8,128)(2,1)S(1)} collective-permute-done((bf16[256,128]{1,0:T(8,128)(2,1)S(1)}, bf16[256,128]{1,0:T(8,128)(2,1)S(1)}, u32[]{:S(2)}, u32[]{:S(2)}) %collective-permute-start.2) | collective-permute-done | bytes 65568 | tf_op jit(solution)/shard_map/ppermute | solution.py:373
  22.2 0.9 %copy-done.2 = bf16[512,256]{1,0:T(8,128)(2,1)S(1)} copy-done((bf16[512,256]{1,0:T(8,128)(2,1)S(1)}, bf16[512,256]{1,0:T(8,128)(2,1)}, u32[]{:S(2)}) %copy-start.2) | copy-done | bytes 262168
  23.1 0.0 copy-done.3
  23.1 0.1 copy-done.4
  23.1 1.6 %tap_grad_slots.2 = (f32[2,2,2,128,128]{4,3,2,1,0:T(8,128)S(1)}, bf16[2,2,2,128,128]{4,3,2,1,0:T(8,128)(2,1)S(1)}) custom-call(s32[1]{0:T(128)} %bitcast.me_ref, bf16[128,2048]{1,0:T(8,128)(2,1)S(1)} %get-tuple-element.25.cot_ref.refs_0_, bf16[128,2048]{1,0:T(8,128)(2,1)S(1)} %collective-permute-done.after_ref.refs_2_, bf16[128,4096]{1,0:T(8,128)(2,1)S(1)} %bitcast.12, ...), custom_call_target="tpu_custom_call" | custom-call | flops 1207959552 | bytes 2359296 | tf_op jit(solution)/shard_map/tap_grad_slots/pallas_call | solution.py:148
  24.8 0.1 collective-permute-start.5
  24.9 1.5 %collective-permute-done.5.got_ref = bf16[2,2,2,128,128]{4,3,2,1,0:T(8,128)(2,1)S(1)} collective-permute-done((bf16[2,2,2,128,128]{4,3,2,1,0:T(8,128)(2,1)S(1)}, bf16[2,2,2,128,128]{4,3,2,1,0:T(8,128)(2,1)S(1)}, u32[]{:S(2)}, u32[]{:S(2)}) %collective-permute-start.5) | collective-permute-done | bytes 262176 | tf_op jit(solution)/shard_map/ppermute | solution.py:373
  26.4 0.1 spread.2
  26.5 0.1 collective-permute-start.6
  26.6 1.7 %tap_grad_slots.3 = (f32[2,2,2,128,128]{4,3,2,1,0:T(8,128)S(1)}, bf16[2,2,2,128,128]{4,3,2,1,0:T(8,128)(2,1)S(1)}) custom-call(s32[1]{0:T(128)} %bitcast.me_ref, bf16[128,2048]{1,0:T(8,128)(2,1)S(1)} %get-tuple-element.26.cot_ref.refs_1_, bf16[128,2048]{1,0:T(8,128)(2,1)S(1)} %collective-permute-done.4.after_ref.refs_3_, bf16[128,4096]{1,0:T(8,128)(2,1)S(1)} %bitcast.13, ...), custom_call_target="tpu_custom_call" | custom-call | flops 1207959552 | bytes 2359296 | tf_op jit(solution)/shard_map/tap_grad_slots/pallas_call | solution.py:148
  28.2 6.7 %collective-permute-done.6 = bf16[4,256,128]{2,1,0:T(8,128)(2,1)S(1)} collective-permute-done((bf16[4,256,128]{2,1,0:T(8,128)(2,1)S(1)}, bf16[4,256,128]{2,1,0:T(8,128)(2,1)S(1)}, u32[]{:S(2)}, u32[]{:S(2)}) %collective-permute-start.6) | collective-permute-done | bytes 262176 | tf_op jit(solution)/shard_map/ppermute | solution.py:373
  34.9 0.1 pad_maximum_fusion.refs_4_
  34.9 0.1 collective-permute-start.7
  35.0 0.5 collective-permute-start.11
  35.5 1.5 %collective-permute-start.8 = (bf16[2,128,128]{2,1,0:T(8,128)(2,1)S(1)}, bf16[2,128,128]{2,1,0:T(8,128)(2,1)S(1)}, u32[]{:S(2)}, u32[]{:S(2)}) collective-permute-start(bf16[2,128,128]{2,1,0:T(8,128)(2,1)S(1)} %get-tuple-element.36), channel_id=1, source_target_pairs={{0,16},{1,17},{2,18},{3,19},{4,20},{5,21},{6,22},{7,23},{8,24},{9,... | collective-permute-start | bytes 196616 | tf_op jit(solution)/shard_map/ppermute | solution.py:373
  37.0 0.5 collective-permute-start.9
  37.5 1.5 %collective-permute-start.10 = (bf16[2,128,128]{2,1,0:T(8,128)(2,1)S(1)}, bf16[2,128,128]{2,1,0:T(8,128)(2,1)S(1)}, u32[]{:S(2)}, u32[]{:S(2)}) collective-permute-start(bf16[2,128,128]{2,1,0:T(8,128)(2,1)S(1)} %get-tuple-element.38), channel_id=1, source_target_pairs={{0,18},{1,19},{2,16},{3,17},{4,22},{5,23},{6,20},{7,21},{8,26},{9,... | collective-permute-start | bytes 196616 | tf_op jit(solution)/shard_map/ppermute | solution.py:373
  39.0 0.0 collective-permute-done.11.got_ref
  39.0 0.1 spread.3
  39.1 1.6 %collective-permute-start.12 = (bf16[2,128,128]{2,1,0:T(8,128)(2,1)S(1)}, bf16[2,128,128]{2,1,0:T(8,128)(2,1)S(1)}, u32[]{:S(2)}, u32[]{:S(2)}) collective-permute-start(bf16[2,128,128]{2,1,0:T(8,128)(2,1)S(1)} %get-tuple-element.41), channel_id=1, source_target_pairs={{0,16},{1,17},{2,18},{3,19},{4,20},{5,21},{6,22},{7,23},{8,24},{9,... | collective-permute-start | bytes 196616 | tf_op jit(solution)/shard_map/ppermute | solution.py:373
  40.6 0.0 collective-permute-done.8.refs_1_
  40.6 0.5 collective-permute-start.13
  41.1 0.8 %collective-permute-done.9.refs_2_ = bf16[2,128,128]{2,1,0:T(8,128)(2,1)S(1)} collective-permute-done((bf16[2,128,128]{2,1,0:T(8,128)(2,1)S(1)}, bf16[2,128,128]{2,1,0:T(8,128)(2,1)S(1)}, u32[]{:S(2)}, u32[]{:S(2)}) %collective-permute-start.9) | collective-permute-done | bytes 65568 | tf_op jit(solution)/shard_map/ppermute | solution.py:373
  41.9 1.0 %collective-permute-start.14 = (bf16[2,128,128]{2,1,0:T(8,128)(2,1)S(1)}, bf16[2,128,128]{2,1,0:T(8,128)(2,1)S(1)}, u32[]{:S(2)}, u32[]{:S(2)}) collective-permute-start(bf16[2,128,128]{2,1,0:T(8,128)(2,1)S(1)} %get-tuple-element.43), channel_id=1, source_target_pairs={{0,18},{1,19},{2,16},{3,17},{4,22},{5,23},{6,20},{7,21},{8,26},{9,... | collective-permute-start | bytes 196616 | tf_op jit(solution)/shard_map/ppermute | solution.py:373
  42.9 0.0 collective-permute-done.10.refs_3_
  42.9 0.6 collective-permute-done.12.refs_5_
  43.5 1.4 %collective-permute-done.13.refs_6_ = bf16[2,128,128]{2,1,0:T(8,128)(2,1)S(1)} collective-permute-done((bf16[2,128,128]{2,1,0:T(8,128)(2,1)S(1)}, bf16[2,128,128]{2,1,0:T(8,128)(2,1)S(1)}, u32[]{:S(2)}, u32[]{:S(2)}) %collective-permute-start.13) | collective-permute-done | bytes 65568 | tf_op jit(solution)/shard_map/ppermute | solution.py:373
  44.9 2.2 %collective-permute-done.14.refs_7_ = bf16[2,128,128]{2,1,0:T(8,128)(2,1)S(1)} collective-permute-done((bf16[2,128,128]{2,1,0:T(8,128)(2,1)S(1)}, bf16[2,128,128]{2,1,0:T(8,128)(2,1)S(1)}, u32[]{:S(2)}, u32[]{:S(2)}) %collective-permute-start.14) | collective-permute-done | bytes 65568 | tf_op jit(solution)/shard_map/ppermute | solution.py:373
  47.1 0.1 along_line.1
  47.2 0.6 collective-permute-start.15
  47.8 1.0 %collective-permute-start.16 = (bf16[128,128]{1,0:T(8,128)(2,1)S(1)}, bf16[128,128]{1,0:T(8,128)(2,1)S(1)}, u32[]{:S(2)}, u32[]{:S(2)}) collective-permute-start(bf16[128,128]{1,0:T(8,128)(2,1)S(1)} %get-tuple-element.46), channel_id=1, source_target_pairs={{0,8},{1,9},{2,10},{3,11},{4,12},{5,13},{6,14},{7,15},{8,0},{9,1},... | collective-permute-start | bytes 98312 | tf_op jit(solution)/shard_map/ppermute | solution.py:373
  48.7 2.9 %collective-permute-start.17 = (bf16[128,128]{1,0:T(8,128)(2,1)S(1)}, bf16[128,128]{1,0:T(8,128)(2,1)S(1)}, u32[]{:S(2)}, u32[]{:S(2)}) collective-permute-start(bf16[128,128]{1,0:T(8,128)(2,1)S(1)} %get-tuple-element.47), channel_id=1, source_target_pairs={{0,12},{1,13},{2,14},{3,15},{4,8},{5,9},{6,10},{7,11},{8,4},{9,5},... | collective-permute-start | bytes 98312 | tf_op jit(solution)/shard_map/ppermute | solution.py:373
  51.6 0.0 collective-permute-done.15.refs_0_
  51.6 1.0 %collective-permute-done.16.refs_1_ = bf16[128,128]{1,0:T(8,128)(2,1)S(1)} collective-permute-done((bf16[128,128]{1,0:T(8,128)(2,1)S(1)}, bf16[128,128]{1,0:T(8,128)(2,1)S(1)}, u32[]{:S(2)}, u32[]{:S(2)}) %collective-permute-start.16) | collective-permute-done | bytes 32800 | tf_op jit(solution)/shard_map/ppermute | solution.py:373
  52.6 1.9 %collective-permute-done.17.refs_2_ = bf16[128,128]{1,0:T(8,128)(2,1)S(1)} collective-permute-done((bf16[128,128]{1,0:T(8,128)(2,1)S(1)}, bf16[128,128]{1,0:T(8,128)(2,1)S(1)}, u32[]{:S(2)}, u32[]{:S(2)}) %collective-permute-start.17) | collective-permute-done | bytes 32800 | tf_op jit(solution)/shard_map/ppermute | solution.py:373
  54.4 0.1 finish.1.mine_ref
  54.5 0.6 collective-permute-start.18
  55.2 3.7 %collective-permute-done.18.other_ref = f32[128,128]{1,0:T(8,128)S(1)} collective-permute-done((f32[128,128]{1,0:T(8,128)S(1)}, f32[128,128]{1,0:T(8,128)S(1)}, u32[]{:S(2)}, u32[]{:S(2)}) %collective-permute-start.18) | collective-permute-done | bytes 65568 | tf_op jit(solution)/shard_map/ppermute | solution.py:373
  58.9 0.7 %join.1 = f32[256,128]{1,0:T(8,128)} custom-call(s32[1]{0:T(128)} %bitcast.me_ref, f32[128,128]{1,0:T(8,128)S(1)} %finish.1.mine_ref, f32[128,128]{1,0:T(8,128)S(1)} %collective-permute-done.18.other_ref), custom_call_target="tpu_custom_call" | custom-call | flops 1 | bytes 262144 | tf_op jit(solution)/shard_map/join/pallas_call | solution.py:243
  59.6 4.0 %value_grad_slots.1 = bf16[128,4096]{1,0:T(8,128)(2,1)} custom-call(s32[1]{0:T(128)} %bitcast.me_ref, bf16[128,2048]{1,0:T(8,128)(2,1)S(1)} %get-tuple-element.25.cot_ref.refs_0_, bf16[128,2048]{1,0:T(8,128)(2,1)S(1)} %get-tuple-element.26.cot_ref.refs_1_, bf16[128,2048]{1,0:T(8,128)(2,1)S(1)} %collective-permute-done.after_ref.refs_2_, ...), custom_call_target="tpu_custom_call" | custom-call | flops 2415919104 | bytes 4194304 | tf_op jit(solution)/shard_map/value_grad_slots/pallas_call | solution.py:314
  (13 shorter events, 0.1 us)
Async XLA Ops:
  0.6 0.7 %copy-start = (s32[1,128]{1,0:T(1,128)S(1)}, s32[1,128]{1,0:T(1,128)}, u32[]{:S(2)}) copy-start(s32[1,128]{1,0:T(1,128)} %ids_ref.1) | copy-start | bytes 1540
  1.3 3.1 %copy-start.5 = (bf16[256,128]{1,0:T(8,128)(2,1)S(1)}, bf16[256,128]{1,0:T(8,128)(2,1)}, u32[]{:S(2)}) copy-start(bf16[256,128]{1,0:T(8,128)(2,1)} %param.14) | copy-start | bytes 196612
  1.3 20.9 %copy-start.1 = (bf16[1,128,4096]{2,1,0:T(8,128)(2,1)S(1)}, bf16[1,128,4096]{2,1,0:T(8,128)(2,1)}, u32[]{:S(2)}) copy-start(bf16[1,128,4096]{2,1,0:T(8,128)(2,1)} %param.12) | copy-start | bytes 3145732
  3.1 19.0 %collective-permute-start = (bf16[128,2048]{1,0:T(8,128)(2,1)S(1)}, bf16[128,2048]{1,0:T(8,128)(2,1)S(1)}, u32[]{:S(2)}, u32[]{:S(2)}) collective-permute-start(bf16[128,2048]{1,0:T(8,128)(2,1)S(1)} %get-tuple-element.25.cot_ref.refs_0_), channel_id=1, source_target_pairs={{1,0},{2,1},{3,2},{4,3},{5,4},{6,5},{7,6},{8,7},{9,8},{10,9},{11,1... | collective-permute-start | bytes 1572872 | tf_op jit(solution)/shard_map/ppermute | solution.py:382
  4.4 15.9 %collective-permute-start.3 = (bf16[256,128]{1,0:T(8,128)(2,1)S(1)}, bf16[256,128]{1,0:T(8,128)(2,1)S(1)}, u32[]{:S(2)}, u32[]{:S(2)}) collective-permute-start(bf16[256,128]{1,0:T(8,128)(2,1)S(1)} %copy-done.5), channel_id=1, source_target_pairs={{0,12},{1,13},{2,14},{3,15},{4,8},{5,9},{6,10},{7,11},{8,4},{9,5},... | collective-permute-start | bytes 196616 | tf_op jit(solution)/shard_map/ppermute | solution.py:373
  11.0 11.1 %collective-permute-start.2 = (bf16[256,128]{1,0:T(8,128)(2,1)S(1)}, bf16[256,128]{1,0:T(8,128)(2,1)S(1)}, u32[]{:S(2)}, u32[]{:S(2)}) collective-permute-start(bf16[256,128]{1,0:T(8,128)(2,1)S(1)} %copy-done.5), channel_id=1, source_target_pairs={{0,8},{1,9},{2,10},{3,11},{4,12},{5,13},{6,14},{7,15},{8,0},{9,1},... | collective-permute-start | bytes 196616 | tf_op jit(solution)/shard_map/ppermute | solution.py:373
  11.0 11.1 %collective-permute-start.1 = (bf16[256,128]{1,0:T(8,128)(2,1)S(1)}, bf16[256,128]{1,0:T(8,128)(2,1)S(1)}, u32[]{:S(2)}, u32[]{:S(2)}) collective-permute-start(bf16[256,128]{1,0:T(8,128)(2,1)S(1)} %copy-done.5), channel_id=1, source_target_pairs={{0,4},{1,5},{2,6},{3,7},{4,0},{5,1},{6,2},{7,3},{8,12},{9,13},{10,... | collective-permute-start | bytes 196616 | tf_op jit(solution)/shard_map/ppermute | solution.py:373
  11.7 14.8 %collective-permute-start.4 = (bf16[128,2048]{1,0:T(8,128)(2,1)S(1)}, bf16[128,2048]{1,0:T(8,128)(2,1)S(1)}, u32[]{:S(2)}, u32[]{:S(2)}) collective-permute-start(bf16[128,2048]{1,0:T(8,128)(2,1)S(1)} %get-tuple-element.26.cot_ref.refs_1_), channel_id=1, source_target_pairs={{1,0},{2,1},{3,2},{4,3},{5,4},{6,5},{7,6},{8,7},{9,8},{10,9},{11,1... | collective-permute-start | bytes 1572872 | tf_op jit(solution)/shard_map/ppermute | solution.py:382
  22.1 1.0 %copy-start.2 = (bf16[512,256]{1,0:T(8,128)(2,1)S(1)}, bf16[512,256]{1,0:T(8,128)(2,1)}, u32[]{:S(2)}) copy-start(bf16[512,256]{1,0:T(8,128)(2,1)} %constant.17.clone.wx_ref.refs_6_) | copy-start | bytes 786436
  22.1 1.0 %copy-start.3 = (bf16[256,256]{1,0:T(8,128)(2,1)S(1)}, bf16[256,256]{1,0:T(8,128)(2,1)}, u32[]{:S(2)}) copy-start(bf16[256,256]{1,0:T(8,128)(2,1)} %constant.19.clone.wi_ref.refs_8_) | copy-start | bytes 393220
  22.1 1.0 %copy-start.4 = (bf16[256,256]{1,0:T(8,128)(2,1)S(1)}, bf16[256,256]{1,0:T(8,128)(2,1)}, u32[]{:S(2)}) copy-start(bf16[256,256]{1,0:T(8,128)(2,1)} %constant.18.clone.wv_ref.refs_7_) | copy-start | bytes 393220
  24.8 1.6 %collective-permute-start.5 = (bf16[2,2,2,128,128]{4,3,2,1,0:T(8,128)(2,1)S(1)}, bf16[2,2,2,128,128]{4,3,2,1,0:T(8,128)(2,1)S(1)}, u32[]{:S(2)}, u32[]{:S(2)}) collective-permute-start(bf16[2,2,2,128,128]{4,3,2,1,0:T(8,128)(2,1)S(1)} %get-tuple-element.30), channel_id=1, source_target_pairs={{0,1},{1,0},{2,3},{3,2},{4,5},{5,4},{6,7},{7,6},{8,9},{9,8},{10,11... | collective-permute-start | bytes 786440 | tf_op jit(solution)/shard_map/ppermute | solution.py:373
  26.5 8.4 %collective-permute-start.6 = (bf16[4,256,128]{2,1,0:T(8,128)(2,1)S(1)}, bf16[4,256,128]{2,1,0:T(8,128)(2,1)S(1)}, u32[]{:S(2)}, u32[]{:S(2)}) collective-permute-start(bf16[4,256,128]{2,1,0:T(8,128)(2,1)S(1)} %get-tuple-element.33), channel_id=1, source_target_pairs={{0,2},{1,3},{2,0},{3,1},{4,6},{5,7},{6,4},{7,5},{8,10},{9,11},{10,... | collective-permute-start | bytes 786440 | tf_op jit(solution)/shard_map/ppermute | solution.py:373
  34.9 24.6 %collective-permute-start.7 = (bf16[2,4,256,128]{3,2,1,0:T(8,128)(2,1)S(1)}, bf16[2,4,256,128]{3,2,1,0:T(8,128)(2,1)S(1)}, u32[]{:S(2)}, u32[]{:S(2)}) collective-permute-start(bf16[2,4,256,128]{3,2,1,0:T(8,128)(2,1)S(1)} %pad_maximum_fusion.refs_4_), channel_id=1, source_target_pairs={{0,1},{1,0},{2,3},{3,2},{4,5},{5,4},{6,7},{7,6},{8,9},{9,8},{10,11... | collective-permute-start | bytes 1572872 | tf_op jit(solution)/shard_map/ppermute | solution.py:373
  35.0 4.0 %collective-permute-start.11 = (bf16[2,2,2,128,128]{4,3,2,1,0:T(8,128)(2,1)S(1)}, bf16[2,2,2,128,128]{4,3,2,1,0:T(8,128)(2,1)S(1)}, u32[]{:S(2)}, u32[]{:S(2)}) collective-permute-start(bf16[2,2,2,128,128]{4,3,2,1,0:T(8,128)(2,1)S(1)} %get-tuple-element.34), channel_id=1, source_target_pairs={{0,1},{1,0},{2,3},{3,2},{4,5},{5,4},{6,7},{7,6},{8,9},{9,8},{10,11... | collective-permute-start | bytes 786440 | tf_op jit(solution)/shard_map/ppermute | solution.py:373
  35.5 5.1 %collective-permute-start.8 = (bf16[2,128,128]{2,1,0:T(8,128)(2,1)S(1)}, bf16[2,128,128]{2,1,0:T(8,128)(2,1)S(1)}, u32[]{:S(2)}, u32[]{:S(2)}) collective-permute-start(bf16[2,128,128]{2,1,0:T(8,128)(2,1)S(1)} %get-tuple-element.36), channel_id=1, source_target_pairs={{0,16},{1,17},{2,18},{3,19},{4,20},{5,21},{6,22},{7,23},{8,24},{9,... | collective-permute-start | bytes 196616 | tf_op jit(solution)/shard_map/ppermute | solution.py:373
  37.0 4.9 %collective-permute-start.9 = (bf16[2,128,128]{2,1,0:T(8,128)(2,1)S(1)}, bf16[2,128,128]{2,1,0:T(8,128)(2,1)S(1)}, u32[]{:S(2)}, u32[]{:S(2)}) collective-permute-start(bf16[2,128,128]{2,1,0:T(8,128)(2,1)S(1)} %get-tuple-element.37), channel_id=1, source_target_pairs={{0,2},{1,3},{2,0},{3,1},{4,6},{5,7},{6,4},{7,5},{8,10},{9,11},{10,... | collective-permute-start | bytes 196616 | tf_op jit(solution)/shard_map/ppermute | solution.py:373
  37.5 5.4 %collective-permute-start.10 = (bf16[2,128,128]{2,1,0:T(8,128)(2,1)S(1)}, bf16[2,128,128]{2,1,0:T(8,128)(2,1)S(1)}, u32[]{:S(2)}, u32[]{:S(2)}) collective-permute-start(bf16[2,128,128]{2,1,0:T(8,128)(2,1)S(1)} %get-tuple-element.38), channel_id=1, source_target_pairs={{0,18},{1,19},{2,16},{3,17},{4,22},{5,23},{6,20},{7,21},{8,26},{9,... | collective-permute-start | bytes 196616 | tf_op jit(solution)/shard_map/ppermute | solution.py:373
  39.1 4.4 %collective-permute-start.12 = (bf16[2,128,128]{2,1,0:T(8,128)(2,1)S(1)}, bf16[2,128,128]{2,1,0:T(8,128)(2,1)S(1)}, u32[]{:S(2)}, u32[]{:S(2)}) collective-permute-start(bf16[2,128,128]{2,1,0:T(8,128)(2,1)S(1)} %get-tuple-element.41), channel_id=1, source_target_pairs={{0,16},{1,17},{2,18},{3,19},{4,20},{5,21},{6,22},{7,23},{8,24},{9,... | collective-permute-start | bytes 196616 | tf_op jit(solution)/shard_map/ppermute | solution.py:373
  40.6 4.3 %collective-permute-start.13 = (bf16[2,128,128]{2,1,0:T(8,128)(2,1)S(1)}, bf16[2,128,128]{2,1,0:T(8,128)(2,1)S(1)}, u32[]{:S(2)}, u32[]{:S(2)}) collective-permute-start(bf16[2,128,128]{2,1,0:T(8,128)(2,1)S(1)} %get-tuple-element.42), channel_id=1, source_target_pairs={{0,2},{1,3},{2,0},{3,1},{4,6},{5,7},{6,4},{7,5},{8,10},{9,11},{10,... | collective-permute-start | bytes 196616 | tf_op jit(solution)/shard_map/ppermute | solution.py:373
  41.9 5.2 %collective-permute-start.14 = (bf16[2,128,128]{2,1,0:T(8,128)(2,1)S(1)}, bf16[2,128,128]{2,1,0:T(8,128)(2,1)S(1)}, u32[]{:S(2)}, u32[]{:S(2)}) collective-permute-start(bf16[2,128,128]{2,1,0:T(8,128)(2,1)S(1)} %get-tuple-element.43), channel_id=1, source_target_pairs={{0,18},{1,19},{2,16},{3,17},{4,22},{5,23},{6,20},{7,21},{8,26},{9,... | collective-permute-start | bytes 196616 | tf_op jit(solution)/shard_map/ppermute | solution.py:373
  47.2 4.5 %collective-permute-start.15 = (bf16[128,128]{1,0:T(8,128)(2,1)S(1)}, bf16[128,128]{1,0:T(8,128)(2,1)S(1)}, u32[]{:S(2)}, u32[]{:S(2)}) collective-permute-start(bf16[128,128]{1,0:T(8,128)(2,1)S(1)} %get-tuple-element.45), channel_id=1, source_target_pairs={{0,4},{1,5},{2,6},{3,7},{4,0},{5,1},{6,2},{7,3},{8,12},{9,13},{10,... | collective-permute-start | bytes 98312 | tf_op jit(solution)/shard_map/ppermute | solution.py:373
  47.8 4.8 %collective-permute-start.16 = (bf16[128,128]{1,0:T(8,128)(2,1)S(1)}, bf16[128,128]{1,0:T(8,128)(2,1)S(1)}, u32[]{:S(2)}, u32[]{:S(2)}) collective-permute-start(bf16[128,128]{1,0:T(8,128)(2,1)S(1)} %get-tuple-element.46), channel_id=1, source_target_pairs={{0,8},{1,9},{2,10},{3,11},{4,12},{5,13},{6,14},{7,15},{8,0},{9,1},... | collective-permute-start | bytes 98312 | tf_op jit(solution)/shard_map/ppermute | solution.py:373
  48.7 5.7 %collective-permute-start.17 = (bf16[128,128]{1,0:T(8,128)(2,1)S(1)}, bf16[128,128]{1,0:T(8,128)(2,1)S(1)}, u32[]{:S(2)}, u32[]{:S(2)}) collective-permute-start(bf16[128,128]{1,0:T(8,128)(2,1)S(1)} %get-tuple-element.47), channel_id=1, source_target_pairs={{0,12},{1,13},{2,14},{3,15},{4,8},{5,9},{6,10},{7,11},{8,4},{9,5},... | collective-permute-start | bytes 98312 | tf_op jit(solution)/shard_map/ppermute | solution.py:373
  54.5 4.3 %collective-permute-start.18 = (f32[128,128]{1,0:T(8,128)S(1)}, f32[128,128]{1,0:T(8,128)S(1)}, u32[]{:S(2)}, u32[]{:S(2)}) collective-permute-start(f32[128,128]{1,0:T(8,128)S(1)} %finish.1.mine_ref), channel_id=1, source_target_pairs={{0,16},{1,17},{2,18},{3,19},{4,20},{5,21},{6,22},{7,23},{8,24},{9,... | collective-permute-start | bytes 196616 | tf_op jit(solution)/shard_map/ppermute | solution.py:373

commit v3 on v2

--- a/solution.py
+++ b/solution.py
@@ -72,10 +72,12 @@
     return pl.CostEstimate(flops=flops, bytes_accessed=nbytes, transcendentals=0)
 
 
-def cotangent_kernel(ids_ref, q_hbm, g_hbm, *refs):
-    *outs, q_ref, g_ref, sems = refs
+def cotangent_kernel(ids_hbm, q_hbm, g_hbm, *refs):
+    *outs, ids_ref, q_ref, g_ref, sems, ids_sem = refs
     width = outs[0].shape[1]
     copies = []
+    ids_copy = pltpu.make_async_copy(ids_hbm, ids_ref, ids_sem)
+    ids_copy.start()
     for i in range(len(outs)):
         cols = pl.ds(i * width, width)
         copies.append(
@@ -87,6 +89,7 @@
         for copy in copies[-1]:
             copy.start()
     positions = ids_ref.shape[1]
+    ids_copy.wait()
     weight = jnp.where(ids_ref[...] < 4, 1.0, 0.1).astype(F32)
     weight = jnp.broadcast_to(weight, (LANES, positions)).T
     for i, out in enumerate(outs):
@@ -104,15 +107,16 @@
     piece = jax.ShapeDtypeStruct((positions, channels // pieces), BF16)
     return pl.pallas_call(
         cotangent_kernel,
-        in_specs=[VMEM_SPEC, HBM_SPEC, HBM_SPEC],
+        in_specs=[HBM_SPEC] * 3,
         out_specs=[VMEM_SPEC] * pieces,
         out_shape=[piece] * pieces,
-        scratch_shapes=[pltpu.VMEM((positions, channels), BF16)] * 2
-        + [pltpu.SemaphoreType.DMA((2, pieces))],
+        scratch_shapes=[pltpu.VMEM(token_ids.shape, token_ids.dtype)]
+        + [pltpu.VMEM((positions, channels), BF16)] * 2
+        + [pltpu.SemaphoreType.DMA((2, pieces)), pltpu.SemaphoreType.DMA],
         compiler_params=params(8),
         cost_estimate=cost(2 * positions * channels, 6 * positions * channels),
         name="cotangent",
-    )(token_ids, *(pltpu.with_memory_space_constraint(x, pltpu.HBM) for x in (queries, out_grad)))
+    )(*(pltpu.with_memory_space_constraint(x, pltpu.HBM) for x in (token_ids, queries, out_grad)))
 
 
 def tap_grad_tile(cot_ref, after_ref, val_ref, wx_ref, wv_ref, wi_ref):
@@ -281,46 +285,41 @@
     return correlate(x, y, wi_ref[...]).astype(BF16)
 
 
-def value_grad_slots_kernel(count, me_ref, *refs):
-    cots, afters = refs[:count], refs[count : 2 * count]
-    mine_ref, other_ref, wx_ref, wf_ref, wi_ref, out_hbm, out_ref, sems = refs[2 * count :]
-    _, depth, _, _ = mine_ref.shape
+def value_grad_slots_kernel(piece, count, me_ref, *refs):
+    cot_ref, after_ref, mine_ref, other_ref, wx_ref, wf_ref, wi_ref = refs[:7]
+    out_hbm, out_ref, sem = refs[-3:]
+    depth = mine_ref.shape[1]
     me = me_ref[0]
     even, row, at = me // 2 % 2 == 0, me // 4 % 2, me // 8
-    width = cots[0].shape[1]
-    copies = []
-    for piece in range(count):
-        filters = []
-        for z in range(piece * depth // count, (piece + 1) * depth // count):
-            for y in range(2):
-                mine, other = mine_ref[y ^ row, z ^ at], other_ref[y ^ row, z ^ at]
-                filters += [jnp.where(even, mine, other), jnp.where(even, other, mine)]
-        cols = pl.ds(piece * width, width)
-        out_ref[:, cols] = value_grad_tile(
-            cots[piece][...], afters[piece][...], jnp.concatenate(filters, axis=0), wx_ref, wf_ref, wi_ref
-        )
-        copies.append(pltpu.make_async_copy(out_ref.at[:, cols], out_hbm.at[:, cols], sems.at[piece]))
-        copies[-1].start()
-    for copy in copies:
-        copy.wait()
-
-
-def value_grad_slots(me, cotangents, afters, mine, other):
-    count = len(cotangents)
-    positions, width = cotangents[0].shape
+    filters = []
+    for z in range(piece * depth // count, (piece + 1) * depth // count):
+        for y in range(2):
+            mine, other = mine_ref[y ^ row, z ^ at], other_ref[y ^ row, z ^ at]
+            filters += [jnp.where(even, mine, other), jnp.where(even, other, mine)]
+    out_ref[...] = value_grad_tile(
+        cot_ref[...], after_ref[...], jnp.concatenate(filters, axis=0), wx_ref, wf_ref, wi_ref
+    )
+    width = cot_ref.shape[1]
+    copy = pltpu.make_async_copy(out_ref, out_hbm.at[:, pl.ds(piece * width, width)], sem)
+    copy.start()
+    copy.wait()
+
+
+def value_grad_slots(me, cotangent, after, mine, other, piece, count, so_far=()):
+    positions, width = cotangent.shape
     taps = mine.shape[-1]
-    channels = count * width
     wx, _, wf, _, wi = transforms(positions, taps)
     return pl.pallas_call(
-        functools.partial(value_grad_slots_kernel, count),
-        in_specs=[SMEM_SPEC] + [VMEM_SPEC] * (2 * count + 5),
+        functools.partial(value_grad_slots_kernel, piece, count),
+        in_specs=[SMEM_SPEC] + [VMEM_SPEC] * 7 + [HBM_SPEC] * len(so_far),
         out_specs=HBM_SPEC,
-        out_shape=jax.ShapeDtypeStruct((positions, channels), BF16),
-        scratch_shapes=[pltpu.VMEM((positions, channels), BF16), pltpu.SemaphoreType.DMA((count,))],
+        out_shape=jax.ShapeDtypeStruct((positions, count * width), BF16),
+        input_output_aliases={8: 0} if so_far else {},
+        scratch_shapes=[pltpu.VMEM((positions, width), BF16), pltpu.SemaphoreType.DMA],
         compiler_params=params(24),
-        cost_estimate=cost(2 * 9 * 128 * 256 * channels, 8 * positions * channels),
+        cost_estimate=cost(2 * 9 * 128 * 256 * width, 8 * positions * width),
         name="value_grad_slots",
-    )(me, *cotangents, *afters, mine, other, wx, wf, wi)
+    )(me, cotangent, after, mine, other, wx, wf, wi, *so_far)
 
 
 def value_grad_plain_kernel(cot_ref, after_ref, f_ref, wx_ref, wf_ref, wi_ref, o_ref):
@@ -382,14 +381,14 @@
         afters.append(lax.ppermute(cot, "ctx", back))
 
     filters = after_both(filters, cots[0])
-    line = jnp.stack([filters] + [swap(filters, 4 * k) for k in range(1, depth)])
-    afters[0] = after_both(afters[0], line)
+    line = [filters] + [swap(filters, 4 * k) for k in range(1, depth)]
 
     keep, send = tap_grad_slots(me, cots[0], afters[0], gated_values, 0, taps)
     own, *sends = spread(keep, swap(send, 1))
     sums = [[own] + [swap(x, bits) for x, bits in zip(sends, hops)]]
 
     afters[1], own = lax.optimization_barrier((afters[1], own))
+    line = jnp.stack(lax.optimization_barrier((*line, own))[:-1])
     line_y = swap(after_both(line, afters[1]), 2)
     keep, send = tap_grad_slots(me, cots[1], afters[1], gated_values, 1, taps)
     mine = jnp.stack([line, after_both(line_y, send)])
@@ -402,7 +401,12 @@
     block = finish(block, got, factor)
     filter_grad = join(me, block, swap(block, parts))
 
-    value_grad = value_grad_slots(me, cots, afters, mine, other)
+    value_grad = ()
+    for piece in range(2):
+        value_grad = [
+            value_grad_slots(me, cots[piece], afters[piece], mine, other, piece, 2, value_grad)
+        ]
+    value_grad = value_grad[0]
     return value_grad[None], filter_grad
 
 

time: 63.7 us -> 68 us (1.068)
  starting transfers between devices: 22.1 us -> 29.1 us
  waiting for transfers between devices: 28.8 us -> 24.8 us
  Pallas kernels: 10.1 us -> 12.9 us
  local copies, waits for them, and re-layouts: 1.62 us -> 0.03 us
    ppermute x17, starting transfers between devices: 19.5 us -> 26.5 us  [swap(): return lax.ppermute(x, AXES, [(i, i ^ bits) for i in range(devices)])]
    ppermute x17, waiting for transfers between devices: 28.8 us -> 23.4 us  [swap(): return lax.ppermute(x, AXES, [(i, i ^ bits) for i in range(devices)])]
    pallas_call x2 -> x3, Pallas kernels: 5.81 us -> 7.7 us  [the longest x2 5.83 us: value_grad_slots(): pl.pallas_call(functools.partial(value_grad_slots_kernel, piece, count),...]
    unnamed x12 -> x10, local copies, waits for them, and re-layouts: 1.62 us -> 0.03 us
    ppermute x2, waiting for transfers between devices: 0.01 us -> 1.33 us  [body(): afters.append(lax.ppermute(cot, 'ctx', back))]
    pallas_call x2, Pallas kernels: 3.3 us -> 4.28 us  [tap_grad_slots(): pl.pallas_call(functools.partial(tap_grad_slots_kernel, first), in_specs=...]
  transfers between devices with their start and end apart: 19 -> 19, of which waited for: 11 -> 12; matrix products, arithmetic and copies ran while one was open for 0% -> 0% of each run, Pallas kernels for 7% -> 8%
where the time goes in v3:
time: 68 us; the launch traced here: 67.8 us
  starting transfers between devices  29.1 us (43%)
  waiting for transfers between devices  24.8 us (36%)
  Pallas kernels  12.9 us (19%)
  between operations  0.82 us (1%)
    ppermute x17, starting transfers between devices, swap(): return lax.ppermute(x, AXES, [(i, i ^ bits) for i in range(devices)])  26.5 us
    ppermute x17, waiting for transfers between devices, swap(): return lax.ppermute(x, AXES, [(i, i ^ bits) for i in range(devices)])  23.4 us
    pallas_call x2, Pallas kernels, value_grad_slots(): pl.pallas_call(functools.partial(value_grad_slots_kernel, piece, count),...  5.83 us
    pallas_call x2, Pallas kernels, tap_grad_slots(): pl.pallas_call(functools.partial(tap_grad_slots_kernel, first), in_specs=...  4.28 us
    ppermute x2, starting transfers between devices, body(): afters.append(lax.ppermute(cot, 'ctx', back))  2.58 us
    pallas_call x1, Pallas kernels, cotangent_of(): pl.pallas_call(cotangent_kernel, in_specs=[HBM_SPEC] * 3, out_specs=[VMEM...  1.87 us
  transfers between devices with their start and end apart: 19, of which 12 were waited for; matrix products, arithmetic and copies ran while one was open for 0% of the time, Pallas kernels for 8%

profile of v3, /device:TPU:0, one launch (start us, length us, event | category | flops | bytes accessed | tf_op | source)
XLA Modules:
  0.0 67.8 jit_solution(18381290838857487444)
XLA Ops:
  0.6 0.0 copy-start
  0.6 0.0 copy-start.1
  0.7 0.0 copy-start.2
  0.7 1.9 %cotangent.1 = (bf16[128,2048]{1,0:T(8,128)(2,1)S(1)}, bf16[128,2048]{1,0:T(8,128)(2,1)S(1)}) custom-call(s32[1,128]{1,0:T(1,128)} %ids_hbm.1, bf16[128,4096]{1,0:T(8,128)(2,1)} %bitcast.15, bf16[128,4096]{1,0:T(8,128)(2,1)} %bitcast.16), custom_call_target="tpu_custom_call" | custom-call | flops 1048576 | bytes 3145728 | tf_op jit(solution)/shard_map/cotangent/pallas_call | solution.py:108
  2.6 1.3 %collective-permute-start.1 = (bf16[128,2048]{1,0:T(8,128)(2,1)S(1)}, bf16[128,2048]{1,0:T(8,128)(2,1)}, u32[]{:S(2)}, u32[]{:S(2)}) collective-permute-start(bf16[128,2048]{1,0:T(8,128)(2,1)S(1)} %get-tuple-element.29.cot_ref.refs_0_), channel_id=1, source_target_pairs={{1,0},{2,1},{3,2},{4,3},{5,4},{6,5},{7,6},{8,7},{9,8},{10,9},{11,1... | collective-permute-start | bytes 1572872 | tf_op jit(solution)/shard_map/ppermute | solution.py:381
  3.9 1.3 %collective-permute-start = (bf16[128,2048]{1,0:T(8,128)(2,1)S(1)}, bf16[128,2048]{1,0:T(8,128)(2,1)S(1)}, u32[]{:S(2)}, u32[]{:S(2)}) collective-permute-start(bf16[128,2048]{1,0:T(8,128)(2,1)S(1)} %get-tuple-element.28.cot_ref.refs_0_), channel_id=1, source_target_pairs={{1,0},{2,1},{3,2},{4,3},{5,4},{6,5},{7,6},{8,7},{9,8},{10,9},{11,1... | collective-permute-start | bytes 1572872 | tf_op jit(solution)/shard_map/ppermute | solution.py:381
  5.2 1.3 %collective-permute-done.1.after_ref.refs_1_ = bf16[128,2048]{1,0:T(8,128)(2,1)} collective-permute-done((bf16[128,2048]{1,0:T(8,128)(2,1)S(1)}, bf16[128,2048]{1,0:T(8,128)(2,1)}, u32[]{:S(2)}, u32[]{:S(2)}) %collective-permute-start.1) | collective-permute-done | bytes 524320 | tf_op jit(solution)/shard_map/ppermute | solution.py:381
  6.5 0.0 copy-start.4
  6.5 2.7 %tap_grad_slots.2 = (f32[2,2,2,128,128]{4,3,2,1,0:T(8,128)S(1)}, bf16[2,2,2,128,128]{4,3,2,1,0:T(8,128)(2,1)S(1)}) custom-call(s32[1]{0:T(128)} %bitcast.me_ref, bf16[128,2048]{1,0:T(8,128)(2,1)S(1)} %get-tuple-element.29.cot_ref.refs_0_, bf16[128,2048]{1,0:T(8,128)(2,1)} %collective-permute-done.1.after_ref.refs_1_, bf16[128,4096]{1,0:T(8,128)(2,1)S(1)} %bitcast.12, ...), custom_call_target="tpu_custom_call" | custom-call | flops 1207959552 | bytes 2359296 | tf_op jit(solution)/shard_map/tap_grad_slots/pallas_call | solution.py:152
  9.2 8.1 %collective-permute-start.2 = (bf16[2,2,2,128,128]{4,3,2,1,0:T(8,128)(2,1)S(1)}, bf16[2,2,2,128,128]{4,3,2,1,0:T(8,128)(2,1)S(1)}, u32[]{:S(2)}, u32[]{:S(2)}) collective-permute-start(bf16[2,2,2,128,128]{4,3,2,1,0:T(8,128)(2,1)S(1)} %get-tuple-element.31), channel_id=1, source_target_pairs={{0,1},{1,0},{2,3},{3,2},{4,5},{5,4},{6,7},{7,6},{8,9},{9,8},{10,11... | collective-permute-start | bytes 786440 | tf_op jit(solution)/shard_map/ppermute | solution.py:372
  17.3 3.6 %collective-permute-start.5 = (bf16[256,128]{1,0:T(8,128)(2,1)S(1)}, bf16[256,128]{1,0:T(8,128)(2,1)S(1)}, u32[]{:S(2)}, u32[]{:S(2)}) collective-permute-start(bf16[256,128]{1,0:T(8,128)(2,1)S(1)} %copy-done.4), channel_id=1, source_target_pairs={{0,12},{1,13},{2,14},{3,15},{4,8},{5,9},{6,10},{7,11},{8,4},{9,5},... | collective-permute-start | bytes 196616 | tf_op jit(solution)/shard_map/ppermute | solution.py:372
  20.9 0.0 collective-permute-start.4
  20.9 0.8 %collective-permute-start.3 = (bf16[256,128]{1,0:T(8,128)(2,1)S(1)}, bf16[256,128]{1,0:T(8,128)(2,1)S(1)}, u32[]{:S(2)}, u32[]{:S(2)}) collective-permute-start(bf16[256,128]{1,0:T(8,128)(2,1)S(1)} %copy-done.4), channel_id=1, source_target_pairs={{0,4},{1,5},{2,6},{3,7},{4,0},{5,1},{6,2},{7,3},{8,12},{9,13},{10,... | collective-permute-start | bytes 196616 | tf_op jit(solution)/shard_map/ppermute | solution.py:372
  21.7 3.7 %collective-permute-done.5 = bf16[256,128]{1,0:T(8,128)(2,1)S(1)} collective-permute-done((bf16[256,128]{1,0:T(8,128)(2,1)S(1)}, bf16[256,128]{1,0:T(8,128)(2,1)S(1)}, u32[]{:S(2)}, u32[]{:S(2)}) %collective-permute-start.5) | collective-permute-done | bytes 65568 | tf_op jit(solution)/shard_map/ppermute | solution.py:372
  25.4 2.3 %collective-permute-done.4 = bf16[256,128]{1,0:T(8,128)(2,1)S(1)} collective-permute-done((bf16[256,128]{1,0:T(8,128)(2,1)S(1)}, bf16[256,128]{1,0:T(8,128)(2,1)S(1)}, u32[]{:S(2)}, u32[]{:S(2)}) %collective-permute-start.4) | collective-permute-done | bytes 65568 | tf_op jit(solution)/shard_map/ppermute | solution.py:372
  27.7 0.0 collective-permute-done.3
  27.8 0.0 collective-permute-done.2.got_ref
  27.9 0.0 collective-permute-done.after_ref.refs_1_
  27.9 1.4 %collective-permute-start.6 = (bf16[4,256,128]{2,1,0:T(8,128)(2,1)S(1)}, bf16[4,256,128]{2,1,0:T(8,128)(2,1)S(1)}, u32[]{:S(2)}, u32[]{:S(2)}) collective-permute-start(bf16[4,256,128]{2,1,0:T(8,128)(2,1)S(1)} %get-tuple-element.39), channel_id=1, source_target_pairs={{0,2},{1,3},{2,0},{3,1},{4,6},{5,7},{6,4},{7,5},{8,10},{9,11},{10,... | collective-permute-start | bytes 786440 | tf_op jit(solution)/shard_map/ppermute | solution.py:372
  29.3 1.6 %tap_grad_slots.3 = (f32[2,2,2,128,128]{4,3,2,1,0:T(8,128)S(1)}, bf16[2,2,2,128,128]{4,3,2,1,0:T(8,128)(2,1)S(1)}) custom-call(s32[1]{0:T(128)} %bitcast.me_ref, bf16[128,2048]{1,0:T(8,128)(2,1)S(1)} %get-tuple-element.28.cot_ref.refs_0_, bf16[128,2048]{1,0:T(8,128)(2,1)S(1)} %collective-permute-done.after_ref.refs_1_, bf16[128,4096]{1,0:T(8,128)(2,1)S(1)} %bitcast.13, ...), custom_call_target="tpu_custom_call" | custom-call | flops 1207959552 | bytes 2359296 | tf_op jit(solution)/shard_map/tap_grad_slots/pallas_call | solution.py:152
  30.9 4.9 %collective-permute-done.6 = bf16[4,256,128]{2,1,0:T(8,128)(2,1)S(1)} collective-permute-done((bf16[4,256,128]{2,1,0:T(8,128)(2,1)S(1)}, bf16[4,256,128]{2,1,0:T(8,128)(2,1)S(1)}, u32[]{:S(2)}, u32[]{:S(2)}) %collective-permute-start.6) | collective-permute-done | bytes 262176 | tf_op jit(solution)/shard_map/ppermute | solution.py:372
  35.8 0.1 pad_maximum_fusion.refs_2_
  35.8 0.1 collective-permute-start.7
  35.9 0.5 collective-permute-start.11
  36.4 1.5 %collective-permute-start.8 = (bf16[2,128,128]{2,1,0:T(8,128)(2,1)S(1)}, bf16[2,128,128]{2,1,0:T(8,128)(2,1)S(1)}, u32[]{:S(2)}, u32[]{:S(2)}) collective-permute-start(bf16[2,128,128]{2,1,0:T(8,128)(2,1)S(1)} %get-tuple-element.42), channel_id=1, source_target_pairs={{0,16},{1,17},{2,18},{3,19},{4,20},{5,21},{6,22},{7,23},{8,24},{9,... | collective-permute-start | bytes 196616 | tf_op jit(solution)/shard_map/ppermute | solution.py:372
  37.9 0.8 %collective-permute-start.9 = (bf16[2,128,128]{2,1,0:T(8,128)(2,1)S(1)}, bf16[2,128,128]{2,1,0:T(8,128)(2,1)S(1)}, u32[]{:S(2)}, u32[]{:S(2)}) collective-permute-start(bf16[2,128,128]{2,1,0:T(8,128)(2,1)S(1)} %get-tuple-element.43), channel_id=1, source_target_pairs={{0,2},{1,3},{2,0},{3,1},{4,6},{5,7},{6,4},{7,5},{8,10},{9,11},{10,... | collective-permute-start | bytes 196616 | tf_op jit(solution)/shard_map/ppermute | solution.py:372
  38.7 1.2 %collective-permute-start.10 = (bf16[2,128,128]{2,1,0:T(8,128)(2,1)S(1)}, bf16[2,128,128]{2,1,0:T(8,128)(2,1)S(1)}, u32[]{:S(2)}, u32[]{:S(2)}) collective-permute-start(bf16[2,128,128]{2,1,0:T(8,128)(2,1)S(1)} %get-tuple-element.44), channel_id=1, source_target_pairs={{0,18},{1,19},{2,16},{3,17},{4,22},{5,23},{6,20},{7,21},{8,26},{9,... | collective-permute-start | bytes 196616 | tf_op jit(solution)/shard_map/ppermute | solution.py:372
  39.9 0.0 collective-permute-done.11.got_ref
  39.9 1.6 %collective-permute-start.12 = (bf16[2,128,128]{2,1,0:T(8,128)(2,1)S(1)}, bf16[2,128,128]{2,1,0:T(8,128)(2,1)S(1)}, u32[]{:S(2)}, u32[]{:S(2)}) collective-permute-start(bf16[2,128,128]{2,1,0:T(8,128)(2,1)S(1)} %get-tuple-element.47), channel_id=1, source_target_pairs={{0,16},{1,17},{2,18},{3,19},{4,20},{5,21},{6,22},{7,23},{8,24},{9,... | collective-permute-start | bytes 196616 | tf_op jit(solution)/shard_map/ppermute | solution.py:372
  41.5 0.8 %collective-permute-start.13 = (bf16[2,128,128]{2,1,0:T(8,128)(2,1)S(1)}, bf16[2,128,128]{2,1,0:T(8,128)(2,1)S(1)}, u32[]{:S(2)}, u32[]{:S(2)}) collective-permute-start(bf16[2,128,128]{2,1,0:T(8,128)(2,1)S(1)} %get-tuple-element.48), channel_id=1, source_target_pairs={{0,2},{1,3},{2,0},{3,1},{4,6},{5,7},{6,4},{7,5},{8,10},{9,11},{10,... | collective-permute-start | bytes 196616 | tf_op jit(solution)/shard_map/ppermute | solution.py:372
  42.3 0.5 collective-permute-done.9.refs_2_
  42.9 0.9 %collective-permute-start.14 = (bf16[2,128,128]{2,1,0:T(8,128)(2,1)S(1)}, bf16[2,128,128]{2,1,0:T(8,128)(2,1)S(1)}, u32[]{:S(2)}, u32[]{:S(2)}) collective-permute-start(bf16[2,128,128]{2,1,0:T(8,128)(2,1)S(1)} %get-tuple-element.49), channel_id=1, source_target_pairs={{0,18},{1,19},{2,16},{3,17},{4,22},{5,23},{6,20},{7,21},{8,26},{9,... | collective-permute-start | bytes 196616 | tf_op jit(solution)/shard_map/ppermute | solution.py:372
  43.8 0.2 collective-permute-done.10.refs_3_
  44.0 0.4 collective-permute-done.12.refs_5_
  44.4 1.6 %collective-permute-done.13.refs_6_ = bf16[2,128,128]{2,1,0:T(8,128)(2,1)S(1)} collective-permute-done((bf16[2,128,128]{2,1,0:T(8,128)(2,1)S(1)}, bf16[2,128,128]{2,1,0:T(8,128)(2,1)S(1)}, u32[]{:S(2)}, u32[]{:S(2)}) %collective-permute-start.13) | collective-permute-done | bytes 65568 | tf_op jit(solution)/shard_map/ppermute | solution.py:372
  46.0 2.0 %collective-permute-done.14.refs_7_ = bf16[2,128,128]{2,1,0:T(8,128)(2,1)S(1)} collective-permute-done((bf16[2,128,128]{2,1,0:T(8,128)(2,1)S(1)}, bf16[2,128,128]{2,1,0:T(8,128)(2,1)S(1)}, u32[]{:S(2)}, u32[]{:S(2)}) %collective-permute-start.14) | collective-permute-done | bytes 65568 | tf_op jit(solution)/shard_map/ppermute | solution.py:372
  48.0 0.1 along_line.1
  48.1 0.1 collective-permute-start.15
  48.2 2.9 %collective-permute-start.16 = (bf16[128,128]{1,0:T(8,128)(2,1)S(1)}, bf16[128,128]{1,0:T(8,128)(2,1)S(1)}, u32[]{:S(2)}, u32[]{:S(2)}) collective-permute-start(bf16[128,128]{1,0:T(8,128)(2,1)S(1)} %get-tuple-element.52), channel_id=1, source_target_pairs={{0,8},{1,9},{2,10},{3,11},{4,12},{5,13},{6,14},{7,15},{8,0},{9,1},... | collective-permute-start | bytes 98312 | tf_op jit(solution)/shard_map/ppermute | solution.py:372
  51.1 1.5 %collective-permute-start.17 = (bf16[128,128]{1,0:T(8,128)(2,1)S(1)}, bf16[128,128]{1,0:T(8,128)(2,1)S(1)}, u32[]{:S(2)}, u32[]{:S(2)}) collective-permute-start(bf16[128,128]{1,0:T(8,128)(2,1)S(1)} %get-tuple-element.53), channel_id=1, source_target_pairs={{0,12},{1,13},{2,14},{3,15},{4,8},{5,9},{6,10},{7,11},{8,4},{9,5},... | collective-permute-start | bytes 98312 | tf_op jit(solution)/shard_map/ppermute | solution.py:372
  52.6 0.8 %collective-permute-done.16.refs_1_ = bf16[128,128]{1,0:T(8,128)(2,1)S(1)} collective-permute-done((bf16[128,128]{1,0:T(8,128)(2,1)S(1)}, bf16[128,128]{1,0:T(8,128)(2,1)S(1)}, u32[]{:S(2)}, u32[]{:S(2)}) %collective-permute-start.16) | collective-permute-done | bytes 32800 | tf_op jit(solution)/shard_map/ppermute | solution.py:372
  53.3 3.5 %collective-permute-done.17.refs_2_ = bf16[128,128]{1,0:T(8,128)(2,1)S(1)} collective-permute-done((bf16[128,128]{1,0:T(8,128)(2,1)S(1)}, bf16[128,128]{1,0:T(8,128)(2,1)S(1)}, u32[]{:S(2)}, u32[]{:S(2)}) %collective-permute-start.17) | collective-permute-done | bytes 32800 | tf_op jit(solution)/shard_map/ppermute | solution.py:372
  56.8 0.1 finish.1.mine_ref
  56.9 0.9 %collective-permute-start.18 = (f32[128,128]{1,0:T(8,128)S(1)}, f32[128,128]{1,0:T(8,128)S(1)}, u32[]{:S(2)}, u32[]{:S(2)}) collective-permute-start(f32[128,128]{1,0:T(8,128)S(1)} %finish.1.mine_ref), channel_id=1, source_target_pairs={{0,16},{1,17},{2,18},{3,19},{4,20},{5,21},{6,22},{7,23},{8,24},{9,... | collective-permute-start | bytes 196616 | tf_op jit(solution)/shard_map/ppermute | solution.py:372
  57.8 3.5 %collective-permute-done.18.other_ref = f32[128,128]{1,0:T(8,128)S(1)} collective-permute-done((f32[128,128]{1,0:T(8,128)S(1)}, f32[128,128]{1,0:T(8,128)S(1)}, u32[]{:S(2)}, u32[]{:S(2)}) %collective-permute-start.18) | collective-permute-done | bytes 65568 | tf_op jit(solution)/shard_map/ppermute | solution.py:372
  61.2 0.7 join.1
  61.9 3.4 %value_grad_slots.2.refs_7_ = bf16[128,4096]{1,0:T(8,128)(2,1)} custom-call(s32[1]{0:T(128)} %bitcast.me_ref, bf16[128,2048]{1,0:T(8,128)(2,1)S(1)} %get-tuple-element.29.cot_ref.refs_0_, bf16[128,2048]{1,0:T(8,128)(2,1)} %collective-permute-done.1.after_ref.refs_1_, bf16[2,4,256,128]{3,2,1,0:T(8,128)(2,1)S(1)} %pad_maximum_fusion.refs_2_, ...), custom_call_target="tpu_custom_call" | custom-call | flops 1207959552 | bytes 2097152 | tf_op jit(solution)/shard_map/value_grad_slots/pallas_call | solution.py:312
  65.4 2.4 %value_grad_slots.3 = bf16[128,4096]{1,0:T(8,128)(2,1)} custom-call(s32[1]{0:T(128)} %bitcast.me_ref, bf16[128,2048]{1,0:T(8,128)(2,1)S(1)} %get-tuple-element.28.cot_ref.refs_0_, bf16[128,2048]{1,0:T(8,128)(2,1)S(1)} %collective-permute-done.after_ref.refs_1_, bf16[2,4,256,128]{3,2,1,0:T(8,128)(2,1)S(1)} %pad_maximum_fusion.refs_2_, ...), custom_call_target="tpu_custom_call", output_to_operand_aliasing={{}: (8, {})} | custom-call | flops 1207959552 | bytes 2097152 | tf_op jit(solution)/shard_map/value_grad_slots/pallas_call | solution.py:312
  (12 shorter events, 0.2 us)
Async XLA Ops:
  0.6 5.9 %copy-start = (bf16[512,256]{1,0:T(8,128)(2,1)S(1)}, bf16[512,256]{1,0:T(8,128)(2,1)}, u32[]{:S(2)}) copy-start(bf16[512,256]{1,0:T(8,128)(2,1)} %constant.17.clone.wx_ref.refs_4_) | copy-start | bytes 786436
  0.6 5.9 %copy-start.1 = (bf16[256,256]{1,0:T(8,128)(2,1)S(1)}, bf16[256,256]{1,0:T(8,128)(2,1)}, u32[]{:S(2)}) copy-start(bf16[256,256]{1,0:T(8,128)(2,1)} %constant.19.clone.wi_ref.refs_6_) | copy-start | bytes 393220
  0.7 5.8 %copy-start.2 = (bf16[256,256]{1,0:T(8,128)(2,1)S(1)}, bf16[256,256]{1,0:T(8,128)(2,1)}, u32[]{:S(2)}) copy-start(bf16[256,256]{1,0:T(8,128)(2,1)} %constant.18.clone.wv_ref.refs_5_) | copy-start | bytes 393220
  0.7 5.8 %copy-start.3 = (bf16[1,128,4096]{2,1,0:T(8,128)(2,1)S(1)}, bf16[1,128,4096]{2,1,0:T(8,128)(2,1)}, u32[]{:S(2)}) copy-start(bf16[1,128,4096]{2,1,0:T(8,128)(2,1)} %param.12) | copy-start | bytes 3145732
  2.6 3.9 %collective-permute-start.1 = (bf16[128,2048]{1,0:T(8,128)(2,1)S(1)}, bf16[128,2048]{1,0:T(8,128)(2,1)}, u32[]{:S(2)}, u32[]{:S(2)}) collective-permute-start(bf16[128,2048]{1,0:T(8,128)(2,1)S(1)} %get-tuple-element.29.cot_ref.refs_0_), channel_id=1, source_target_pairs={{1,0},{2,1},{3,2},{4,3},{5,4},{6,5},{7,6},{8,7},{9,8},{10,9},{11,1... | collective-permute-start | bytes 1572872 | tf_op jit(solution)/shard_map/ppermute | solution.py:381
  3.9 24.0 %collective-permute-start = (bf16[128,2048]{1,0:T(8,128)(2,1)S(1)}, bf16[128,2048]{1,0:T(8,128)(2,1)S(1)}, u32[]{:S(2)}, u32[]{:S(2)}) collective-permute-start(bf16[128,2048]{1,0:T(8,128)(2,1)S(1)} %get-tuple-element.28.cot_ref.refs_0_), channel_id=1, source_target_pairs={{1,0},{2,1},{3,2},{4,3},{5,4},{6,5},{7,6},{8,7},{9,8},{10,9},{11,1... | collective-permute-start | bytes 1572872 | tf_op jit(solution)/shard_map/ppermute | solution.py:381
  6.5 10.8 %copy-start.4 = (bf16[256,128]{1,0:T(8,128)(2,1)S(1)}, bf16[256,128]{1,0:T(8,128)(2,1)}, u32[]{:S(2)}) copy-start(bf16[256,128]{1,0:T(8,128)(2,1)} %param.14) | copy-start | bytes 196612
  9.2 18.6 %collective-permute-start.2 = (bf16[2,2,2,128,128]{4,3,2,1,0:T(8,128)(2,1)S(1)}, bf16[2,2,2,128,128]{4,3,2,1,0:T(8,128)(2,1)S(1)}, u32[]{:S(2)}, u32[]{:S(2)}) collective-permute-start(bf16[2,2,2,128,128]{4,3,2,1,0:T(8,128)(2,1)S(1)} %get-tuple-element.31), channel_id=1, source_target_pairs={{0,1},{1,0},{2,3},{3,2},{4,5},{5,4},{6,7},{7,6},{8,9},{9,8},{10,11... | collective-permute-start | bytes 786440 | tf_op jit(solution)/shard_map/ppermute | solution.py:372
  17.3 8.1 %collective-permute-start.5 = (bf16[256,128]{1,0:T(8,128)(2,1)S(1)}, bf16[256,128]{1,0:T(8,128)(2,1)S(1)}, u32[]{:S(2)}, u32[]{:S(2)}) collective-permute-start(bf16[256,128]{1,0:T(8,128)(2,1)S(1)} %copy-done.4), channel_id=1, source_target_pairs={{0,12},{1,13},{2,14},{3,15},{4,8},{5,9},{6,10},{7,11},{8,4},{9,5},... | collective-permute-start | bytes 196616 | tf_op jit(solution)/shard_map/ppermute | solution.py:372
  20.9 6.8 %collective-permute-start.4 = (bf16[256,128]{1,0:T(8,128)(2,1)S(1)}, bf16[256,128]{1,0:T(8,128)(2,1)S(1)}, u32[]{:S(2)}, u32[]{:S(2)}) collective-permute-start(bf16[256,128]{1,0:T(8,128)(2,1)S(1)} %copy-done.4), channel_id=1, source_target_pairs={{0,8},{1,9},{2,10},{3,11},{4,12},{5,13},{6,14},{7,15},{8,0},{9,1},... | collective-permute-start | bytes 196616 | tf_op jit(solution)/shard_map/ppermute | solution.py:372
  20.9 6.8 %collective-permute-start.3 = (bf16[256,128]{1,0:T(8,128)(2,1)S(1)}, bf16[256,128]{1,0:T(8,128)(2,1)S(1)}, u32[]{:S(2)}, u32[]{:S(2)}) collective-permute-start(bf16[256,128]{1,0:T(8,128)(2,1)S(1)} %copy-done.4), channel_id=1, source_target_pairs={{0,4},{1,5},{2,6},{3,7},{4,0},{5,1},{6,2},{7,3},{8,12},{9,13},{10,... | collective-permute-start | bytes 196616 | tf_op jit(solution)/shard_map/ppermute | solution.py:372
  27.9 7.9 %collective-permute-start.6 = (bf16[4,256,128]{2,1,0:T(8,128)(2,1)S(1)}, bf16[4,256,128]{2,1,0:T(8,128)(2,1)S(1)}, u32[]{:S(2)}, u32[]{:S(2)}) collective-permute-start(bf16[4,256,128]{2,1,0:T(8,128)(2,1)S(1)} %get-tuple-element.39), channel_id=1, source_target_pairs={{0,2},{1,3},{2,0},{3,1},{4,6},{5,7},{6,4},{7,5},{8,10},{9,11},{10,... | collective-permute-start | bytes 786440 | tf_op jit(solution)/shard_map/ppermute | solution.py:372
  35.8 26.1 %collective-permute-start.7 = (bf16[2,4,256,128]{3,2,1,0:T(8,128)(2,1)S(1)}, bf16[2,4,256,128]{3,2,1,0:T(8,128)(2,1)S(1)}, u32[]{:S(2)}, u32[]{:S(2)}) collective-permute-start(bf16[2,4,256,128]{3,2,1,0:T(8,128)(2,1)S(1)} %pad_maximum_fusion.refs_2_), channel_id=1, source_target_pairs={{0,1},{1,0},{2,3},{3,2},{4,5},{5,4},{6,7},{7,6},{8,9},{9,8},{10,11... | collective-permute-start | bytes 1572872 | tf_op jit(solution)/shard_map/ppermute | solution.py:372
  35.9 4.0 %collective-permute-start.11 = (bf16[2,2,2,128,128]{4,3,2,1,0:T(8,128)(2,1)S(1)}, bf16[2,2,2,128,128]{4,3,2,1,0:T(8,128)(2,1)S(1)}, u32[]{:S(2)}, u32[]{:S(2)}) collective-permute-start(bf16[2,2,2,128,128]{4,3,2,1,0:T(8,128)(2,1)S(1)} %get-tuple-element.40), channel_id=1, source_target_pairs={{0,1},{1,0},{2,3},{3,2},{4,5},{5,4},{6,7},{7,6},{8,9},{9,8},{10,11... | collective-permute-start | bytes 786440 | tf_op jit(solution)/shard_map/ppermute | solution.py:372
  36.4 5.1 %collective-permute-start.8 = (bf16[2,128,128]{2,1,0:T(8,128)(2,1)S(1)}, bf16[2,128,128]{2,1,0:T(8,128)(2,1)S(1)}, u32[]{:S(2)}, u32[]{:S(2)}) collective-permute-start(bf16[2,128,128]{2,1,0:T(8,128)(2,1)S(1)} %get-tuple-element.42), channel_id=1, source_target_pairs={{0,16},{1,17},{2,18},{3,19},{4,20},{5,21},{6,22},{7,23},{8,24},{9,... | collective-permute-start | bytes 196616 | tf_op jit(solution)/shard_map/ppermute | solution.py:372
  37.9 5.0 %collective-permute-start.9 = (bf16[2,128,128]{2,1,0:T(8,128)(2,1)S(1)}, bf16[2,128,128]{2,1,0:T(8,128)(2,1)S(1)}, u32[]{:S(2)}, u32[]{:S(2)}) collective-permute-start(bf16[2,128,128]{2,1,0:T(8,128)(2,1)S(1)} %get-tuple-element.43), channel_id=1, source_target_pairs={{0,2},{1,3},{2,0},{3,1},{4,6},{5,7},{6,4},{7,5},{8,10},{9,11},{10,... | collective-permute-start | bytes 196616 | tf_op jit(solution)/shard_map/ppermute | solution.py:372
  38.7 5.3 %collective-permute-start.10 = (bf16[2,128,128]{2,1,0:T(8,128)(2,1)S(1)}, bf16[2,128,128]{2,1,0:T(8,128)(2,1)S(1)}, u32[]{:S(2)}, u32[]{:S(2)}) collective-permute-start(bf16[2,128,128]{2,1,0:T(8,128)(2,1)S(1)} %get-tuple-element.44), channel_id=1, source_target_pairs={{0,18},{1,19},{2,16},{3,17},{4,22},{5,23},{6,20},{7,21},{8,26},{9,... | collective-permute-start | bytes 196616 | tf_op jit(solution)/shard_map/ppermute | solution.py:372
  39.9 4.5 %collective-permute-start.12 = (bf16[2,128,128]{2,1,0:T(8,128)(2,1)S(1)}, bf16[2,128,128]{2,1,0:T(8,128)(2,1)S(1)}, u32[]{:S(2)}, u32[]{:S(2)}) collective-permute-start(bf16[2,128,128]{2,1,0:T(8,128)(2,1)S(1)} %get-tuple-element.47), channel_id=1, source_target_pairs={{0,16},{1,17},{2,18},{3,19},{4,20},{5,21},{6,22},{7,23},{8,24},{9,... | collective-permute-start | bytes 196616 | tf_op jit(solution)/shard_map/ppermute | solution.py:372
  41.5 4.5 %collective-permute-start.13 = (bf16[2,128,128]{2,1,0:T(8,128)(2,1)S(1)}, bf16[2,128,128]{2,1,0:T(8,128)(2,1)S(1)}, u32[]{:S(2)}, u32[]{:S(2)}) collective-permute-start(bf16[2,128,128]{2,1,0:T(8,128)(2,1)S(1)} %get-tuple-element.48), channel_id=1, source_target_pairs={{0,2},{1,3},{2,0},{3,1},{4,6},{5,7},{6,4},{7,5},{8,10},{9,11},{10,... | collective-permute-start | bytes 196616 | tf_op jit(solution)/shard_map/ppermute | solution.py:372
  42.9 5.2 %collective-permute-start.14 = (bf16[2,128,128]{2,1,0:T(8,128)(2,1)S(1)}, bf16[2,128,128]{2,1,0:T(8,128)(2,1)S(1)}, u32[]{:S(2)}, u32[]{:S(2)}) collective-permute-start(bf16[2,128,128]{2,1,0:T(8,128)(2,1)S(1)} %get-tuple-element.49), channel_id=1, source_target_pairs={{0,18},{1,19},{2,16},{3,17},{4,22},{5,23},{6,20},{7,21},{8,26},{9,... | collective-permute-start | bytes 196616 | tf_op jit(solution)/shard_map/ppermute | solution.py:372
  48.1 4.5 %collective-permute-start.15 = (bf16[128,128]{1,0:T(8,128)(2,1)S(1)}, bf16[128,128]{1,0:T(8,128)(2,1)S(1)}, u32[]{:S(2)}, u32[]{:S(2)}) collective-permute-start(bf16[128,128]{1,0:T(8,128)(2,1)S(1)} %get-tuple-element.51), channel_id=1, source_target_pairs={{0,4},{1,5},{2,6},{3,7},{4,0},{5,1},{6,2},{7,3},{8,12},{9,13},{10,... | collective-permute-start | bytes 98312 | tf_op jit(solution)/shard_map/ppermute | solution.py:372
  48.2 5.1 %collective-permute-start.16 = (bf16[128,128]{1,0:T(8,128)(2,1)S(1)}, bf16[128,128]{1,0:T(8,128)(2,1)S(1)}, u32[]{:S(2)}, u32[]{:S(2)}) collective-permute-start(bf16[128,128]{1,0:T(8,128)(2,1)S(1)} %get-tuple-element.52), channel_id=1, source_target_pairs={{0,8},{1,9},{2,10},{3,11},{4,12},{5,13},{6,14},{7,15},{8,0},{9,1},... | collective-permute-start | bytes 98312 | tf_op jit(solution)/shard_map/ppermute | solution.py:372
  51.1 5.7 %collective-permute-start.17 = (bf16[128,128]{1,0:T(8,128)(2,1)S(1)}, bf16[128,128]{1,0:T(8,128)(2,1)S(1)}, u32[]{:S(2)}, u32[]{:S(2)}) collective-permute-start(bf16[128,128]{1,0:T(8,128)(2,1)S(1)} %get-tuple-element.53), channel_id=1, source_target_pairs={{0,12},{1,13},{2,14},{3,15},{4,8},{5,9},{6,10},{7,11},{8,4},{9,5},... | collective-permute-start | bytes 98312 | tf_op jit(solution)/shard_map/ppermute | solution.py:372
  56.9 4.3 %collective-permute-start.18 = (f32[128,128]{1,0:T(8,128)S(1)}, f32[128,128]{1,0:T(8,128)S(1)}, u32[]{:S(2)}, u32[]{:S(2)}) collective-permute-start(f32[128,128]{1,0:T(8,128)S(1)} %finish.1.mine_ref), channel_id=1, source_target_pairs={{0,16},{1,17},{2,18},{3,19},{4,20},{5,21},{6,22},{7,23},{8,24},{9,... | collective-permute-start | bytes 196616 | tf_op jit(solution)/shard_map/ppermute | solution.py:372

commit v4 on v3

--- a/solution.py
+++ b/solution.py
@@ -161,6 +161,25 @@
     )(me, cotangent, after, values, wx, wv, wi)
 
 
+def collect_kernel(*refs):
+    *ins, out_ref = refs
+    for i, ref in enumerate(ins):
+        out_ref[i] = ref[...]
+
+
+def collect(arrays):
+    first = arrays[0]
+    return pl.pallas_call(
+        collect_kernel,
+        in_specs=[VMEM_SPEC] * len(arrays),
+        out_specs=VMEM_SPEC,
+        out_shape=jax.ShapeDtypeStruct((len(arrays), *first.shape), first.dtype),
+        compiler_params=params(8),
+        cost_estimate=cost(1, 4 * len(arrays) * first.size),
+        name="collect",
+    )(*arrays)
+
+
 def spread_kernel(keep_ref, got_ref, mine_ref, *out_refs):
     mine_ref[...] = keep_ref[0, 0] + got_ref[0, 0].astype(F32)
     for (x, y), out_ref in zip(((1, 0), (0, 1), (1, 1)), out_refs):
@@ -371,27 +390,22 @@
     def swap(x, bits):
         return lax.ppermute(x, AXES, [(i, i ^ bits) for i in range(devices)])
 
-    def after_both(x, *others):
-        return lax.optimization_barrier((x, *others))[0]
-
     hops = (parts, 2, parts + 2)
+    line = [filters] + [swap(filters, 4 * k) for k in range(1, depth)]
+
     cots = cotangent_of(token_ids, queries, out_grad, 2)
     afters = []
     for cot in cots:
         afters.append(lax.ppermute(cot, "ctx", back))
 
-    filters = after_both(filters, cots[0])
-    line = [filters] + [swap(filters, 4 * k) for k in range(1, depth)]
-
     keep, send = tap_grad_slots(me, cots[0], afters[0], gated_values, 0, taps)
     own, *sends = spread(keep, swap(send, 1))
     sums = [[own] + [swap(x, bits) for x, bits in zip(sends, hops)]]
 
-    afters[1], own = lax.optimization_barrier((afters[1], own))
-    line = jnp.stack(lax.optimization_barrier((*line, own))[:-1])
-    line_y = swap(after_both(line, afters[1]), 2)
+    line = collect(line)
+    line_y = swap(line, 2)
     keep, send = tap_grad_slots(me, cots[1], afters[1], gated_values, 1, taps)
-    mine = jnp.stack([line, after_both(line_y, send)])
+    mine = collect([line, line_y])
     own, *sends = spread(keep, swap(send, 1))
     sums.append([own] + [swap(x, bits) for x, bits in zip(sends, hops)])
     other = swap(mine, 1)

time: 68 us -> 64.9 us (0.954)
  starting transfers between devices: 29.1 us -> 22.5 us
  waiting for transfers between devices: 24.8 us -> 28.1 us
    ppermute x17, starting transfers between devices: 26.5 us -> 19.7 us  [swap(): return lax.ppermute(x, AXES, [(i, i ^ bits) for i in range(devices)])]
    ppermute x17, waiting for transfers between devices: 23.4 us -> 28.1 us  [swap(): return lax.ppermute(x, AXES, [(i, i ^ bits) for i in range(devices)])]
    ppermute x2, waiting for transfers between devices: 1.33 us -> 0.01 us  [body(): afters.append(lax.ppermute(cot, 'ctx', back))]
  transfers between devices with their start and end apart: 19 -> 19, of which waited for: 12 -> 9; matrix products, arithmetic and copies ran while one was open for 0% -> 0% of each run, Pallas kernels for 8% -> 16%
where the time goes in v4:
time: 64.9 us; the launch traced here: 64.6 us
  waiting for transfers between devices  28.1 us (43%)
  starting transfers between devices  22.5 us (35%)
  Pallas kernels  13.1 us (20%)
  between operations  0.87 us (1%)
    ppermute x17, waiting for transfers between devices, swap(): return lax.ppermute(x, AXES, [(i, i ^ bits) for i in range(devices)])  28.1 us
    ppermute x17, starting transfers between devices, swap(): return lax.ppermute(x, AXES, [(i, i ^ bits) for i in range(devices)])  19.7 us
    pallas_call x2, Pallas kernels, value_grad_slots(): pl.pallas_call(functools.partial(value_grad_slots_kernel, piece, count),...  5.99 us
    pallas_call x2, Pallas kernels, tap_grad_slots(): pl.pallas_call(functools.partial(tap_grad_slots_kernel, first), in_specs=...  4.35 us
    ppermute x2, starting transfers between devices, body(): afters.append(lax.ppermute(cot, 'ctx', back))  2.72 us
    pallas_call x1, Pallas kernels, cotangent_of(): pl.pallas_call(cotangent_kernel, in_specs=[HBM_SPEC] * 3, out_specs=[VMEM...  1.79 us
  transfers between devices with their start and end apart: 19, of which 9 were waited for; matrix products, arithmetic and copies ran while one was open for 0% of the time, Pallas kernels for 16%

profile of v4, /device:TPU:0, one launch (start us, length us, event | category | flops | bytes accessed | tf_op | source)
XLA Modules:
  0.0 64.6 jit_solution(8369719176169441277)
XLA Ops:
  0.6 1.8 %cotangent.1 = (bf16[128,2048]{1,0:T(8,128)(2,1)S(1)}, bf16[128,2048]{1,0:T(8,128)(2,1)S(1)}) custom-call(s32[1,128]{1,0:T(1,128)} %ids_hbm.1, bf16[128,4096]{1,0:T(8,128)(2,1)} %bitcast.8, bf16[128,4096]{1,0:T(8,128)(2,1)} %bitcast.9), custom_call_target="tpu_custom_call" | custom-call | flops 1048576 | bytes 3145728 | tf_op jit(solution)/shard_map/cotangent/pallas_call | solution.py:108
  2.4 0.0 copy-start.4
  2.4 1.4 %collective-permute-start = (bf16[128,2048]{1,0:T(8,128)(2,1)S(1)}, bf16[128,2048]{1,0:T(8,128)(2,1)S(1)}, u32[]{:S(2)}, u32[]{:S(2)}) collective-permute-start(bf16[128,2048]{1,0:T(8,128)(2,1)S(1)} %get-tuple-element.20.refs_0_.cot_ref), channel_id=1, source_target_pairs={{1,0},{2,1},{3,2},{4,3},{5,4},{6,5},{7,6},{8,7},{9,8},{10,9},{11,1... | collective-permute-start | bytes 1572872 | tf_op jit(solution)/shard_map/ppermute | solution.py:399
  3.9 1.3 %collective-permute-start.6 = (bf16[128,2048]{1,0:T(8,128)(2,1)S(1)}, bf16[128,2048]{1,0:T(8,128)(2,1)}, u32[]{:S(2)}, u32[]{:S(2)}) collective-permute-start(bf16[128,2048]{1,0:T(8,128)(2,1)S(1)} %get-tuple-element.21.refs_0_.cot_ref), channel_id=1, source_target_pairs={{1,0},{2,1},{3,2},{4,3},{5,4},{6,5},{7,6},{8,7},{9,8},{10,9},{11,1... | collective-permute-start | bytes 1572872 | tf_op jit(solution)/shard_map/ppermute | solution.py:399
  5.2 5.9 %collective-permute-start.1 = (bf16[256,128]{1,0:T(8,128)(2,1)S(1)}, bf16[256,128]{1,0:T(8,128)(2,1)S(1)}, u32[]{:S(2)}, u32[]{:S(2)}) collective-permute-start(bf16[256,128]{1,0:T(8,128)(2,1)S(1)} %copy-done.3), channel_id=1, source_target_pairs={{0,4},{1,5},{2,6},{3,7},{4,0},{5,1},{6,2},{7,3},{8,12},{9,13},{10,... | collective-permute-start | bytes 196616 | tf_op jit(solution)/shard_map/ppermute | solution.py:391
  11.1 2.6 %collective-permute-start.2 = (bf16[256,128]{1,0:T(8,128)(2,1)S(1)}, bf16[256,128]{1,0:T(8,128)(2,1)S(1)}, u32[]{:S(2)}, u32[]{:S(2)}) collective-permute-start(bf16[256,128]{1,0:T(8,128)(2,1)S(1)} %copy-done.3), channel_id=1, source_target_pairs={{0,8},{1,9},{2,10},{3,11},{4,12},{5,13},{6,14},{7,15},{8,0},{9,1},... | collective-permute-start | bytes 196616 | tf_op jit(solution)/shard_map/ppermute | solution.py:391
  13.7 0.0 collective-permute-start.3
  13.7 10.3 %collective-permute-done.1.refs_1_ = bf16[256,128]{1,0:T(8,128)(2,1)S(1)} collective-permute-done((bf16[256,128]{1,0:T(8,128)(2,1)S(1)}, bf16[256,128]{1,0:T(8,128)(2,1)S(1)}, u32[]{:S(2)}, u32[]{:S(2)}) %collective-permute-start.1) | collective-permute-done | bytes 65568 | tf_op jit(solution)/shard_map/ppermute | solution.py:391
  24.0 1.7 %collective-permute-done.2.refs_2_ = bf16[256,128]{1,0:T(8,128)(2,1)S(1)} collective-permute-done((bf16[256,128]{1,0:T(8,128)(2,1)S(1)}, bf16[256,128]{1,0:T(8,128)(2,1)S(1)}, u32[]{:S(2)}, u32[]{:S(2)}) %collective-permute-start.2) | collective-permute-done | bytes 65568 | tf_op jit(solution)/shard_map/ppermute | solution.py:391
  25.7 1.8 %collective-permute-done.3.refs_3_ = bf16[256,128]{1,0:T(8,128)(2,1)S(1)} collective-permute-done((bf16[256,128]{1,0:T(8,128)(2,1)S(1)}, bf16[256,128]{1,0:T(8,128)(2,1)S(1)}, u32[]{:S(2)}, u32[]{:S(2)}) %collective-permute-start.3) | collective-permute-done | bytes 65568 | tf_op jit(solution)/shard_map/ppermute | solution.py:391
  27.5 0.1 collective-permute-start.4
  27.6 0.0 copy-start
  27.6 0.0 copy-start.1
  27.7 0.0 copy-start.2
  27.7 6.3 %collective-permute-done.4.refs_1_ = bf16[4,256,128]{2,1,0:T(8,128)(2,1)S(1)} collective-permute-done((bf16[4,256,128]{2,1,0:T(8,128)(2,1)S(1)}, bf16[4,256,128]{2,1,0:T(8,128)(2,1)S(1)}, u32[]{:S(2)}, u32[]{:S(2)}) %collective-permute-start.4) | collective-permute-done | bytes 262176 | tf_op jit(solution)/shard_map/ppermute | solution.py:391
  34.0 0.1 collective-permute-start.5
  34.1 0.0 collective-permute-done.refs_1_.after_ref
  34.2 1.7 %tap_grad_slots.3 = (f32[2,2,2,128,128]{4,3,2,1,0:T(8,128)S(1)}, bf16[2,2,2,128,128]{4,3,2,1,0:T(8,128)(2,1)S(1)}) custom-call(s32[1]{0:T(128)} %bitcast.me_ref, bf16[128,2048]{1,0:T(8,128)(2,1)S(1)} %get-tuple-element.20.refs_0_.cot_ref, bf16[128,2048]{1,0:T(8,128)(2,1)S(1)} %collective-permute-done.refs_1_.after_ref, bf16[128,4096]{1,0:T(8,128)(2,1)S(1)} %bitcast.5, ...), custom_call_target="tpu_custom_call" | custom-call | flops 1207959552 | bytes 2359296 | tf_op jit(solution)/shard_map/tap_grad_slots/pallas_call | solution.py:152
  35.8 0.5 collective-permute-start.11
  36.4 0.0 collective-permute-done.6.refs_1_.after_ref
  36.4 2.7 %tap_grad_slots.2 = (f32[2,2,2,128,128]{4,3,2,1,0:T(8,128)S(1)}, bf16[2,2,2,128,128]{4,3,2,1,0:T(8,128)(2,1)S(1)}) custom-call(s32[1]{0:T(128)} %bitcast.me_ref, bf16[128,2048]{1,0:T(8,128)(2,1)S(1)} %get-tuple-element.21.refs_0_.cot_ref, bf16[128,2048]{1,0:T(8,128)(2,1)} %collective-permute-done.6.refs_1_.after_ref, bf16[128,4096]{1,0:T(8,128)(2,1)S(1)} %bitcast.6, ...), custom_call_target="tpu_custom_call" | custom-call | flops 1207959552 | bytes 2359296 | tf_op jit(solution)/shard_map/tap_grad_slots/pallas_call | solution.py:152
  39.1 0.1 collective-permute-start.7
  39.2 0.0 collective-permute-done.11.got_ref
  39.2 1.6 %collective-permute-start.12 = (bf16[2,128,128]{2,1,0:T(8,128)(2,1)S(1)}, bf16[2,128,128]{2,1,0:T(8,128)(2,1)S(1)}, u32[]{:S(2)}, u32[]{:S(2)}) collective-permute-start(bf16[2,128,128]{2,1,0:T(8,128)(2,1)S(1)} %get-tuple-element.31), channel_id=1, source_target_pairs={{0,16},{1,17},{2,18},{3,19},{4,20},{5,21},{6,22},{7,23},{8,24},{9,... | collective-permute-start | bytes 196616 | tf_op jit(solution)/shard_map/ppermute | solution.py:391
  40.8 0.0 collective-permute-start.13
  40.8 2.0 %collective-permute-start.14 = (bf16[2,128,128]{2,1,0:T(8,128)(2,1)S(1)}, bf16[2,128,128]{2,1,0:T(8,128)(2,1)S(1)}, u32[]{:S(2)}, u32[]{:S(2)}) collective-permute-start(bf16[2,128,128]{2,1,0:T(8,128)(2,1)S(1)} %get-tuple-element.33), channel_id=1, source_target_pairs={{0,18},{1,19},{2,16},{3,17},{4,22},{5,23},{6,20},{7,21},{8,26},{9,... | collective-permute-start | bytes 196616 | tf_op jit(solution)/shard_map/ppermute | solution.py:391
  42.8 0.0 collective-permute-done.7.got_ref
  42.8 1.0 %collective-permute-start.10 = (bf16[2,128,128]{2,1,0:T(8,128)(2,1)S(1)}, bf16[2,128,128]{2,1,0:T(8,128)(2,1)S(1)}, u32[]{:S(2)}, u32[]{:S(2)}) collective-permute-start(bf16[2,128,128]{2,1,0:T(8,128)(2,1)S(1)} %get-tuple-element.27), channel_id=1, source_target_pairs={{0,18},{1,19},{2,16},{3,17},{4,22},{5,23},{6,20},{7,21},{8,26},{9,... | collective-permute-start | bytes 196616 | tf_op jit(solution)/shard_map/ppermute | solution.py:391
  43.8 0.0 collective-permute-done.12.refs_5_
  43.8 1.4 %collective-permute-start.8 = (bf16[2,128,128]{2,1,0:T(8,128)(2,1)S(1)}, bf16[2,128,128]{2,1,0:T(8,128)(2,1)S(1)}, u32[]{:S(2)}, u32[]{:S(2)}) collective-permute-start(bf16[2,128,128]{2,1,0:T(8,128)(2,1)S(1)} %get-tuple-element.25), channel_id=1, source_target_pairs={{0,16},{1,17},{2,18},{3,19},{4,20},{5,21},{6,22},{7,23},{8,24},{9,... | collective-permute-start | bytes 196616 | tf_op jit(solution)/shard_map/ppermute | solution.py:391
  45.2 1.9 %collective-permute-done.13.refs_6_ = bf16[2,128,128]{2,1,0:T(8,128)(2,1)S(1)} collective-permute-done((bf16[2,128,128]{2,1,0:T(8,128)(2,1)S(1)}, bf16[2,128,128]{2,1,0:T(8,128)(2,1)S(1)}, u32[]{:S(2)}, u32[]{:S(2)}) %collective-permute-start.13) | collective-permute-done | bytes 65568 | tf_op jit(solution)/shard_map/ppermute | solution.py:391
  47.1 0.0 collective-permute-start.9
  47.2 0.0 collective-permute-done.14.refs_7_
  47.2 1.5 %collective-permute-done.10.refs_3_ = bf16[2,128,128]{2,1,0:T(8,128)(2,1)S(1)} collective-permute-done((bf16[2,128,128]{2,1,0:T(8,128)(2,1)S(1)}, bf16[2,128,128]{2,1,0:T(8,128)(2,1)S(1)}, u32[]{:S(2)}, u32[]{:S(2)}) %collective-permute-start.10) | collective-permute-done | bytes 65568 | tf_op jit(solution)/shard_map/ppermute | solution.py:391
  48.6 0.3 collective-permute-done.8.refs_1_
  49.0 2.5 %collective-permute-done.9.refs_2_ = bf16[2,128,128]{2,1,0:T(8,128)(2,1)S(1)} collective-permute-done((bf16[2,128,128]{2,1,0:T(8,128)(2,1)S(1)}, bf16[2,128,128]{2,1,0:T(8,128)(2,1)S(1)}, u32[]{:S(2)}, u32[]{:S(2)}) %collective-permute-start.9) | collective-permute-done | bytes 65568 | tf_op jit(solution)/shard_map/ppermute | solution.py:391
  51.4 0.1 along_line.1
  51.5 0.9 %collective-permute-start.15 = (bf16[128,128]{1,0:T(8,128)(2,1)S(1)}, bf16[128,128]{1,0:T(8,128)(2,1)S(1)}, u32[]{:S(2)}, u32[]{:S(2)}) collective-permute-start(bf16[128,128]{1,0:T(8,128)(2,1)S(1)} %get-tuple-element.35), channel_id=1, source_target_pairs={{0,4},{1,5},{2,6},{3,7},{4,0},{5,1},{6,2},{7,3},{8,12},{9,13},{10,... | collective-permute-start | bytes 98312 | tf_op jit(solution)/shard_map/ppermute | solution.py:391
  52.4 0.0 collective-permute-start.16
  52.4 3.5 %collective-permute-start.17 = (bf16[128,128]{1,0:T(8,128)(2,1)S(1)}, bf16[128,128]{1,0:T(8,128)(2,1)S(1)}, u32[]{:S(2)}, u32[]{:S(2)}) collective-permute-start(bf16[128,128]{1,0:T(8,128)(2,1)S(1)} %get-tuple-element.37), channel_id=1, source_target_pairs={{0,12},{1,13},{2,14},{3,15},{4,8},{5,9},{6,10},{7,11},{8,4},{9,5},... | collective-permute-start | bytes 98312 | tf_op jit(solution)/shard_map/ppermute | solution.py:391
  55.9 3.5 %value_grad_slots.2.refs_7_ = bf16[128,4096]{1,0:T(8,128)(2,1)} custom-call(s32[1]{0:T(128)} %bitcast.me_ref, bf16[128,2048]{1,0:T(8,128)(2,1)S(1)} %get-tuple-element.21.refs_0_.cot_ref, bf16[128,2048]{1,0:T(8,128)(2,1)} %collective-permute-done.6.refs_1_.after_ref, bf16[2,4,256,128]{3,2,1,0:T(8,128)(2,1)S(1)} %collect.3.refs_2_, ...), custom_call_target="tpu_custom_call" | custom-call | flops 1207959552 | bytes 2097152 | tf_op jit(solution)/shard_map/value_grad_slots/pallas_call | solution.py:331
  59.5 0.0 collective-permute-done.16.refs_1_
  59.5 0.0 collective-permute-done.17.refs_2_
  59.5 0.1 finish.1.mine_ref
  59.6 0.1 collective-permute-start.18
  59.7 2.5 %value_grad_slots.3 = bf16[128,4096]{1,0:T(8,128)(2,1)} custom-call(s32[1]{0:T(128)} %bitcast.me_ref, bf16[128,2048]{1,0:T(8,128)(2,1)S(1)} %get-tuple-element.20.refs_0_.cot_ref, bf16[128,2048]{1,0:T(8,128)(2,1)S(1)} %collective-permute-done.refs_1_.after_ref, bf16[2,4,256,128]{3,2,1,0:T(8,128)(2,1)S(1)} %collect.3.refs_2_, ...), custom_call_target="tpu_custom_call", output_to_operand_aliasing={{}: (8, {})} | custom-call | flops 1207959552 | bytes 2097152 | tf_op jit(solution)/shard_map/value_grad_slots/pallas_call | solution.py:331
  62.2 1.8 %collective-permute-done.18.other_ref = f32[128,128]{1,0:T(8,128)S(1)} collective-permute-done((f32[128,128]{1,0:T(8,128)S(1)}, f32[128,128]{1,0:T(8,128)S(1)}, u32[]{:S(2)}, u32[]{:S(2)}) %collective-permute-start.18) | collective-permute-done | bytes 65568 | tf_op jit(solution)/shard_map/ppermute | solution.py:391
  63.9 0.7 %join.1 = f32[256,128]{1,0:T(8,128)} custom-call(s32[1]{0:T(128)} %bitcast.me_ref, f32[128,128]{1,0:T(8,128)S(1)} %finish.1.mine_ref, f32[128,128]{1,0:T(8,128)S(1)} %collective-permute-done.18.other_ref), custom_call_target="tpu_custom_call" | custom-call | flops 1 | bytes 262144 | tf_op jit(solution)/shard_map/join/pallas_call | solution.py:266
  (12 shorter events, 0.2 us)
Async XLA Ops:
  0.6 4.6 %copy-start.3 = (bf16[256,128]{1,0:T(8,128)(2,1)S(1)}, bf16[256,128]{1,0:T(8,128)(2,1)}, u32[]{:S(2)}) copy-start(bf16[256,128]{1,0:T(8,128)(2,1)} %refs_0_.1) | copy-start | bytes 196612
  2.4 31.7 %copy-start.4 = (bf16[1,128,4096]{2,1,0:T(8,128)(2,1)S(1)}, bf16[1,128,4096]{2,1,0:T(8,128)(2,1)}, u32[]{:S(2)}) copy-start(bf16[1,128,4096]{2,1,0:T(8,128)(2,1)} %param.12) | copy-start | bytes 3145732
  2.4 31.7 %collective-permute-start = (bf16[128,2048]{1,0:T(8,128)(2,1)S(1)}, bf16[128,2048]{1,0:T(8,128)(2,1)S(1)}, u32[]{:S(2)}, u32[]{:S(2)}) collective-permute-start(bf16[128,2048]{1,0:T(8,128)(2,1)S(1)} %get-tuple-element.20.refs_0_.cot_ref), channel_id=1, source_target_pairs={{1,0},{2,1},{3,2},{4,3},{5,4},{6,5},{7,6},{8,7},{9,8},{10,9},{11,1... | collective-permute-start | bytes 1572872 | tf_op jit(solution)/shard_map/ppermute | solution.py:399
  3.9 32.5 %collective-permute-start.6 = (bf16[128,2048]{1,0:T(8,128)(2,1)S(1)}, bf16[128,2048]{1,0:T(8,128)(2,1)}, u32[]{:S(2)}, u32[]{:S(2)}) collective-permute-start(bf16[128,2048]{1,0:T(8,128)(2,1)S(1)} %get-tuple-element.21.refs_0_.cot_ref), channel_id=1, source_target_pairs={{1,0},{2,1},{3,2},{4,3},{5,4},{6,5},{7,6},{8,7},{9,8},{10,9},{11,1... | collective-permute-start | bytes 1572872 | tf_op jit(solution)/shard_map/ppermute | solution.py:399
  5.2 18.8 %collective-permute-start.1 = (bf16[256,128]{1,0:T(8,128)(2,1)S(1)}, bf16[256,128]{1,0:T(8,128)(2,1)S(1)}, u32[]{:S(2)}, u32[]{:S(2)}) collective-permute-start(bf16[256,128]{1,0:T(8,128)(2,1)S(1)} %copy-done.3), channel_id=1, source_target_pairs={{0,4},{1,5},{2,6},{3,7},{4,0},{5,1},{6,2},{7,3},{8,12},{9,13},{10,... | collective-permute-start | bytes 196616 | tf_op jit(solution)/shard_map/ppermute | solution.py:391
  11.1 14.6 %collective-permute-start.2 = (bf16[256,128]{1,0:T(8,128)(2,1)S(1)}, bf16[256,128]{1,0:T(8,128)(2,1)S(1)}, u32[]{:S(2)}, u32[]{:S(2)}) collective-permute-start(bf16[256,128]{1,0:T(8,128)(2,1)S(1)} %copy-done.3), channel_id=1, source_target_pairs={{0,8},{1,9},{2,10},{3,11},{4,12},{5,13},{6,14},{7,15},{8,0},{9,1},... | collective-permute-start | bytes 196616 | tf_op jit(solution)/shard_map/ppermute | solution.py:391
  13.7 13.9 %collective-permute-start.3 = (bf16[256,128]{1,0:T(8,128)(2,1)S(1)}, bf16[256,128]{1,0:T(8,128)(2,1)S(1)}, u32[]{:S(2)}, u32[]{:S(2)}) collective-permute-start(bf16[256,128]{1,0:T(8,128)(2,1)S(1)} %copy-done.3), channel_id=1, source_target_pairs={{0,12},{1,13},{2,14},{3,15},{4,8},{5,9},{6,10},{7,11},{8,4},{9,5},... | collective-permute-start | bytes 196616 | tf_op jit(solution)/shard_map/ppermute | solution.py:391
  27.5 6.4 %collective-permute-start.4 = (bf16[4,256,128]{2,1,0:T(8,128)(2,1)S(1)}, bf16[4,256,128]{2,1,0:T(8,128)(2,1)S(1)}, u32[]{:S(2)}, u32[]{:S(2)}) collective-permute-start(bf16[4,256,128]{2,1,0:T(8,128)(2,1)S(1)} %collect.2.refs_0_), channel_id=1, source_target_pairs={{0,2},{1,3},{2,0},{3,1},{4,6},{5,7},{6,4},{7,5},{8,10},{9,11},{10,... | collective-permute-start | bytes 786440 | tf_op jit(solution)/shard_map/ppermute | solution.py:391
  27.6 6.5 %copy-start = (bf16[512,256]{1,0:T(8,128)(2,1)S(1)}, bf16[512,256]{1,0:T(8,128)(2,1)}, u32[]{:S(2)}) copy-start(bf16[512,256]{1,0:T(8,128)(2,1)} %constant.17.clone.refs_4_.wx_ref) | copy-start | bytes 786436
  27.6 6.5 %copy-start.1 = (bf16[256,256]{1,0:T(8,128)(2,1)S(1)}, bf16[256,256]{1,0:T(8,128)(2,1)}, u32[]{:S(2)}) copy-start(bf16[256,256]{1,0:T(8,128)(2,1)} %constant.18.clone.refs_5_.wv_ref) | copy-start | bytes 393220
  27.7 6.5 %copy-start.2 = (bf16[256,256]{1,0:T(8,128)(2,1)S(1)}, bf16[256,256]{1,0:T(8,128)(2,1)}, u32[]{:S(2)}) copy-start(bf16[256,256]{1,0:T(8,128)(2,1)} %constant.19.clone.refs_6_.wi_ref) | copy-start | bytes 393220
  34.0 21.9 %collective-permute-start.5 = (bf16[2,4,256,128]{3,2,1,0:T(8,128)(2,1)S(1)}, bf16[2,4,256,128]{3,2,1,0:T(8,128)(2,1)S(1)}, u32[]{:S(2)}, u32[]{:S(2)}) collective-permute-start(bf16[2,4,256,128]{3,2,1,0:T(8,128)(2,1)S(1)} %collect.3.refs_2_), channel_id=1, source_target_pairs={{0,1},{1,0},{2,3},{3,2},{4,5},{5,4},{6,7},{7,6},{8,9},{9,8},{10,11... | collective-permute-start | bytes 1572872 | tf_op jit(solution)/shard_map/ppermute | solution.py:391
  35.8 3.3 %collective-permute-start.11 = (bf16[2,2,2,128,128]{4,3,2,1,0:T(8,128)(2,1)S(1)}, bf16[2,2,2,128,128]{4,3,2,1,0:T(8,128)(2,1)S(1)}, u32[]{:S(2)}, u32[]{:S(2)}) collective-permute-start(bf16[2,2,2,128,128]{4,3,2,1,0:T(8,128)(2,1)S(1)} %get-tuple-element.29), channel_id=1, source_target_pairs={{0,1},{1,0},{2,3},{3,2},{4,5},{5,4},{6,7},{7,6},{8,9},{9,8},{10,11... | collective-permute-start | bytes 786440 | tf_op jit(solution)/shard_map/ppermute | solution.py:391
  39.1 3.7 %collective-permute-start.7 = (bf16[2,2,2,128,128]{4,3,2,1,0:T(8,128)(2,1)S(1)}, bf16[2,2,2,128,128]{4,3,2,1,0:T(8,128)(2,1)S(1)}, u32[]{:S(2)}, u32[]{:S(2)}) collective-permute-start(bf16[2,2,2,128,128]{4,3,2,1,0:T(8,128)(2,1)S(1)} %get-tuple-element.23), channel_id=1, source_target_pairs={{0,1},{1,0},{2,3},{3,2},{4,5},{5,4},{6,7},{7,6},{8,9},{9,8},{10,11... | collective-permute-start | bytes 786440 | tf_op jit(solution)/shard_map/ppermute | solution.py:391
  39.2 4.6 %collective-permute-start.12 = (bf16[2,128,128]{2,1,0:T(8,128)(2,1)S(1)}, bf16[2,128,128]{2,1,0:T(8,128)(2,1)S(1)}, u32[]{:S(2)}, u32[]{:S(2)}) collective-permute-start(bf16[2,128,128]{2,1,0:T(8,128)(2,1)S(1)} %get-tuple-element.31), channel_id=1, source_target_pairs={{0,16},{1,17},{2,18},{3,19},{4,20},{5,21},{6,22},{7,23},{8,24},{9,... | collective-permute-start | bytes 196616 | tf_op jit(solution)/shard_map/ppermute | solution.py:391
  40.8 6.4 %collective-permute-start.13 = (bf16[2,128,128]{2,1,0:T(8,128)(2,1)S(1)}, bf16[2,128,128]{2,1,0:T(8,128)(2,1)S(1)}, u32[]{:S(2)}, u32[]{:S(2)}) collective-permute-start(bf16[2,128,128]{2,1,0:T(8,128)(2,1)S(1)} %get-tuple-element.32), channel_id=1, source_target_pairs={{0,2},{1,3},{2,0},{3,1},{4,6},{5,7},{6,4},{7,5},{8,10},{9,11},{10,... | collective-permute-start | bytes 196616 | tf_op jit(solution)/shard_map/ppermute | solution.py:391
  40.8 6.4 %collective-permute-start.14 = (bf16[2,128,128]{2,1,0:T(8,128)(2,1)S(1)}, bf16[2,128,128]{2,1,0:T(8,128)(2,1)S(1)}, u32[]{:S(2)}, u32[]{:S(2)}) collective-permute-start(bf16[2,128,128]{2,1,0:T(8,128)(2,1)S(1)} %get-tuple-element.33), channel_id=1, source_target_pairs={{0,18},{1,19},{2,16},{3,17},{4,22},{5,23},{6,20},{7,21},{8,26},{9,... | collective-permute-start | bytes 196616 | tf_op jit(solution)/shard_map/ppermute | solution.py:391
  42.8 5.8 %collective-permute-start.10 = (bf16[2,128,128]{2,1,0:T(8,128)(2,1)S(1)}, bf16[2,128,128]{2,1,0:T(8,128)(2,1)S(1)}, u32[]{:S(2)}, u32[]{:S(2)}) collective-permute-start(bf16[2,128,128]{2,1,0:T(8,128)(2,1)S(1)} %get-tuple-element.27), channel_id=1, source_target_pairs={{0,18},{1,19},{2,16},{3,17},{4,22},{5,23},{6,20},{7,21},{8,26},{9,... | collective-permute-start | bytes 196616 | tf_op jit(solution)/shard_map/ppermute | solution.py:391
  43.8 5.1 %collective-permute-start.8 = (bf16[2,128,128]{2,1,0:T(8,128)(2,1)S(1)}, bf16[2,128,128]{2,1,0:T(8,128)(2,1)S(1)}, u32[]{:S(2)}, u32[]{:S(2)}) collective-permute-start(bf16[2,128,128]{2,1,0:T(8,128)(2,1)S(1)} %get-tuple-element.25), channel_id=1, source_target_pairs={{0,16},{1,17},{2,18},{3,19},{4,20},{5,21},{6,22},{7,23},{8,24},{9,... | collective-permute-start | bytes 196616 | tf_op jit(solution)/shard_map/ppermute | solution.py:391
  47.1 4.3 %collective-permute-start.9 = (bf16[2,128,128]{2,1,0:T(8,128)(2,1)S(1)}, bf16[2,128,128]{2,1,0:T(8,128)(2,1)S(1)}, u32[]{:S(2)}, u32[]{:S(2)}) collective-permute-start(bf16[2,128,128]{2,1,0:T(8,128)(2,1)S(1)} %get-tuple-element.26), channel_id=1, source_target_pairs={{0,2},{1,3},{2,0},{3,1},{4,6},{5,7},{6,4},{7,5},{8,10},{9,11},{10,... | collective-permute-start | bytes 196616 | tf_op jit(solution)/shard_map/ppermute | solution.py:391
  51.5 8.0 %collective-permute-start.15 = (bf16[128,128]{1,0:T(8,128)(2,1)S(1)}, bf16[128,128]{1,0:T(8,128)(2,1)S(1)}, u32[]{:S(2)}, u32[]{:S(2)}) collective-permute-start(bf16[128,128]{1,0:T(8,128)(2,1)S(1)} %get-tuple-element.35), channel_id=1, source_target_pairs={{0,4},{1,5},{2,6},{3,7},{4,0},{5,1},{6,2},{7,3},{8,12},{9,13},{10,... | collective-permute-start | bytes 98312 | tf_op jit(solution)/shard_map/ppermute | solution.py:391
  52.4 7.1 %collective-permute-start.16 = (bf16[128,128]{1,0:T(8,128)(2,1)S(1)}, bf16[128,128]{1,0:T(8,128)(2,1)S(1)}, u32[]{:S(2)}, u32[]{:S(2)}) collective-permute-start(bf16[128,128]{1,0:T(8,128)(2,1)S(1)} %get-tuple-element.36), channel_id=1, source_target_pairs={{0,8},{1,9},{2,10},{3,11},{4,12},{5,13},{6,14},{7,15},{8,0},{9,1},... | collective-permute-start | bytes 98312 | tf_op jit(solution)/shard_map/ppermute | solution.py:391
  52.4 7.1 %collective-permute-start.17 = (bf16[128,128]{1,0:T(8,128)(2,1)S(1)}, bf16[128,128]{1,0:T(8,128)(2,1)S(1)}, u32[]{:S(2)}, u32[]{:S(2)}) collective-permute-start(bf16[128,128]{1,0:T(8,128)(2,1)S(1)} %get-tuple-element.37), channel_id=1, source_target_pairs={{0,12},{1,13},{2,14},{3,15},{4,8},{5,9},{6,10},{7,11},{8,4},{9,5},... | collective-permute-start | bytes 98312 | tf_op jit(solution)/shard_map/ppermute | solution.py:391
  59.6 4.3 %collective-permute-start.18 = (f32[128,128]{1,0:T(8,128)S(1)}, f32[128,128]{1,0:T(8,128)S(1)}, u32[]{:S(2)}, u32[]{:S(2)}) collective-permute-start(f32[128,128]{1,0:T(8,128)S(1)} %finish.1.mine_ref), channel_id=1, source_target_pairs={{0,16},{1,17},{2,18},{3,19},{4,20},{5,21},{6,22},{7,23},{8,24},{9,... | collective-permute-start | bytes 196616 | tf_op jit(solution)/shard_map/ppermute | solution.py:391

commit v5 on v4

--- a/solution.py
+++ b/solution.py
@@ -48,15 +48,22 @@
     return both[:rows] + both[rows:]
 
 
-def correlate(x, y, inverse):
+def cross(x, y):
     half = x.shape[0] // 2
     a, b, c, d = x[:half], x[half:], y[:half], y[half:]
-    product = jnp.concatenate([a * c + b * d, b * c - a * d], axis=0)
+    return jnp.concatenate([a * c + b * d, b * c - a * d], axis=0)
+
+
+def inverted(product, inverse):
     high = product.astype(BF16)
     low = (product - high.astype(F32)).astype(BF16)
     rows = inverse.shape[0] // 2
     both = mul(inverse, high)
     return both[:rows] + both[rows:] + mul(inverse[:rows], low)
+
+
+def spectrum_of_values(matrix, values):
+    return mul(matrix, jnp.concatenate([values, values], axis=0))
 
 
 VMEM_SPEC = pl.BlockSpec(memory_space=pltpu.VMEM)
@@ -119,46 +126,159 @@
     )(*(pltpu.with_memory_space_constraint(x, pltpu.HBM) for x in (token_ids, queries, out_grad)))
 
 
-def tap_grad_tile(cot_ref, after_ref, val_ref, wx_ref, wv_ref, wi_ref):
-    x = spectrum_of_window(wx_ref[...], cot_ref[...], after_ref[...])
-    values = val_ref[...]
-    y = mul(wv_ref[...], jnp.concatenate([values, values], axis=0))
-    return correlate(x, y, wi_ref[...])
-
-
-def tap_grad_slots_kernel(
-    first, me_ref, cot_ref, after_ref, val_ref, wx_ref, wv_ref, wi_ref, keep_ref, send_ref, tmp_ref
+def cotangent_pair_kernel(pieces, shard, me_ref, ids_hbm, q_hbm, g_hbm, *refs):
+    halos, (own_ref, other_ref) = refs[: 2 * pieces], refs[2 * pieces : 2 * pieces + 2]
+    ids_ref, q_ref, g_ref, sems, ids_sem = refs[2 * pieces + 2 :]
+    core0 = me_ref[0] // 2 % 2 == 0
+    width = q_ref.shape[1] // pieces
+    copies = []
+    ids_copy = pltpu.make_async_copy(ids_hbm, ids_ref, ids_sem)
+    ids_copy.start()
+    for i in range(pieces):
+        cols = pl.ds(i * width, width)
+        copies.append(
+            [
+                pltpu.make_async_copy(src.at[:, cols], dst.at[:, cols], sems.at[n, i])
+                for n, (src, dst) in enumerate(((q_hbm, q_ref), (g_hbm, g_ref)))
+            ]
+        )
+        for copy in copies[-1]:
+            copy.start()
+    positions = ids_ref.shape[1]
+    ids_copy.wait()
+    weight = jnp.where(ids_ref[...] < 4, 1.0, 0.1).astype(F32)
+    weight = jnp.broadcast_to(weight, (LANES, positions)).T
+
+    def cotangent(at):
+        cols = pl.ds(at, LANES)
+        return (weight * g_ref[:, cols].astype(F32) * q_ref[:, cols].astype(F32)).astype(BF16)
+
+    for i in range(pieces):
+        for copy in copies[i]:
+            copy.wait()
+        for at in range(0, width // 2, LANES):
+            source = i * width + at // shard * 2 * shard + at % shard
+            even, odd = cotangent(source), cotangent(source + shard)
+            halos[2 * i][:, at : at + LANES] = even
+            halos[2 * i + 1][:, at : at + LANES] = odd
+            cols = pl.ds(i * width // 2 + at, LANES)
+            own_ref[:, cols] = jnp.where(core0, even, odd)
+            other_ref[:, cols] = jnp.where(core0, odd, even)
+
+
+def cotangent_pair(me, token_ids, queries, out_grad, pieces, shard):
+    positions, channels = queries.shape
+    piece = jax.ShapeDtypeStruct((positions, channels // 2 // pieces), BF16)
+    half = jax.ShapeDtypeStruct((positions, channels // 2), BF16)
+    return pl.pallas_call(
+        functools.partial(cotangent_pair_kernel, pieces, shard),
+        in_specs=[SMEM_SPEC] + [HBM_SPEC] * 3,
+        out_specs=[VMEM_SPEC] * (2 * pieces + 2),
+        out_shape=[piece] * (2 * pieces) + [half] * 2,
+        scratch_shapes=[pltpu.VMEM(token_ids.shape, token_ids.dtype)]
+        + [pltpu.VMEM((positions, channels), BF16)] * 2
+        + [pltpu.SemaphoreType.DMA((2, pieces)), pltpu.SemaphoreType.DMA],
+        compiler_params=params(8),
+        cost_estimate=cost(2 * positions * channels, 8 * positions * channels),
+        name="cotangent_pair",
+    )(me, *(pltpu.with_memory_space_constraint(x, pltpu.HBM) for x in (token_ids, queries, out_grad)))
+
+
+def split_kernel(shard, me_ref, src_hbm, own_ref, other_ref, sems):
+    core = me_ref[0] // 2 % 2
+    copies = []
+    for n, (parity, ref) in enumerate(((core, own_ref), (1 - core, other_ref))):
+        for at in range(0, own_ref.shape[1], shard):
+            cols = pl.ds(pl.multiple_of(2 * at + parity * shard, shard), shard)
+            copy = pltpu.make_async_copy(
+                src_hbm.at[:, cols], ref.at[:, pl.ds(at, shard)], sems.at[n, at // shard]
+            )
+            copy.start()
+            copies.append(copy)
+    for copy in copies:
+        copy.wait()
+
+
+def split(me, values, shard):
+    positions, channels = values.shape
+    half = jax.ShapeDtypeStruct((positions, channels // 2), values.dtype)
+    return pl.pallas_call(
+        functools.partial(split_kernel, shard),
+        in_specs=[SMEM_SPEC, HBM_SPEC],
+        out_specs=[VMEM_SPEC] * 2,
+        out_shape=[half] * 2,
+        scratch_shapes=[pltpu.SemaphoreType.DMA((2, channels // 2 // shard))],
+        compiler_params=params(8),
+        cost_estimate=cost(1, 4 * positions * channels),
+        name="split",
+    )(me, pltpu.with_memory_space_constraint(values, pltpu.HBM))
+
+
+def near_window_kernel(
+    me_ref, own_ref, got_ref, val_ref, val_got_ref, wx_ref, wv_ref, x_ref, product_ref, v_ref
 ):
-    width = cot_ref.shape[1]
-    x = spectrum_of_window(wx_ref[...], cot_ref[...], after_ref[...])
-    values = val_ref[:, first * width : (first + 1) * width]
-    y = mul(wv_ref[...], jnp.concatenate([values, values], axis=0))
-    out = correlate(x, y, wi_ref[...])
-    low, row = me_ref[0] % 4, me_ref[0] // 4 % 2
-    for tile in range(width // (4 * LANES)):
-        for block in range(4):
-            at = (tile * 4 + block) * LANES
-            tmp_ref[tile, block ^ low] = out[:, at : at + LANES]
-        for half in range(2):
-            keep_ref[half, tile % 2 ^ row, tile // 2] = tmp_ref[tile, half]
-            send_ref[half, tile % 2 ^ row, tile // 2] = tmp_ref[tile, 2 + half].astype(BF16)
-
-
-def tap_grad_slots(me, cotangent, after, values, first, taps):
-    positions, width = cotangent.shape
-    wx, wv, _, wi, _ = transforms(positions, taps)
-    tiles = width // (4 * LANES)
-    shape = (2, 2, tiles // 2, taps, LANES)
-    return pl.pallas_call(
-        functools.partial(tap_grad_slots_kernel, first),
+    core0 = me_ref[0] // 2 % 2 == 0
+    own, got = own_ref[...], got_ref[...]
+    x = spectrum_of_window(wx_ref[...], jnp.where(core0, own, got), jnp.where(core0, got, own))
+    x_ref[...] = x
+    own, got = val_ref[...], val_got_ref[...]
+    v_ref[...] = spectrum_of_values(wv_ref[...], jnp.where(core0, got, own))
+    product_ref[...] = cross(x, spectrum_of_values(wv_ref[...], jnp.where(core0, own, got)))
+
+
+def near_window(me, own, got, values, values_got, taps):
+    positions, width = own.shape
+    wx, wv, _, _, _ = transforms(positions, taps)
+    spectrum = jax.ShapeDtypeStruct((wx.shape[1], width), F32)
+    return pl.pallas_call(
+        near_window_kernel,
         in_specs=[SMEM_SPEC] + [VMEM_SPEC] * 6,
-        out_specs=[VMEM_SPEC, VMEM_SPEC],
-        out_shape=[jax.ShapeDtypeStruct(shape, F32), jax.ShapeDtypeStruct(shape, BF16)],
-        scratch_shapes=[pltpu.VMEM((tiles, 4, taps, LANES), F32)],
+        out_specs=[VMEM_SPEC] * 3,
+        out_shape=[spectrum] * 3,
         compiler_params=params(24),
-        cost_estimate=cost(2 * 9 * 128 * 256 * width, 9 * positions * width),
-        name="tap_grad_slots",
-    )(me, cotangent, after, values, wx, wv, wi)
+        cost_estimate=cost(2 * 8 * 128 * 256 * width, 32 * positions * width),
+        name="near_window",
+    )(me, own, got, values, values_got, wx, wv)
+
+
+def tap_grad_kernel(
+    piece, me_ref, own_ref, got_ref, after0_ref, after1_ref, product_ref, v_ref, wx_ref, wi_ref, *refs
+):
+    mine_ref, *send_refs, x_ref, tmp_ref = refs
+    width = after0_ref.shape[1]
+    cols = pl.ds(piece * width, width)
+    me = me_ref[0]
+    core0, row, rank = me // 2 % 2 == 0, me // 4 % 2, me % 2
+    own = jnp.where(core0, got_ref[:, cols], own_ref[:, cols])
+    after = jnp.where(core0, after0_ref[...], after1_ref[...])
+    x = spectrum_of_window(wx_ref[...], own, after)
+    x_ref[...] = x
+    out = inverted(product_ref[:, cols] + cross(x, v_ref[:, cols]), wi_ref[...])
+    for block in range(width // LANES):
+        half, y, z = block % 2, block // 2 % 2, block // 4
+        tmp_ref[(half ^ rank) + 2 * (y ^ row), z] = out[:, block * LANES : (block + 1) * LANES]
+    mine_ref[...] = tmp_ref[0]
+    for k, ref in enumerate(send_refs, 1):
+        ref[...] = tmp_ref[k].astype(BF16)
+
+
+def tap_grad(me, own, got, afters, product, v, piece, taps):
+    positions, width = afters[0].shape
+    wx, _, _, wi, _ = transforms(positions, taps)
+    depth = width // (4 * LANES)
+    block = (depth, taps, LANES)
+    return pl.pallas_call(
+        functools.partial(tap_grad_kernel, piece),
+        in_specs=[SMEM_SPEC] + [VMEM_SPEC] * 8,
+        out_specs=[VMEM_SPEC] * 5,
+        out_shape=[jax.ShapeDtypeStruct(block, F32)]
+        + [jax.ShapeDtypeStruct(block, BF16)] * 3
+        + [jax.ShapeDtypeStruct((wx.shape[1], width), F32)],
+        scratch_shapes=[pltpu.VMEM((4, *block), F32)],
+        compiler_params=params(24),
+        cost_estimate=cost(2 * 7 * 128 * 256 * width, 24 * positions * width),
+        name="tap_grad",
+    )(me, own, got, *afters, product, v, wx, wi)
 
 
 def collect_kernel(*refs):
@@ -178,25 +298,6 @@
         cost_estimate=cost(1, 4 * len(arrays) * first.size),
         name="collect",
     )(*arrays)
-
-
-def spread_kernel(keep_ref, got_ref, mine_ref, *out_refs):
-    mine_ref[...] = keep_ref[0, 0] + got_ref[0, 0].astype(F32)
-    for (x, y), out_ref in zip(((1, 0), (0, 1), (1, 1)), out_refs):
-        out_ref[...] = (keep_ref[x, y] + got_ref[x, y].astype(F32)).astype(BF16)
-
-
-def spread(keep, got):
-    block = keep.shape[2:]
-    return pl.pallas_call(
-        spread_kernel,
-        in_specs=[VMEM_SPEC] * 2,
-        out_specs=[VMEM_SPEC] * 4,
-        out_shape=[jax.ShapeDtypeStruct(block, F32)] + [jax.ShapeDtypeStruct(block, BF16)] * 3,
-        compiler_params=params(8),
-        cost_estimate=cost(keep.size, 8 * keep.size),
-        name="spread",
-    )(keep, got)
 
 
 def line_kernel(pieces, me_ref, *refs):
@@ -254,28 +355,51 @@
     )(mine, *got)
 
 
-def join_kernel(me_ref, mine_ref, other_ref, out_ref):
-    rank = me_ref[0] % 2
-    rows = mine_ref.shape[0]
-    out_ref[pl.ds(pl.multiple_of(rank * rows, rows), rows), :] = mine_ref[...]
-    out_ref[pl.ds(pl.multiple_of((1 - rank) * rows, rows), rows), :] = other_ref[...]
-
-
-def join(me, mine, other):
-    rows, taps = mine.shape
-    return pl.pallas_call(
-        join_kernel,
-        in_specs=[SMEM_SPEC, VMEM_SPEC, VMEM_SPEC],
-        out_specs=VMEM_SPEC,
-        out_shape=jax.ShapeDtypeStruct((2 * rows, taps), F32),
-        compiler_params=params(8),
-        cost_estimate=cost(1, 16 * rows * taps),
-        name="join",
-    )(me, mine, other)
+def place_kernel(shard, me_ref, tap_ref, tap_got_ref, val_ref, val_got_ref, val_hbm, tap_hbm, sems, tap_sems):
+    core, rank = me_ref[0] // 2 % 2, me_ref[0] % 2
+    rows = tap_ref.shape[0]
+    copies = []
+    for n, (half, ref) in enumerate(((rank, tap_ref), (1 - rank, tap_got_ref))):
+        at = pl.ds(pl.multiple_of(half * rows, rows), rows)
+        copies.append(pltpu.make_async_copy(ref, tap_hbm.at[at, :], tap_sems.at[n]))
+    for n, (parity, ref) in enumerate(((core, val_ref), (1 - core, val_got_ref))):
+        for at in range(0, ref.shape[1], shard):
+            cols = pl.ds(pl.multiple_of(2 * at + parity * shard, shard), shard)
+            copies.append(
+                pltpu.make_async_copy(
+                    ref.at[:, pl.ds(at, shard)], val_hbm.at[:, cols], sems.at[n, at // shard]
+                )
+            )
+    for copy in copies:
+        copy.start()
+    for copy in copies:
+        copy.wait()
+
+
+def place(me, taps_mine, taps_got, values, values_got, shard):
+    rows, taps = taps_mine.shape
+    positions, width = values.shape
+    return pl.pallas_call(
+        functools.partial(place_kernel, shard),
+        in_specs=[SMEM_SPEC] + [VMEM_SPEC] * 4,
+        out_specs=[HBM_SPEC] * 2,
+        out_shape=[
+            jax.ShapeDtypeStruct((positions, 2 * width), values.dtype),
+            jax.ShapeDtypeStruct((2 * rows, taps), F32),
+        ],
+        scratch_shapes=[
+            pltpu.SemaphoreType.DMA((2, width // shard)),
+            pltpu.SemaphoreType.DMA((2,)),
+        ],
+        compiler_params=params(8),
+        cost_estimate=cost(1, 4 * positions * width),
+        name="place",
+    )(me, taps_mine, taps_got, values, values_got)
 
 
 def tap_grad_plain_kernel(cot_ref, after_ref, val_ref, wx_ref, wv_ref, wi_ref, o_ref):
-    o_ref[...] = tap_grad_tile(cot_ref, after_ref, val_ref, wx_ref, wv_ref, wi_ref)
+    x = spectrum_of_window(wx_ref[...], cot_ref[...], after_ref[...])
+    o_ref[...] = inverted(cross(x, spectrum_of_values(wv_ref[...], val_ref[...])), wi_ref[...])
 
 
 def tap_grad_plain(cotangent, after, values, taps, tile):
@@ -293,58 +417,53 @@
     )(cotangent, after, values, wx, wv, wi)
 
 
-def value_grad_tile(own, after, filters, wx_ref, wf_ref, wi_ref):
-    x = spectrum_of_window(wx_ref[...], own, after)
-    y = lax.dot_general(
-        wf_ref[...],
+def spectrum_of_filters(matrix, filters):
+    return lax.dot_general(
+        matrix,
         jnp.concatenate([filters, filters], axis=1),
         (((1,), (1,)), ((), ())),
         preferred_element_type=F32,
     )
-    return correlate(x, y, wi_ref[...]).astype(BF16)
-
-
-def value_grad_slots_kernel(piece, count, me_ref, *refs):
-    cot_ref, after_ref, mine_ref, other_ref, wx_ref, wf_ref, wi_ref = refs[:7]
-    out_hbm, out_ref, sem = refs[-3:]
-    depth = mine_ref.shape[1]
+
+
+def value_grad_kernel(pieces, me_ref, x_ref, *refs):
+    next_refs = refs[:pieces]
+    line_ref, line_y_ref, wf_ref, wi_ref, own_ref, other_ref = refs[pieces:]
+    depth = line_ref.shape[0]
     me = me_ref[0]
-    even, row, at = me // 2 % 2 == 0, me // 4 % 2, me // 8
-    filters = []
-    for z in range(piece * depth // count, (piece + 1) * depth // count):
-        for y in range(2):
-            mine, other = mine_ref[y ^ row, z ^ at], other_ref[y ^ row, z ^ at]
-            filters += [jnp.where(even, mine, other), jnp.where(even, other, mine)]
-    out_ref[...] = value_grad_tile(
-        cot_ref[...], after_ref[...], jnp.concatenate(filters, axis=0), wx_ref, wf_ref, wi_ref
-    )
-    width = cot_ref.shape[1]
-    copy = pltpu.make_async_copy(out_ref, out_hbm.at[:, pl.ds(piece * width, width)], sem)
-    copy.start()
-    copy.wait()
-
-
-def value_grad_slots(me, cotangent, after, mine, other, piece, count, so_far=()):
-    positions, width = cotangent.shape
-    taps = mine.shape[-1]
-    wx, _, wf, _, wi = transforms(positions, taps)
-    return pl.pallas_call(
-        functools.partial(value_grad_slots_kernel, piece, count),
-        in_specs=[SMEM_SPEC] + [VMEM_SPEC] * 7 + [HBM_SPEC] * len(so_far),
-        out_specs=HBM_SPEC,
-        out_shape=jax.ShapeDtypeStruct((positions, count * width), BF16),
-        input_output_aliases={8: 0} if so_far else {},
-        scratch_shapes=[pltpu.VMEM((positions, width), BF16), pltpu.SemaphoreType.DMA],
+    core0, row, at = me // 2 % 2 == 0, me // 4 % 2, me // 8
+    for piece, next_ref in enumerate(next_refs):
+        filters = []
+        for z in range(piece * depth // pieces, (piece + 1) * depth // pieces):
+            for y in range(2):
+                filters.append(jnp.where(row == y, line_ref[z ^ at], line_y_ref[z ^ at]))
+        spectrum = spectrum_of_filters(wf_ref[...], jnp.concatenate(filters, axis=0))
+        width = next_ref.shape[1]
+        cols = pl.ds(piece * width, width)
+        first = inverted(cross(x_ref[:, cols], spectrum), wi_ref[...]).astype(BF16)
+        second = inverted(cross(next_ref[...], spectrum), wi_ref[...]).astype(BF16)
+        own_ref[:, cols] = jnp.where(core0, first, second)
+        other_ref[:, cols] = jnp.where(core0, second, first)
+
+
+def value_grad_pair(me, near, far, line, line_y, positions):
+    _, _, wf, _, wi = transforms(positions, line.shape[-1])
+    half = jax.ShapeDtypeStruct((positions, near.shape[1]), BF16)
+    return pl.pallas_call(
+        functools.partial(value_grad_kernel, len(far)),
+        in_specs=[SMEM_SPEC] + [VMEM_SPEC] * (5 + len(far)),
+        out_specs=[VMEM_SPEC] * 2,
+        out_shape=[half] * 2,
         compiler_params=params(24),
-        cost_estimate=cost(2 * 9 * 128 * 256 * width, 8 * positions * width),
-        name="value_grad_slots",
-    )(me, cotangent, after, mine, other, wx, wf, wi, *so_far)
+        cost_estimate=cost(2 * 8 * 128 * 256 * near.shape[1], 24 * positions * near.shape[1]),
+        name="value_grad_pair",
+    )(me, near, *far, line, line_y, wf, wi)
 
 
 def value_grad_plain_kernel(cot_ref, after_ref, f_ref, wx_ref, wf_ref, wi_ref, o_ref):
-    o_ref[...] = value_grad_tile(
-        cot_ref[...], after_ref[...], f_ref[...], wx_ref, wf_ref, wi_ref
-    )
+    x = spectrum_of_window(wx_ref[...], cot_ref[...], after_ref[...])
+    product = cross(x, spectrum_of_filters(wf_ref[...], f_ref[...]))
+    o_ref[...] = inverted(product, wi_ref[...]).astype(BF16)
 
 
 def value_grad_plain(cotangent, after, filters, tile):
@@ -370,11 +489,16 @@
     seqs, parts = lax.axis_size("dp"), lax.axis_size("ctx")
     factor = float(seqs * parts * positions) ** -0.5
 
-    staged = seqs == 2 and parts >= 8 and parts & (parts - 1) == 0 and shard == 2 * LANES
-    back = [(i, i - 1) for i in range(1, parts)]
+    staged = (
+        seqs == 2
+        and parts >= 8
+        and parts & (parts - 1) == 0
+        and shard == 2 * LANES
+        and positions == taps == LANES
+    )
     if not staged:
         (cotangent,) = cotangent_of(token_ids, queries, out_grad, 1)
-        after = lax.ppermute(cotangent, "ctx", back)
+        after = lax.ppermute(cotangent, "ctx", [(i, i - 1) for i in range(1, parts)])
         all_filters = lax.all_gather(filters, "ctx", axis=0, tiled=True)
         value_grad = value_grad_plain(cotangent, after, all_filters, 512)
         share = tap_grad_plain(cotangent, after, gated_values, taps, 512)
@@ -383,44 +507,49 @@
 
     devices = seqs * parts
     depth = parts // 4
+    pieces = 2
     rank = lax.axis_index("dp")
-    place = lax.axis_index("ctx")
-    me = (place * 2 + rank).astype(jnp.int32).reshape(1)
+    part = lax.axis_index("ctx")
+    me = (part * 2 + rank).astype(jnp.int32).reshape(1)
 
     def swap(x, bits):
         return lax.ppermute(x, AXES, [(i, i ^ bits) for i in range(devices)])
 
+    def to_previous_chip(x, core):
+        pairs = [
+            (seq * parts + i, seq * parts + i - 2 + core)
+            for seq in range(seqs)
+            for i in range(2, parts, 2)
+        ]
+        return lax.ppermute(x, AXES, pairs)
+
     hops = (parts, 2, parts + 2)
     line = [filters] + [swap(filters, 4 * k) for k in range(1, depth)]
 
-    cots = cotangent_of(token_ids, queries, out_grad, 2)
-    afters = []
-    for cot in cots:
-        afters.append(lax.ppermute(cot, "ctx", back))
-
-    keep, send = tap_grad_slots(me, cots[0], afters[0], gated_values, 0, taps)
-    own, *sends = spread(keep, swap(send, 1))
-    sums = [[own] + [swap(x, bits) for x, bits in zip(sends, hops)]]
+    *halos, own, other = cotangent_pair(me, token_ids, queries, out_grad, pieces, shard)
+    afters = [
+        [to_previous_chip(halos[2 * i + core], core) for core in range(2)]
+        for i in range(pieces)
+    ]
+    got = swap(other, 1)
+    values, other = split(me, gated_values, shard)
+    values_got = swap(other, 1)
+    near, product, v = near_window(me, own, got, values, values_got, taps)
+
+    sums, far = [], []
+    for i in range(pieces):
+        mine, *sends, x = tap_grad(me, own, got, afters[i], product, v, i, taps)
+        sums.append([mine] + [swap(x, bits) for x, bits in zip(sends, hops)])
+        far.append(x)
 
     line = collect(line)
     line_y = swap(line, 2)
-    keep, send = tap_grad_slots(me, cots[1], afters[1], gated_values, 1, taps)
-    mine = collect([line, line_y])
-    own, *sends = spread(keep, swap(send, 1))
-    sums.append([own] + [swap(x, bits) for x, bits in zip(sends, hops)])
-    other = swap(mine, 1)
+    grad, other = value_grad_pair(me, near, far, line, line_y, positions)
+    grad_got = swap(other, 1)
 
     block, *sends = along_line(me, sums)
-    got = [swap(x, 4 * k) for k, x in enumerate(sends, 1)]
-    block = finish(block, got, factor)
-    filter_grad = join(me, block, swap(block, parts))
-
-    value_grad = ()
-    for piece in range(2):
-        value_grad = [
-            value_grad_slots(me, cots[piece], afters[piece], mine, other, piece, 2, value_grad)
-        ]
-    value_grad = value_grad[0]
+    block = finish(block, [swap(x, 4 * k) for k, x in enumerate(sends, 1)], factor)
+    value_grad, filter_grad = place(me, block, swap(block, parts), grad, grad_got, shard)
     return value_grad[None], filter_grad
 
 

time: 64.9 us -> 63.6 us (0.980)
  starting transfers between devices: 22.5 us -> 28.6 us
  waiting for transfers between devices: 28.1 us -> 23.3 us
  Pallas kernels: 13.1 us -> 10.6 us
    ppermute x17, waiting for transfers between devices: 28.1 us -> 19.7 us  [swap(): return lax.ppermute(x, AXES, [(i, i ^ bits) for i in range(devices)])]
    ppermute x17, starting transfers between devices: 19.7 us -> 24.7 us  [swap(): return lax.ppermute(x, AXES, [(i, i ^ bits) for i in range(devices)])]
    ppermute x2 -> x4, waiting for transfers between devices: 0.01 us -> 3.58 us  [to_previous_chip(): return lax.ppermute(x, AXES, pairs)]
    pallas_call x8 -> x7, Pallas kernels: 12.9 us -> 10.4 us  [the longest x1 2.3 us: value_grad_pair(): pl.pallas_call(functools.partial(value_grad_kernel, len(far)), in_specs=[...]
    ppermute x2 -> x4, starting transfers between devices: 2.72 us -> 3.91 us  [to_previous_chip(): return lax.ppermute(x, AXES, pairs)]
  transfers between devices with their start and end apart: 19 -> 21, of which waited for: 9 -> 9; matrix products, arithmetic and copies ran while one was open for 0% -> 0% of each run, Pallas kernels for 16% -> 8%
where the time goes in v5:
time: 63.6 us; the launch traced here: 63.3 us
  starting transfers between devices  28.6 us (45%)
  waiting for transfers between devices  23.3 us (37%)
  Pallas kernels  10.6 us (17%)
  between operations  0.83 us (1%)
    ppermute x17, starting transfers between devices, swap(): return lax.ppermute(x, AXES, [(i, i ^ bits) for i in range(devices)])  24.7 us
    ppermute x17, waiting for transfers between devices, swap(): return lax.ppermute(x, AXES, [(i, i ^ bits) for i in range(devices)])  19.7 us
    ppermute x4, starting transfers between devices, to_previous_chip(): return lax.ppermute(x, AXES, pairs)  3.91 us
    ppermute x4, waiting for transfers between devices, to_previous_chip(): return lax.ppermute(x, AXES, pairs)  3.58 us
    pallas_call x1, Pallas kernels, value_grad_pair(): pl.pallas_call(functools.partial(value_grad_kernel, len(far)), in_specs=[...  2.3 us
    pallas_call x2, Pallas kernels, tap_grad(): pl.pallas_call(functools.partial(tap_grad_kernel, piece), in_specs=[SMEM_...  2.05 us
    pallas_call x1, Pallas kernels, cotangent_pair(): pl.pallas_call(functools.partial(cotangent_pair_kernel, pieces, shard), i...  2.02 us
    pallas_call x1, Pallas kernels, near_window(): pl.pallas_call(near_window_kernel, in_specs=[SMEM_SPEC] + [VMEM_SPEC] * 6...  1.47 us
  transfers between devices with their start and end apart: 21, of which 9 were waited for; matrix products, arithmetic and copies ran while one was open for 0% of the time, Pallas kernels for 8%

profile of v5, /device:TPU:0, one launch (start us, length us, event | category | flops | bytes accessed | tf_op | source)
XLA Modules:
  0.0 63.3 jit_solution(7620154429662096300)
XLA Ops:
  0.6 0.0 copy-start.1
  0.6 0.0 copy-start.2
  0.7 2.0 %cotangent_pair.1 = (bf16[128,1024]{1,0:T(8,128)(2,1)S(1)}, bf16[128,1024]{1,0:T(8,128)(2,1)S(1)}, bf16[128,1024]{1,0:T(8,128)(2,1)S(1)}, bf16[128,1024]{1,0:T(8...) custom-call(s32[1]{0:T(128)} %bitcast.me_ref, s32[1,128]{1,0:T(1,128)} %ids_hbm.1, ...), custom_call_target="tpu_custom_call" | custom-call | flops 1048576 | bytes 4194304 | tf_op jit(solution)/shard_map/cotangent_pair/pallas_call | solution.py:173
  2.7 0.6 collective-permute-start
  3.3 1.4 %split.1 = (bf16[128,2048]{1,0:T(8,128)(2,1)S(1)}, bf16[128,2048]{1,0:T(8,128)(2,1)S(1)}) custom-call(s32[1]{0:T(128)} %bitcast.me_ref, bf16[128,4096]{1,0:T(8,128)(2,1)} %bitcast.5), custom_call_target="tpu_custom_call" | custom-call | flops 1 | bytes 2097152 | tf_op jit(solution)/shard_map/split/pallas_call | solution.py:205
  4.7 0.1 collective-permute-start.3
  4.8 3.0 %collective-permute-start.16 = (bf16[256,128]{1,0:T(8,128)(2,1)S(1)}, bf16[256,128]{1,0:T(8,128)(2,1)S(1)}, u32[]{:S(2)}, u32[]{:S(2)}) collective-permute-start(bf16[256,128]{1,0:T(8,128)(2,1)S(1)} %copy-done.3), channel_id=1, source_target_pairs={{0,4},{1,5},{2,6},{3,7},{4,0},{5,1},{6,2},{7,3},{8,12},{9,13},{10,... | collective-permute-start | bytes 196616 | tf_op jit(solution)/shard_map/ppermute | solution.py:516
  7.8 2.6 %collective-permute-start.17 = (bf16[256,128]{1,0:T(8,128)(2,1)S(1)}, bf16[256,128]{1,0:T(8,128)(2,1)S(1)}, u32[]{:S(2)}, u32[]{:S(2)}) collective-permute-start(bf16[256,128]{1,0:T(8,128)(2,1)S(1)} %copy-done.3), channel_id=1, source_target_pairs={{0,8},{1,9},{2,10},{3,11},{4,12},{5,13},{6,14},{7,15},{8,0},{9,1},... | collective-permute-start | bytes 196616 | tf_op jit(solution)/shard_map/ppermute | solution.py:516
  10.4 0.0 collective-permute-start.18
  10.4 0.0 collective-permute-done.16.refs_1_
  10.4 1.3 %collective-permute-start.7 = (bf16[128,1024]{1,0:T(8,128)(2,1)S(1)}, bf16[128,1024]{1,0:T(8,128)(2,1)S(1)}, u32[]{:S(2)}, u32[]{:S(2)}) collective-permute-start(bf16[128,1024]{1,0:T(8,128)(2,1)S(1)} %get-tuple-element.43), channel_id=1, source_target_pairs={{2,0},{4,2},{6,4},{8,6},{10,8},{12,10},{14,12},{18,16},{20,18},{22... | collective-permute-start | bytes 786440 | tf_op jit(solution)/shard_map/ppermute | solution.py:524
  11.7 3.6 %collective-permute-done.17.refs_2_ = bf16[256,128]{1,0:T(8,128)(2,1)S(1)} collective-permute-done((bf16[256,128]{1,0:T(8,128)(2,1)S(1)}, bf16[256,128]{1,0:T(8,128)(2,1)S(1)}, u32[]{:S(2)}, u32[]{:S(2)}) %collective-permute-start.17) | collective-permute-done | bytes 65568 | tf_op jit(solution)/shard_map/ppermute | solution.py:516
  15.3 0.7 %collective-permute-start.8 = (bf16[128,1024]{1,0:T(8,128)(2,1)S(1)}, bf16[128,1024]{1,0:T(8,128)(2,1)S(1)}, u32[]{:S(2)}, u32[]{:S(2)}) collective-permute-start(bf16[128,1024]{1,0:T(8,128)(2,1)S(1)} %get-tuple-element.44), channel_id=1, source_target_pairs={{2,1},{4,3},{6,5},{8,7},{10,9},{12,11},{14,13},{18,17},{20,19},{22... | collective-permute-start | bytes 786440 | tf_op jit(solution)/shard_map/ppermute | solution.py:524
  16.0 0.6 collective-permute-done.18.refs_3_
  16.5 1.3 %collective-permute-start.1 = (bf16[128,1024]{1,0:T(8,128)(2,1)S(1)}, bf16[128,1024]{1,0:T(8,128)(2,1)S(1)}, u32[]{:S(2)}, u32[]{:S(2)}) collective-permute-start(bf16[128,1024]{1,0:T(8,128)(2,1)S(1)} %get-tuple-element.33), channel_id=1, source_target_pairs={{2,0},{4,2},{6,4},{8,6},{10,8},{12,10},{14,12},{18,16},{20,18},{22... | collective-permute-start | bytes 786440 | tf_op jit(solution)/shard_map/ppermute | solution.py:524
  17.8 0.0 collective-permute-done.got_ref
  17.8 0.7 %collective-permute-start.2 = (bf16[128,1024]{1,0:T(8,128)(2,1)S(1)}, bf16[128,1024]{1,0:T(8,128)(2,1)S(1)}, u32[]{:S(2)}, u32[]{:S(2)}) collective-permute-start(bf16[128,1024]{1,0:T(8,128)(2,1)S(1)} %get-tuple-element.34), channel_id=1, source_target_pairs={{2,1},{4,3},{6,5},{8,7},{10,9},{12,11},{14,13},{18,17},{20,19},{22... | collective-permute-start | bytes 786440 | tf_op jit(solution)/shard_map/ppermute | solution.py:524
  18.6 0.0 copy-start
  18.6 3.3 %collective-permute-start.19 = (bf16[4,256,128]{2,1,0:T(8,128)(2,1)S(1)}, bf16[4,256,128]{2,1,0:T(8,128)(2,1)S(1)}, u32[]{:S(2)}, u32[]{:S(2)}) collective-permute-start(bf16[4,256,128]{2,1,0:T(8,128)(2,1)S(1)} %collect.1.refs_2_), channel_id=1, source_target_pairs={{0,2},{1,3},{2,0},{3,1},{4,6},{5,7},{6,4},{7,5},{8,10},{9,11},{10,... | collective-permute-start | bytes 786440 | tf_op jit(solution)/shard_map/ppermute | solution.py:516
  21.9 1.5 %near_window.1 = (f32[256,2048]{1,0:T(8,128)S(1)}, f32[256,2048]{1,0:T(8,128)S(1)}, f32[256,2048]{1,0:T(8,128)S(1)}) custom-call(s32[1]{0:T(128)} %bitcast.me_ref, bf16[128,2048]{1,0:T(8,128)(2,1)S(1)} %get-tuple-element.31.own_ref, bf16[128,2048]{1,0:T(8,128)(2,1)S(1)} %collective-permute-done.got_ref, bf16[128,2048]{1,0:T(8,128)(2,1)S(1)} %get-tuple-element.35.val_ref, ...), custom_call_target="tpu_custom_call" | custom-call | flops 1073741824 | bytes 8388608 | tf_op jit(solution)/shard_map/near_window/pallas_call | solution.py:233
  23.4 0.0 collective-permute-done.7.after0_ref
  23.4 1.0 %tap_grad.3 = (f32[2,128,128]{2,1,0:T(8,128)S(1)}, bf16[2,128,128]{2,1,0:T(8,128)(2,1)S(1)}, bf16[2,128,128]{2,1,0:T(8,128)(2,1)S(1)}, bf16[2,128,128]{2,1,0:T(8,128)(2,1)S(1)}, f32[256,1024]{1,0:T(8,128)S(1)}) custom-call(s32[1]{0:T(128)} %bitcast.me_ref, bf16[128,2048]{1,0:T(8,128)(2,1)S(1)} %get-tuple-element.31.own_ref, ...), custom_call_target="tpu_custom_call" | custom-call | flops 469762048 | bytes 3145728 | tf_op jit(solution)/shard_map/tap_grad/pallas_call | solution.py:270
  24.5 3.6 %collective-permute-done.1.after0_ref = bf16[128,1024]{1,0:T(8,128)(2,1)S(1)} collective-permute-done((bf16[128,1024]{1,0:T(8,128)(2,1)S(1)}, bf16[128,1024]{1,0:T(8,128)(2,1)S(1)}, u32[]{:S(2)}, u32[]{:S(2)}) %collective-permute-start.1) | collective-permute-done | bytes 262176 | tf_op jit(solution)/shard_map/ppermute | solution.py:524
  28.0 1.0 %tap_grad.2 = (f32[2,128,128]{2,1,0:T(8,128)S(1)}, bf16[2,128,128]{2,1,0:T(8,128)(2,1)S(1)}, bf16[2,128,128]{2,1,0:T(8,128)(2,1)S(1)}, bf16[2,128,128]{2,1,0:T(8,128)(2,1)S(1)}, f32[256,1024]{1,0:T(8,128)S(1)}) custom-call(s32[1]{0:T(128)} %bitcast.me_ref, bf16[128,2048]{1,0:T(8,128)(2,1)S(1)} %get-tuple-element.31.own_ref, ...), custom_call_target="tpu_custom_call" | custom-call | flops 469762048 | bytes 3145728 | tf_op jit(solution)/shard_map/tap_grad/pallas_call | solution.py:270
  29.1 4.6 %collective-permute-done.19.refs_3_ = bf16[4,256,128]{2,1,0:T(8,128)(2,1)S(1)} collective-permute-done((bf16[4,256,128]{2,1,0:T(8,128)(2,1)S(1)}, bf16[4,256,128]{2,1,0:T(8,128)(2,1)S(1)}, u32[]{:S(2)}, u32[]{:S(2)}) %collective-permute-start.19) | collective-permute-done | bytes 262176 | tf_op jit(solution)/shard_map/ppermute | solution.py:516
  33.7 2.3 %value_grad_pair.1 = (bf16[128,2048]{1,0:T(8,128)(2,1)S(1)}, bf16[128,2048]{1,0:T(8,128)(2,1)S(1)}) custom-call(s32[1]{0:T(128)} %bitcast.me_ref, f32[256,2048]{1,0:T(8,128)S(1)} %get-tuple-element.53.x_ref, f32[256,1024]{1,0:T(8,128)S(1)} %get-tuple-element.54.refs_0_, f32[256,1024]{1,0:T(8,128)S(1)} %get-tuple-element.55.refs_1_, ...), custom_call_target="tpu_custom_call" | custom-call | flops 1073741824 | bytes 6291456 | tf_op jit(solution)/shard_map/value_grad_pair/pallas_call | solution.py:452
  36.0 0.1 collective-permute-start.20
  36.0 1.7 %collective-permute-start.10 = (bf16[2,128,128]{2,1,0:T(8,128)(2,1)S(1)}, bf16[2,128,128]{2,1,0:T(8,128)(2,1)S(1)}, u32[]{:S(2)}, u32[]{:S(2)}) collective-permute-start(bf16[2,128,128]{2,1,0:T(8,128)(2,1)S(1)} %get-tuple-element.47), channel_id=1, source_target_pairs={{0,2},{1,3},{2,0},{3,1},{4,6},{5,7},{6,4},{7,5},{8,10},{9,11},{10,... | collective-permute-start | bytes 196616 | tf_op jit(solution)/shard_map/ppermute | solution.py:516
  37.8 1.3 %collective-permute-start.11 = (bf16[2,128,128]{2,1,0:T(8,128)(2,1)S(1)}, bf16[2,128,128]{2,1,0:T(8,128)(2,1)S(1)}, u32[]{:S(2)}, u32[]{:S(2)}) collective-permute-start(bf16[2,128,128]{2,1,0:T(8,128)(2,1)S(1)} %get-tuple-element.48), channel_id=1, source_target_pairs={{0,18},{1,19},{2,16},{3,17},{4,22},{5,23},{6,20},{7,21},{8,26},{9,... | collective-permute-start | bytes 196616 | tf_op jit(solution)/shard_map/ppermute | solution.py:516
  39.1 0.5 collective-permute-start.9
  39.6 1.5 %collective-permute-start.4 = (bf16[2,128,128]{2,1,0:T(8,128)(2,1)S(1)}, bf16[2,128,128]{2,1,0:T(8,128)(2,1)S(1)}, u32[]{:S(2)}, u32[]{:S(2)}) collective-permute-start(bf16[2,128,128]{2,1,0:T(8,128)(2,1)S(1)} %get-tuple-element.40), channel_id=1, source_target_pairs={{0,16},{1,17},{2,18},{3,19},{4,20},{5,21},{6,22},{7,23},{8,24},{9,... | collective-permute-start | bytes 196616 | tf_op jit(solution)/shard_map/ppermute | solution.py:516
  41.1 2.5 %collective-permute-start.5 = (bf16[2,128,128]{2,1,0:T(8,128)(2,1)S(1)}, bf16[2,128,128]{2,1,0:T(8,128)(2,1)S(1)}, u32[]{:S(2)}, u32[]{:S(2)}) collective-permute-start(bf16[2,128,128]{2,1,0:T(8,128)(2,1)S(1)} %get-tuple-element.41), channel_id=1, source_target_pairs={{0,2},{1,3},{2,0},{3,1},{4,6},{5,7},{6,4},{7,5},{8,10},{9,11},{10,... | collective-permute-start | bytes 196616 | tf_op jit(solution)/shard_map/ppermute | solution.py:516
  43.6 0.0 collective-permute-done.11.refs_7_
  43.6 1.3 %collective-permute-start.6 = (bf16[2,128,128]{2,1,0:T(8,128)(2,1)S(1)}, bf16[2,128,128]{2,1,0:T(8,128)(2,1)S(1)}, u32[]{:S(2)}, u32[]{:S(2)}) collective-permute-start(bf16[2,128,128]{2,1,0:T(8,128)(2,1)S(1)} %get-tuple-element.42), channel_id=1, source_target_pairs={{0,18},{1,19},{2,16},{3,17},{4,22},{5,23},{6,20},{7,21},{8,26},{9,... | collective-permute-start | bytes 196616 | tf_op jit(solution)/shard_map/ppermute | solution.py:516
  44.9 0.0 collective-permute-done.9.refs_5_
  44.9 0.0 collective-permute-done.4.refs_1_
  44.9 1.2 %collective-permute-done.5.refs_2_ = bf16[2,128,128]{2,1,0:T(8,128)(2,1)S(1)} collective-permute-done((bf16[2,128,128]{2,1,0:T(8,128)(2,1)S(1)}, bf16[2,128,128]{2,1,0:T(8,128)(2,1)S(1)}, u32[]{:S(2)}, u32[]{:S(2)}) %collective-permute-start.5) | collective-permute-done | bytes 65568 | tf_op jit(solution)/shard_map/ppermute | solution.py:516
  46.2 2.6 %collective-permute-done.6.refs_3_ = bf16[2,128,128]{2,1,0:T(8,128)(2,1)S(1)} collective-permute-done((bf16[2,128,128]{2,1,0:T(8,128)(2,1)S(1)}, bf16[2,128,128]{2,1,0:T(8,128)(2,1)S(1)}, u32[]{:S(2)}, u32[]{:S(2)}) %collective-permute-start.6) | collective-permute-done | bytes 65568 | tf_op jit(solution)/shard_map/ppermute | solution.py:516
  48.8 0.1 along_line.1
  48.9 1.5 %collective-permute-start.12 = (bf16[128,128]{1,0:T(8,128)(2,1)S(1)}, bf16[128,128]{1,0:T(8,128)(2,1)S(1)}, u32[]{:S(2)}, u32[]{:S(2)}) collective-permute-start(bf16[128,128]{1,0:T(8,128)(2,1)S(1)} %get-tuple-element.50), channel_id=1, source_target_pairs={{0,4},{1,5},{2,6},{3,7},{4,0},{5,1},{6,2},{7,3},{8,12},{9,13},{10,... | collective-permute-start | bytes 98312 | tf_op jit(solution)/shard_map/ppermute | solution.py:516
  50.4 1.6 %collective-permute-start.13 = (bf16[128,128]{1,0:T(8,128)(2,1)S(1)}, bf16[128,128]{1,0:T(8,128)(2,1)S(1)}, u32[]{:S(2)}, u32[]{:S(2)}) collective-permute-start(bf16[128,128]{1,0:T(8,128)(2,1)S(1)} %get-tuple-element.51), channel_id=1, source_target_pairs={{0,8},{1,9},{2,10},{3,11},{4,12},{5,13},{6,14},{7,15},{8,0},{9,1},... | collective-permute-start | bytes 98312 | tf_op jit(solution)/shard_map/ppermute | solution.py:516
  52.0 1.4 %collective-permute-start.14 = (bf16[128,128]{1,0:T(8,128)(2,1)S(1)}, bf16[128,128]{1,0:T(8,128)(2,1)S(1)}, u32[]{:S(2)}, u32[]{:S(2)}) collective-permute-start(bf16[128,128]{1,0:T(8,128)(2,1)S(1)} %get-tuple-element.52), channel_id=1, source_target_pairs={{0,12},{1,13},{2,14},{3,15},{4,8},{5,9},{6,10},{7,11},{8,4},{9,5},... | collective-permute-start | bytes 98312 | tf_op jit(solution)/shard_map/ppermute | solution.py:516
  53.4 1.8 %collective-permute-done.13.refs_1_ = bf16[128,128]{1,0:T(8,128)(2,1)S(1)} collective-permute-done((bf16[128,128]{1,0:T(8,128)(2,1)S(1)}, bf16[128,128]{1,0:T(8,128)(2,1)S(1)}, u32[]{:S(2)}, u32[]{:S(2)}) %collective-permute-start.13) | collective-permute-done | bytes 32800 | tf_op jit(solution)/shard_map/ppermute | solution.py:516
  55.2 2.5 %collective-permute-done.14.refs_2_ = bf16[128,128]{1,0:T(8,128)(2,1)S(1)} collective-permute-done((bf16[128,128]{1,0:T(8,128)(2,1)S(1)}, bf16[128,128]{1,0:T(8,128)(2,1)S(1)}, u32[]{:S(2)}, u32[]{:S(2)}) %collective-permute-start.14) | collective-permute-done | bytes 32800 | tf_op jit(solution)/shard_map/ppermute | solution.py:516
  57.7 0.1 finish.1.tap_ref
  57.8 1.6 %collective-permute-start.15 = (f32[128,128]{1,0:T(8,128)S(1)}, f32[128,128]{1,0:T(8,128)S(1)}, u32[]{:S(2)}, u32[]{:S(2)}) collective-permute-start(f32[128,128]{1,0:T(8,128)S(1)} %finish.1.tap_ref), channel_id=1, source_target_pairs={{0,16},{1,17},{2,18},{3,19},{4,20},{5,21},{6,22},{7,23},{8,24},{9,... | collective-permute-start | bytes 196616 | tf_op jit(solution)/shard_map/ppermute | solution.py:516
  59.4 2.7 %collective-permute-done.15.tap_got_ref = f32[128,128]{1,0:T(8,128)S(1)} collective-permute-done((f32[128,128]{1,0:T(8,128)S(1)}, f32[128,128]{1,0:T(8,128)S(1)}, u32[]{:S(2)}, u32[]{:S(2)}) %collective-permute-start.15) | collective-permute-done | bytes 65568 | tf_op jit(solution)/shard_map/ppermute | solution.py:516
  62.1 1.2 %place.1 = (bf16[128,4096]{1,0:T(8,128)(2,1)}, f32[256,128]{1,0:T(8,128)}) custom-call(s32[1]{0:T(128)} %bitcast.me_ref, f32[128,128]{1,0:T(8,128)S(1)} %finish.1.tap_ref, f32[128,128]{1,0:T(8,128)S(1)} %collective-permute-done.15.tap_got_ref, bf16[128,2048]{1,0:T(8,128)(2,1)S(1)} %get-tuple-element.56.val_ref, ...), custom_call_target="tpu_custom_call" | custom-call | flops 1 | bytes 1048576 | tf_op jit(solution)/shard_map/place/pallas_call | solution.py:382
  (12 shorter events, 0.0 us)
Async XLA Ops:
  0.6 21.3 %copy-start.1 = (bf16[512,256]{1,0:T(8,128)(2,1)S(1)}, bf16[512,256]{1,0:T(8,128)(2,1)}, u32[]{:S(2)}) copy-start(bf16[512,256]{1,0:T(8,128)(2,1)} %constant.17.clone.wx_ref) | copy-start | bytes 786436
  0.6 21.3 %copy-start.2 = (bf16[256,256]{1,0:T(8,128)(2,1)S(1)}, bf16[256,256]{1,0:T(8,128)(2,1)}, u32[]{:S(2)}) copy-start(bf16[256,256]{1,0:T(8,128)(2,1)} %constant.18.clone.wv_ref.refs_4_) | copy-start | bytes 393220
  0.7 4.1 %copy-start.3 = (bf16[256,128]{1,0:T(8,128)(2,1)S(1)}, bf16[256,128]{1,0:T(8,128)(2,1)}, u32[]{:S(2)}) copy-start(bf16[256,128]{1,0:T(8,128)(2,1)} %refs_0_.1) | copy-start | bytes 196612
  2.7 15.1 %collective-permute-start = (bf16[128,2048]{1,0:T(8,128)(2,1)S(1)}, bf16[128,2048]{1,0:T(8,128)(2,1)S(1)}, u32[]{:S(2)}, u32[]{:S(2)}) collective-permute-start(bf16[128,2048]{1,0:T(8,128)(2,1)S(1)} %get-tuple-element.32), channel_id=1, source_target_pairs={{0,1},{1,0},{2,3},{3,2},{4,5},{5,4},{6,7},{7,6},{8,9},{9,8},{10,11... | collective-permute-start | bytes 1572872 | tf_op jit(solution)/shard_map/ppermute | solution.py:516
  4.7 13.9 %collective-permute-start.3 = (bf16[128,2048]{1,0:T(8,128)(2,1)S(1)}, bf16[128,2048]{1,0:T(8,128)(2,1)S(1)}, u32[]{:S(2)}, u32[]{:S(2)}) collective-permute-start(bf16[128,2048]{1,0:T(8,128)(2,1)S(1)} %get-tuple-element.36), channel_id=1, source_target_pairs={{0,1},{1,0},{2,3},{3,2},{4,5},{5,4},{6,7},{7,6},{8,9},{9,8},{10,11... | collective-permute-start | bytes 1572872 | tf_op jit(solution)/shard_map/ppermute | solution.py:516
  4.8 5.6 %collective-permute-start.16 = (bf16[256,128]{1,0:T(8,128)(2,1)S(1)}, bf16[256,128]{1,0:T(8,128)(2,1)S(1)}, u32[]{:S(2)}, u32[]{:S(2)}) collective-permute-start(bf16[256,128]{1,0:T(8,128)(2,1)S(1)} %copy-done.3), channel_id=1, source_target_pairs={{0,4},{1,5},{2,6},{3,7},{4,0},{5,1},{6,2},{7,3},{8,12},{9,13},{10,... | collective-permute-start | bytes 196616 | tf_op jit(solution)/shard_map/ppermute | solution.py:516
  7.8 7.5 %collective-permute-start.17 = (bf16[256,128]{1,0:T(8,128)(2,1)S(1)}, bf16[256,128]{1,0:T(8,128)(2,1)S(1)}, u32[]{:S(2)}, u32[]{:S(2)}) collective-permute-start(bf16[256,128]{1,0:T(8,128)(2,1)S(1)} %copy-done.3), channel_id=1, source_target_pairs={{0,8},{1,9},{2,10},{3,11},{4,12},{5,13},{6,14},{7,15},{8,0},{9,1},... | collective-permute-start | bytes 196616 | tf_op jit(solution)/shard_map/ppermute | solution.py:516
  10.4 6.2 %collective-permute-start.18 = (bf16[256,128]{1,0:T(8,128)(2,1)S(1)}, bf16[256,128]{1,0:T(8,128)(2,1)S(1)}, u32[]{:S(2)}, u32[]{:S(2)}) collective-permute-start(bf16[256,128]{1,0:T(8,128)(2,1)S(1)} %copy-done.3), channel_id=1, source_target_pairs={{0,12},{1,13},{2,14},{3,15},{4,8},{5,9},{6,10},{7,11},{8,4},{9,5},... | collective-permute-start | bytes 196616 | tf_op jit(solution)/shard_map/ppermute | solution.py:516
  10.4 13.0 %collective-permute-start.7 = (bf16[128,1024]{1,0:T(8,128)(2,1)S(1)}, bf16[128,1024]{1,0:T(8,128)(2,1)S(1)}, u32[]{:S(2)}, u32[]{:S(2)}) collective-permute-start(bf16[128,1024]{1,0:T(8,128)(2,1)S(1)} %get-tuple-element.43), channel_id=1, source_target_pairs={{2,0},{4,2},{6,4},{8,6},{10,8},{12,10},{14,12},{18,16},{20,18},{22... | collective-permute-start | bytes 786440 | tf_op jit(solution)/shard_map/ppermute | solution.py:524
  15.3 8.1 %collective-permute-start.8 = (bf16[128,1024]{1,0:T(8,128)(2,1)S(1)}, bf16[128,1024]{1,0:T(8,128)(2,1)S(1)}, u32[]{:S(2)}, u32[]{:S(2)}) collective-permute-start(bf16[128,1024]{1,0:T(8,128)(2,1)S(1)} %get-tuple-element.44), channel_id=1, source_target_pairs={{2,1},{4,3},{6,5},{8,7},{10,9},{12,11},{14,13},{18,17},{20,19},{22... | collective-permute-start | bytes 786440 | tf_op jit(solution)/shard_map/ppermute | solution.py:524
  16.5 11.5 %collective-permute-start.1 = (bf16[128,1024]{1,0:T(8,128)(2,1)S(1)}, bf16[128,1024]{1,0:T(8,128)(2,1)S(1)}, u32[]{:S(2)}, u32[]{:S(2)}) collective-permute-start(bf16[128,1024]{1,0:T(8,128)(2,1)S(1)} %get-tuple-element.33), channel_id=1, source_target_pairs={{2,0},{4,2},{6,4},{8,6},{10,8},{12,10},{14,12},{18,16},{20,18},{22... | collective-permute-start | bytes 786440 | tf_op jit(solution)/shard_map/ppermute | solution.py:524
  17.8 10.2 %collective-permute-start.2 = (bf16[128,1024]{1,0:T(8,128)(2,1)S(1)}, bf16[128,1024]{1,0:T(8,128)(2,1)S(1)}, u32[]{:S(2)}, u32[]{:S(2)}) collective-permute-start(bf16[128,1024]{1,0:T(8,128)(2,1)S(1)} %get-tuple-element.34), channel_id=1, source_target_pairs={{2,1},{4,3},{6,5},{8,7},{10,9},{12,11},{14,13},{18,17},{20,19},{22... | collective-permute-start | bytes 786440 | tf_op jit(solution)/shard_map/ppermute | solution.py:524
  18.6 4.9 %copy-start = (bf16[256,256]{1,0:T(8,128)(2,1)S(1)}, bf16[256,256]{1,0:T(8,128)(2,1)}, u32[]{:S(2)}) copy-start(bf16[256,256]{1,0:T(8,128)(2,1)} %constant.19.clone.wi_ref.refs_5_) | copy-start | bytes 393220
  18.6 15.1 %collective-permute-start.19 = (bf16[4,256,128]{2,1,0:T(8,128)(2,1)S(1)}, bf16[4,256,128]{2,1,0:T(8,128)(2,1)S(1)}, u32[]{:S(2)}, u32[]{:S(2)}) collective-permute-start(bf16[4,256,128]{2,1,0:T(8,128)(2,1)S(1)} %collect.1.refs_2_), channel_id=1, source_target_pairs={{0,2},{1,3},{2,0},{3,1},{4,6},{5,7},{6,4},{7,5},{8,10},{9,11},{10,... | collective-permute-start | bytes 786440 | tf_op jit(solution)/shard_map/ppermute | solution.py:516
  36.0 26.2 %collective-permute-start.20 = (bf16[128,2048]{1,0:T(8,128)(2,1)S(1)}, bf16[128,2048]{1,0:T(8,128)(2,1)S(1)}, u32[]{:S(2)}, u32[]{:S(2)}) collective-permute-start(bf16[128,2048]{1,0:T(8,128)(2,1)S(1)} %get-tuple-element.57), channel_id=1, source_target_pairs={{0,1},{1,0},{2,3},{3,2},{4,5},{5,4},{6,7},{7,6},{8,9},{9,8},{10,11... | collective-permute-start | bytes 1572872 | tf_op jit(solution)/shard_map/ppermute | solution.py:516
  36.0 5.0 %collective-permute-start.10 = (bf16[2,128,128]{2,1,0:T(8,128)(2,1)S(1)}, bf16[2,128,128]{2,1,0:T(8,128)(2,1)S(1)}, u32[]{:S(2)}, u32[]{:S(2)}) collective-permute-start(bf16[2,128,128]{2,1,0:T(8,128)(2,1)S(1)} %get-tuple-element.47), channel_id=1, source_target_pairs={{0,2},{1,3},{2,0},{3,1},{4,6},{5,7},{6,4},{7,5},{8,10},{9,11},{10,... | collective-permute-start | bytes 196616 | tf_op jit(solution)/shard_map/ppermute | solution.py:516
  37.8 5.8 %collective-permute-start.11 = (bf16[2,128,128]{2,1,0:T(8,128)(2,1)S(1)}, bf16[2,128,128]{2,1,0:T(8,128)(2,1)S(1)}, u32[]{:S(2)}, u32[]{:S(2)}) collective-permute-start(bf16[2,128,128]{2,1,0:T(8,128)(2,1)S(1)} %get-tuple-element.48), channel_id=1, source_target_pairs={{0,18},{1,19},{2,16},{3,17},{4,22},{5,23},{6,20},{7,21},{8,26},{9,... | collective-permute-start | bytes 196616 | tf_op jit(solution)/shard_map/ppermute | solution.py:516
  39.1 5.9 %collective-permute-start.9 = (bf16[2,128,128]{2,1,0:T(8,128)(2,1)S(1)}, bf16[2,128,128]{2,1,0:T(8,128)(2,1)S(1)}, u32[]{:S(2)}, u32[]{:S(2)}) collective-permute-start(bf16[2,128,128]{2,1,0:T(8,128)(2,1)S(1)} %get-tuple-element.46), channel_id=1, source_target_pairs={{0,16},{1,17},{2,18},{3,19},{4,20},{5,21},{6,22},{7,23},{8,24},{9,... | collective-permute-start | bytes 196616 | tf_op jit(solution)/shard_map/ppermute | solution.py:516
  39.6 5.3 %collective-permute-start.4 = (bf16[2,128,128]{2,1,0:T(8,128)(2,1)S(1)}, bf16[2,128,128]{2,1,0:T(8,128)(2,1)S(1)}, u32[]{:S(2)}, u32[]{:S(2)}) collective-permute-start(bf16[2,128,128]{2,1,0:T(8,128)(2,1)S(1)} %get-tuple-element.40), channel_id=1, source_target_pairs={{0,16},{1,17},{2,18},{3,19},{4,20},{5,21},{6,22},{7,23},{8,24},{9,... | collective-permute-start | bytes 196616 | tf_op jit(solution)/shard_map/ppermute | solution.py:516
  41.1 5.1 %collective-permute-start.5 = (bf16[2,128,128]{2,1,0:T(8,128)(2,1)S(1)}, bf16[2,128,128]{2,1,0:T(8,128)(2,1)S(1)}, u32[]{:S(2)}, u32[]{:S(2)}) collective-permute-start(bf16[2,128,128]{2,1,0:T(8,128)(2,1)S(1)} %get-tuple-element.41), channel_id=1, source_target_pairs={{0,2},{1,3},{2,0},{3,1},{4,6},{5,7},{6,4},{7,5},{8,10},{9,11},{10,... | collective-permute-start | bytes 196616 | tf_op jit(solution)/shard_map/ppermute | solution.py:516
  43.6 5.2 %collective-permute-start.6 = (bf16[2,128,128]{2,1,0:T(8,128)(2,1)S(1)}, bf16[2,128,128]{2,1,0:T(8,128)(2,1)S(1)}, u32[]{:S(2)}, u32[]{:S(2)}) collective-permute-start(bf16[2,128,128]{2,1,0:T(8,128)(2,1)S(1)} %get-tuple-element.42), channel_id=1, source_target_pairs={{0,18},{1,19},{2,16},{3,17},{4,22},{5,23},{6,20},{7,21},{8,26},{9,... | collective-permute-start | bytes 196616 | tf_op jit(solution)/shard_map/ppermute | solution.py:516
  48.9 4.5 %collective-permute-start.12 = (bf16[128,128]{1,0:T(8,128)(2,1)S(1)}, bf16[128,128]{1,0:T(8,128)(2,1)S(1)}, u32[]{:S(2)}, u32[]{:S(2)}) collective-permute-start(bf16[128,128]{1,0:T(8,128)(2,1)S(1)} %get-tuple-element.50), channel_id=1, source_target_pairs={{0,4},{1,5},{2,6},{3,7},{4,0},{5,1},{6,2},{7,3},{8,12},{9,13},{10,... | collective-permute-start | bytes 98312 | tf_op jit(solution)/shard_map/ppermute | solution.py:516
  50.4 4.8 %collective-permute-start.13 = (bf16[128,128]{1,0:T(8,128)(2,1)S(1)}, bf16[128,128]{1,0:T(8,128)(2,1)S(1)}, u32[]{:S(2)}, u32[]{:S(2)}) collective-permute-start(bf16[128,128]{1,0:T(8,128)(2,1)S(1)} %get-tuple-element.51), channel_id=1, source_target_pairs={{0,8},{1,9},{2,10},{3,11},{4,12},{5,13},{6,14},{7,15},{8,0},{9,1},... | collective-permute-start | bytes 98312 | tf_op jit(solution)/shard_map/ppermute | solution.py:516
  52.0 5.7 %collective-permute-start.14 = (bf16[128,128]{1,0:T(8,128)(2,1)S(1)}, bf16[128,128]{1,0:T(8,128)(2,1)S(1)}, u32[]{:S(2)}, u32[]{:S(2)}) collective-permute-start(bf16[128,128]{1,0:T(8,128)(2,1)S(1)} %get-tuple-element.52), channel_id=1, source_target_pairs={{0,12},{1,13},{2,14},{3,15},{4,8},{5,9},{6,10},{7,11},{8,4},{9,5},... | collective-permute-start | bytes 98312 | tf_op jit(solution)/shard_map/ppermute | solution.py:516
  57.8 4.3 %collective-permute-start.15 = (f32[128,128]{1,0:T(8,128)S(1)}, f32[128,128]{1,0:T(8,128)S(1)}, u32[]{:S(2)}, u32[]{:S(2)}) collective-permute-start(f32[128,128]{1,0:T(8,128)S(1)} %finish.1.tap_ref), channel_id=1, source_target_pairs={{0,16},{1,17},{2,18},{3,19},{4,20},{5,21},{6,22},{7,23},{8,24},{9,... | collective-permute-start | bytes 196616 | tf_op jit(solution)/shard_map/ppermute | solution.py:516

commit v6 on v5

--- a/solution.py
+++ b/solution.py
@@ -126,9 +126,9 @@
     )(*(pltpu.with_memory_space_constraint(x, pltpu.HBM) for x in (token_ids, queries, out_grad)))
 
 
-def cotangent_pair_kernel(pieces, shard, me_ref, ids_hbm, q_hbm, g_hbm, *refs):
-    halos, (own_ref, other_ref) = refs[: 2 * pieces], refs[2 * pieces : 2 * pieces + 2]
-    ids_ref, q_ref, g_ref, sems, ids_sem = refs[2 * pieces + 2 :]
+def cotangent_pair_kernel(
+    pieces, shard, me_ref, ids_hbm, q_hbm, g_hbm, own_ref, other_ref, ids_ref, q_ref, g_ref, sems, ids_sem
+):
     core0 = me_ref[0] // 2 % 2 == 0
     width = q_ref.shape[1] // pieces
     copies = []
@@ -159,8 +159,6 @@
         for at in range(0, width // 2, LANES):
             source = i * width + at // shard * 2 * shard + at % shard
             even, odd = cotangent(source), cotangent(source + shard)
-            halos[2 * i][:, at : at + LANES] = even
-            halos[2 * i + 1][:, at : at + LANES] = odd
             cols = pl.ds(i * width // 2 + at, LANES)
             own_ref[:, cols] = jnp.where(core0, even, odd)
             other_ref[:, cols] = jnp.where(core0, odd, even)
@@ -168,13 +166,12 @@
 
 def cotangent_pair(me, token_ids, queries, out_grad, pieces, shard):
     positions, channels = queries.shape
-    piece = jax.ShapeDtypeStruct((positions, channels // 2 // pieces), BF16)
     half = jax.ShapeDtypeStruct((positions, channels // 2), BF16)
     return pl.pallas_call(
         functools.partial(cotangent_pair_kernel, pieces, shard),
         in_specs=[SMEM_SPEC] + [HBM_SPEC] * 3,
-        out_specs=[VMEM_SPEC] * (2 * pieces + 2),
-        out_shape=[piece] * (2 * pieces) + [half] * 2,
+        out_specs=[VMEM_SPEC] * 2,
+        out_shape=[half] * 2,
         scratch_shapes=[pltpu.VMEM(token_ids.shape, token_ids.dtype)]
         + [pltpu.VMEM((positions, channels), BF16)] * 2
         + [pltpu.SemaphoreType.DMA((2, pieces)), pltpu.SemaphoreType.DMA],
@@ -182,6 +179,27 @@
         cost_estimate=cost(2 * positions * channels, 8 * positions * channels),
         name="cotangent_pair",
     )(me, *(pltpu.with_memory_space_constraint(x, pltpu.HBM) for x in (token_ids, queries, out_grad)))
+
+
+def heads_kernel(me_ref, own_ref, got_ref, *head_refs):
+    core0 = me_ref[0] // 2 % 2 == 0
+    for i, ref in enumerate(head_refs):
+        cols = pl.ds(i * ref.shape[1], ref.shape[1])
+        ref[...] = jnp.where(core0, own_ref[:, cols], got_ref[:, cols])
+
+
+def heads(me, own, got, pieces):
+    positions, width = own.shape
+    piece = jax.ShapeDtypeStruct((positions, width // pieces), own.dtype)
+    return pl.pallas_call(
+        heads_kernel,
+        in_specs=[SMEM_SPEC] + [VMEM_SPEC] * 2,
+        out_specs=[VMEM_SPEC] * pieces,
+        out_shape=[piece] * pieces,
+        compiler_params=params(8),
+        cost_estimate=cost(1, 6 * positions * width),
+        name="heads",
+    )(me, own, got)
 
 
 def split_kernel(shard, me_ref, src_hbm, own_ref, other_ref, sems):
@@ -242,43 +260,52 @@
 
 
 def tap_grad_kernel(
-    piece, me_ref, own_ref, got_ref, after0_ref, after1_ref, product_ref, v_ref, wx_ref, wi_ref, *refs
+    piece, me_ref, own_ref, got_ref, after_ref, product_ref, v_ref, wx_ref, wi_ref, *refs
 ):
-    mine_ref, *send_refs, x_ref, tmp_ref = refs
-    width = after0_ref.shape[1]
+    width = after_ref.shape[1]
     cols = pl.ds(piece * width, width)
     me = me_ref[0]
     core0, row, rank = me // 2 % 2 == 0, me // 4 % 2, me % 2
     own = jnp.where(core0, got_ref[:, cols], own_ref[:, cols])
-    after = jnp.where(core0, after0_ref[...], after1_ref[...])
-    x = spectrum_of_window(wx_ref[...], own, after)
+    x = spectrum_of_window(wx_ref[...], own, after_ref[...])
+    out = inverted(product_ref[:, cols] + cross(x, v_ref[:, cols]), wi_ref[...])
+    if len(refs) == 2:
+        out_ref, x_ref = refs
+        out_ref[...], x_ref[...] = out, x
+        return
+    before_refs, (mine_ref, *send_refs, x_ref, tmp_ref) = refs[:piece], refs[piece:]
     x_ref[...] = x
-    out = inverted(product_ref[:, cols] + cross(x, v_ref[:, cols]), wi_ref[...])
-    for block in range(width // LANES):
+    per_piece = width // LANES
+    for block in range((piece + 1) * per_piece):
         half, y, z = block % 2, block // 2 % 2, block // 4
-        tmp_ref[(half ^ rank) + 2 * (y ^ row), z] = out[:, block * LANES : (block + 1) * LANES]
+        at = block % per_piece * LANES
+        source = before_refs[block // per_piece] if block < piece * per_piece else out
+        tmp_ref[(half ^ rank) + 2 * (y ^ row), z] = source[:, at : at + LANES]
     mine_ref[...] = tmp_ref[0]
     for k, ref in enumerate(send_refs, 1):
         ref[...] = tmp_ref[k].astype(BF16)
 
 
-def tap_grad(me, own, got, afters, product, v, piece, taps):
-    positions, width = afters[0].shape
+def tap_grad(me, own, got, after, product, v, taps, piece, pieces, before):
+    positions, width = after.shape
     wx, _, _, wi, _ = transforms(positions, taps)
-    depth = width // (4 * LANES)
-    block = (depth, taps, LANES)
+    block = (pieces * width // (4 * LANES), taps, LANES)
+    last = piece == pieces - 1
+    out_shape = [jax.ShapeDtypeStruct((taps, width), F32)]
+    if last:
+        out_shape = [jax.ShapeDtypeStruct(block, F32)] + [jax.ShapeDtypeStruct(block, BF16)] * 3
+    out_shape.append(jax.ShapeDtypeStruct((wx.shape[1], width), F32))
+    before = list(before) if last else []
     return pl.pallas_call(
         functools.partial(tap_grad_kernel, piece),
-        in_specs=[SMEM_SPEC] + [VMEM_SPEC] * 8,
-        out_specs=[VMEM_SPEC] * 5,
-        out_shape=[jax.ShapeDtypeStruct(block, F32)]
-        + [jax.ShapeDtypeStruct(block, BF16)] * 3
-        + [jax.ShapeDtypeStruct((wx.shape[1], width), F32)],
-        scratch_shapes=[pltpu.VMEM((4, *block), F32)],
+        in_specs=[SMEM_SPEC] + [VMEM_SPEC] * (7 + len(before)),
+        out_specs=[VMEM_SPEC] * len(out_shape),
+        out_shape=out_shape,
+        scratch_shapes=[pltpu.VMEM((4, *block), F32)] if last else [],
         compiler_params=params(24),
         cost_estimate=cost(2 * 7 * 128 * 256 * width, 24 * positions * width),
         name="tap_grad",
-    )(me, own, got, *afters, product, v, wx, wi)
+    )(me, own, got, after, product, v, wx, wi, *before)
 
 
 def collect_kernel(*refs):
@@ -355,46 +382,59 @@
     )(mine, *got)
 
 
-def place_kernel(shard, me_ref, tap_ref, tap_got_ref, val_ref, val_got_ref, val_hbm, tap_hbm, sems, tap_sems):
-    core, rank = me_ref[0] // 2 % 2, me_ref[0] % 2
-    rows = tap_ref.shape[0]
+def place_kernel(shard, me_ref, own_ref, got_ref, out_hbm, sems):
+    core = me_ref[0] // 2 % 2
     copies = []
-    for n, (half, ref) in enumerate(((rank, tap_ref), (1 - rank, tap_got_ref))):
-        at = pl.ds(pl.multiple_of(half * rows, rows), rows)
-        copies.append(pltpu.make_async_copy(ref, tap_hbm.at[at, :], tap_sems.at[n]))
-    for n, (parity, ref) in enumerate(((core, val_ref), (1 - core, val_got_ref))):
+    for n, (parity, ref) in enumerate(((core, own_ref), (1 - core, got_ref))):
         for at in range(0, ref.shape[1], shard):
             cols = pl.ds(pl.multiple_of(2 * at + parity * shard, shard), shard)
-            copies.append(
-                pltpu.make_async_copy(
-                    ref.at[:, pl.ds(at, shard)], val_hbm.at[:, cols], sems.at[n, at // shard]
-                )
+            copy = pltpu.make_async_copy(
+                ref.at[:, pl.ds(at, shard)], out_hbm.at[:, cols], sems.at[n, at // shard]
             )
-    for copy in copies:
-        copy.start()
+            copy.start()
+            copies.append(copy)
     for copy in copies:
         copy.wait()
 
 
-def place(me, taps_mine, taps_got, values, values_got, shard):
-    rows, taps = taps_mine.shape
-    positions, width = values.shape
+def place(me, own, got, shard):
+    positions, width = own.shape
     return pl.pallas_call(
         functools.partial(place_kernel, shard),
-        in_specs=[SMEM_SPEC] + [VMEM_SPEC] * 4,
-        out_specs=[HBM_SPEC] * 2,
-        out_shape=[
-            jax.ShapeDtypeStruct((positions, 2 * width), values.dtype),
-            jax.ShapeDtypeStruct((2 * rows, taps), F32),
-        ],
-        scratch_shapes=[
-            pltpu.SemaphoreType.DMA((2, width // shard)),
-            pltpu.SemaphoreType.DMA((2,)),
-        ],
-        compiler_params=params(8),
-        cost_estimate=cost(1, 4 * positions * width),
+        in_specs=[SMEM_SPEC] + [VMEM_SPEC] * 2,
+        out_specs=HBM_SPEC,
+        out_shape=jax.ShapeDtypeStruct((positions, 2 * width), own.dtype),
+        scratch_shapes=[pltpu.SemaphoreType.DMA((2, width // shard))],
+        compiler_params=params(8),
+        cost_estimate=cost(1, 8 * positions * width),
         name="place",
-    )(me, taps_mine, taps_got, values, values_got)
+    )(me, own, got)
+
+
+def join_kernel(me_ref, mine_ref, other_ref, out_hbm, sems):
+    rank = me_ref[0] % 2
+    rows = mine_ref.shape[0]
+    copies = []
+    for n, (half, ref) in enumerate(((rank, mine_ref), (1 - rank, other_ref))):
+        at = pl.ds(pl.multiple_of(half * rows, rows), rows)
+        copies.append(pltpu.make_async_copy(ref, out_hbm.at[at, :], sems.at[n]))
+        copies[-1].start()
+    for copy in copies:
+        copy.wait()
+
+
+def join(me, mine, other):
+    rows, taps = mine.shape
+    return pl.pallas_call(
+        join_kernel,
+        in_specs=[SMEM_SPEC] + [VMEM_SPEC] * 2,
+        out_specs=HBM_SPEC,
+        out_shape=jax.ShapeDtypeStruct((2 * rows, taps), F32),
+        scratch_shapes=[pltpu.SemaphoreType.DMA((2,))],
+        compiler_params=params(8),
+        cost_estimate=cost(1, 16 * rows * taps),
+        name="join",
+    )(me, mine, other)
 
 
 def tap_grad_plain_kernel(cot_ref, after_ref, val_ref, wx_ref, wv_ref, wi_ref, o_ref):
@@ -428,15 +468,15 @@
 
 def value_grad_kernel(pieces, me_ref, x_ref, *refs):
     next_refs = refs[:pieces]
-    line_ref, line_y_ref, wf_ref, wi_ref, own_ref, other_ref = refs[pieces:]
-    depth = line_ref.shape[0]
+    filters_ref, wf_ref, wi_ref, own_ref, other_ref = refs[pieces:]
+    depth = filters_ref.shape[0]
     me = me_ref[0]
     core0, row, at = me // 2 % 2 == 0, me // 4 % 2, me // 8
     for piece, next_ref in enumerate(next_refs):
         filters = []
         for z in range(piece * depth // pieces, (piece + 1) * depth // pieces):
             for y in range(2):
-                filters.append(jnp.where(row == y, line_ref[z ^ at], line_y_ref[z ^ at]))
+                filters.append(filters_ref[z ^ at, y ^ row])
         spectrum = spectrum_of_filters(wf_ref[...], jnp.concatenate(filters, axis=0))
         width = next_ref.shape[1]
         cols = pl.ds(piece * width, width)
@@ -446,18 +486,18 @@
         other_ref[:, cols] = jnp.where(core0, second, first)
 
 
-def value_grad_pair(me, near, far, line, line_y, positions):
-    _, _, wf, _, wi = transforms(positions, line.shape[-1])
+def value_grad_pair(me, near, far, filters, positions):
+    _, _, wf, _, wi = transforms(positions, filters.shape[-1])
     half = jax.ShapeDtypeStruct((positions, near.shape[1]), BF16)
     return pl.pallas_call(
         functools.partial(value_grad_kernel, len(far)),
-        in_specs=[SMEM_SPEC] + [VMEM_SPEC] * (5 + len(far)),
+        in_specs=[SMEM_SPEC] + [VMEM_SPEC] * (4 + len(far)),
         out_specs=[VMEM_SPEC] * 2,
         out_shape=[half] * 2,
         compiler_params=params(24),
         cost_estimate=cost(2 * 8 * 128 * 256 * near.shape[1], 24 * positions * near.shape[1]),
         name="value_grad_pair",
-    )(me, near, *far, line, line_y, wf, wi)
+    )(me, near, *far, filters, wf, wi)
 
 
 def value_grad_plain_kernel(cot_ref, after_ref, f_ref, wx_ref, wf_ref, wi_ref, o_ref):
@@ -515,41 +555,38 @@
     def swap(x, bits):
         return lax.ppermute(x, AXES, [(i, i ^ bits) for i in range(devices)])
 
-    def to_previous_chip(x, core):
-        pairs = [
-            (seq * parts + i, seq * parts + i - 2 + core)
-            for seq in range(seqs)
-            for i in range(2, parts, 2)
-        ]
-        return lax.ppermute(x, AXES, pairs)
-
+    back = [(seq * parts + i, seq * parts + i - 2) for seq in range(seqs) for i in range(2, parts)]
     hops = (parts, 2, parts + 2)
-    line = [filters] + [swap(filters, 4 * k) for k in range(1, depth)]
-
-    *halos, own, other = cotangent_pair(me, token_ids, queries, out_grad, pieces, shard)
-    afters = [
-        [to_previous_chip(halos[2 * i + core], core) for core in range(2)]
-        for i in range(pieces)
-    ]
+    filters_y = swap(filters, 2)
+
+    own, other = cotangent_pair(me, token_ids, queries, out_grad, 2 * pieces, shard)
     got = swap(other, 1)
+    afters = []
+    for head in heads(me, own, got, pieces):
+        afters.append(lax.ppermute(head, AXES, back))
     values, other = split(me, gated_values, shard)
     values_got = swap(other, 1)
     near, product, v = near_window(me, own, got, values, values_got, taps)
 
-    sums, far = [], []
+    shares, far = [], []
     for i in range(pieces):
-        mine, *sends, x = tap_grad(me, own, got, afters[i], product, v, i, taps)
-        sums.append([mine] + [swap(x, bits) for x, bits in zip(sends, hops)])
+        *shares, x = tap_grad(
+            me, own, got, afters[i], product, v, taps, i, pieces, shares
+        )
         far.append(x)
-
-    line = collect(line)
-    line_y = swap(line, 2)
-    grad, other = value_grad_pair(me, near, far, line, line_y, positions)
+    mine, *sends = shares
+    sums = [[mine] + [swap(x, bits) for x, bits in zip(sends, hops)]]
+
+    filters = collect([filters, filters_y])
+    filters = [filters] + [swap(filters, 4 * k) for k in range(1, depth)]
+    filters = collect(filters)
+    grad, other = value_grad_pair(me, near, far, filters, positions)
     grad_got = swap(other, 1)
 
     block, *sends = along_line(me, sums)
     block = finish(block, [swap(x, 4 * k) for k, x in enumerate(sends, 1)], factor)
-    value_grad, filter_grad = place(me, block, swap(block, parts), grad, grad_got, shard)
+    value_grad = place(me, grad, grad_got, shard)
+    filter_grad = join(me, block, swap(block, parts))
     return value_grad[None], filter_grad
 
 

time: 63.6 us -> 64.6 us (1.016)
  waiting for transfers between devices: 23.3 us -> 26.5 us
  starting transfers between devices: 28.6 us -> 25.7 us
    ppermute x17 -> x14, waiting for transfers between devices: 19.7 us -> 26.5 us  [swap(): return lax.ppermute(x, AXES, [(i, i ^ bits) for i in range(devices)])]
    ppermute x4 -> x2, waiting for transfers between devices: 3.58 us -> 0.01 us  [body(): afters.append(lax.ppermute(head, AXES, back))]
    ppermute x17 -> x14, starting transfers between devices: 24.7 us -> 23.2 us  [swap(): return lax.ppermute(x, AXES, [(i, i ^ bits) for i in range(devices)])]
    ppermute x4 -> x2, starting transfers between devices: 3.91 us -> 2.57 us  [body(): afters.append(lax.ppermute(head, AXES, back))]
    pallas_call x0 -> x2, Pallas kernels: none -> 0.72 us  [the longest x1 0.67 us: join(): pl.pallas_call(join_kernel, in_specs=[SMEM_SPEC] + [VMEM_SPEC] * 2, out_s...]
  transfers between devices with their start and end apart: 21 -> 16, of which waited for: 9 -> 7; matrix products, arithmetic and copies ran while one was open for 0% -> 0% of each run, Pallas kernels for 8% -> 7%
where the time goes in v6:
time: 64.6 us; the launch traced here: 64.3 us
  waiting for transfers between devices  26.5 us (41%)
  starting transfers between devices  25.7 us (40%)
  Pallas kernels  11.2 us (17%)
  between operations  0.84 us (1%)
    ppermute x14, waiting for transfers between devices, swap(): return lax.ppermute(x, AXES, [(i, i ^ bits) for i in range(devices)])  26.5 us
    ppermute x14, starting transfers between devices, swap(): return lax.ppermute(x, AXES, [(i, i ^ bits) for i in range(devices)])  23.2 us
    ppermute x2, starting transfers between devices, body(): afters.append(lax.ppermute(head, AXES, back))  2.57 us
    pallas_call x1, Pallas kernels, value_grad_pair(): pl.pallas_call(functools.partial(value_grad_kernel, len(far)), in_specs=[...  2.28 us
    pallas_call x2, Pallas kernels, tap_grad(): pl.pallas_call(functools.partial(tap_grad_kernel, piece), in_specs=[SMEM_...  2.1 us
    pallas_call x1, Pallas kernels, cotangent_pair(): pl.pallas_call(functools.partial(cotangent_pair_kernel, pieces, shard), i...  1.93 us
    pallas_call x1, Pallas kernels, near_window(): pl.pallas_call(near_window_kernel, in_specs=[SMEM_SPEC] + [VMEM_SPEC] * 6...  1.47 us
    pallas_call x1, Pallas kernels, split(): pl.pallas_call(functools.partial(split_kernel, shard), in_specs=[SMEM_SPE...  1.39 us
  transfers between devices with their start and end apart: 16, of which 7 were waited for; matrix products, arithmetic and copies ran while one was open for 0% of the time, Pallas kernels for 7%

profile of v6, /device:TPU:0, one launch (start us, length us, event | category | flops | bytes accessed | tf_op | source)
XLA Modules:
  0.0 64.3 jit_solution(8093100853778119047)
XLA Ops:
  0.6 0.0 copy-start.3
  0.6 1.9 %cotangent_pair.1 = (bf16[128,2048]{1,0:T(8,128)(2,1)S(1)}, bf16[128,2048]{1,0:T(8,128)(2,1)S(1)}) custom-call(s32[1]{0:T(128)} %bitcast.me_ref, s32[1,128]{1,0:T(1,128)} %ids_hbm.1, bf16[128,4096]{1,0:T(8,128)(2,1)} %bitcast.7, bf16[128,4096]{1,0:T(8,128)(2,1)} %bitcast.8), custom_call_target="tpu_custom_call" | custom-call | flops 1048576 | bytes 4194304 | tf_op jit(solution)/shard_map/cotangent_pair/pallas_call | solution.py:170
  2.6 0.0 copy-start.1
  2.6 0.0 copy-start.2
  2.6 0.6 collective-permute-start
  3.2 1.4 %split.1 = (bf16[128,2048]{1,0:T(8,128)(2,1)S(1)}, bf16[128,2048]{1,0:T(8,128)(2,1)S(1)}) custom-call(s32[1]{0:T(128)} %bitcast.me_ref, bf16[128,4096]{1,0:T(8,128)(2,1)} %bitcast.6), custom_call_target="tpu_custom_call" | custom-call | flops 1 | bytes 2097152 | tf_op jit(solution)/shard_map/split/pallas_call | solution.py:223
  4.6 0.1 collective-permute-start.1
  4.7 3.0 %collective-permute-start.4 = (bf16[256,128]{1,0:T(8,128)(2,1)S(1)}, bf16[256,128]{1,0:T(8,128)(2,1)S(1)}, u32[]{:S(2)}, u32[]{:S(2)}) collective-permute-start(bf16[256,128]{1,0:T(8,128)(2,1)S(1)} %copy-done.3), channel_id=1, source_target_pairs={{0,2},{1,3},{2,0},{3,1},{4,6},{5,7},{6,4},{7,5},{8,10},{9,11},{10,... | collective-permute-start | bytes 196616 | tf_op jit(solution)/shard_map/ppermute | solution.py:556
  7.6 2.3 %collective-permute-done.4.refs_1_ = bf16[256,128]{1,0:T(8,128)(2,1)S(1)} collective-permute-done((bf16[256,128]{1,0:T(8,128)(2,1)S(1)}, bf16[256,128]{1,0:T(8,128)(2,1)S(1)}, u32[]{:S(2)}, u32[]{:S(2)}) %collective-permute-start.4) | collective-permute-done | bytes 65568 | tf_op jit(solution)/shard_map/ppermute | solution.py:556
  10.0 2.0 %collective-permute-start.5 = (bf16[2,256,128]{2,1,0:T(8,128)(2,1)S(1)}, bf16[2,256,128]{2,1,0:T(8,128)(2,1)S(1)}, u32[]{:S(2)}, u32[]{:S(2)}) collective-permute-start(bf16[2,256,128]{2,1,0:T(8,128)(2,1)S(1)} %collect.2.refs_0_), channel_id=1, source_target_pairs={{0,4},{1,5},{2,6},{3,7},{4,0},{5,1},{6,2},{7,3},{8,12},{9,13},{10,... | collective-permute-start | bytes 393224 | tf_op jit(solution)/shard_map/ppermute | solution.py:556
  12.0 0.0 collective-permute-done.got_ref
  12.0 0.1 heads.1
  12.1 1.3 %collective-permute-start.2 = (bf16[128,1024]{1,0:T(8,128)(2,1)S(1)}, bf16[128,1024]{1,0:T(8,128)(2,1)S(1)}, u32[]{:S(2)}, u32[]{:S(2)}) collective-permute-start(bf16[128,1024]{1,0:T(8,128)(2,1)S(1)} %get-tuple-element.29), channel_id=1, source_target_pairs={{2,0},{3,1},{4,2},{5,3},{6,4},{7,5},{8,6},{9,7},{10,8},{11,9},{12,... | collective-permute-start | bytes 786440 | tf_op jit(solution)/shard_map/ppermute | solution.py:566
  13.4 3.5 %collective-permute-start.6 = (bf16[2,256,128]{2,1,0:T(8,128)(2,1)S(1)}, bf16[2,256,128]{2,1,0:T(8,128)(2,1)S(1)}, u32[]{:S(2)}, u32[]{:S(2)}) collective-permute-start(bf16[2,256,128]{2,1,0:T(8,128)(2,1)S(1)} %collect.2.refs_0_), channel_id=1, source_target_pairs={{0,8},{1,9},{2,10},{3,11},{4,12},{5,13},{6,14},{7,15},{8,0},{9,1},... | collective-permute-start | bytes 393224 | tf_op jit(solution)/shard_map/ppermute | solution.py:556
  17.0 2.5 %collective-permute-start.7 = (bf16[2,256,128]{2,1,0:T(8,128)(2,1)S(1)}, bf16[2,256,128]{2,1,0:T(8,128)(2,1)S(1)}, u32[]{:S(2)}, u32[]{:S(2)}) collective-permute-start(bf16[2,256,128]{2,1,0:T(8,128)(2,1)S(1)} %collect.2.refs_0_), channel_id=1, source_target_pairs={{0,12},{1,13},{2,14},{3,15},{4,8},{5,9},{6,10},{7,11},{8,4},{9,5},... | collective-permute-start | bytes 393224 | tf_op jit(solution)/shard_map/ppermute | solution.py:556
  19.4 0.0 collective-permute-done.5.refs_1_
  19.4 1.3 %collective-permute-start.3 = (bf16[128,1024]{1,0:T(8,128)(2,1)S(1)}, bf16[128,1024]{1,0:T(8,128)(2,1)S(1)}, u32[]{:S(2)}, u32[]{:S(2)}) collective-permute-start(bf16[128,1024]{1,0:T(8,128)(2,1)S(1)} %get-tuple-element.33), channel_id=1, source_target_pairs={{2,0},{3,1},{4,2},{5,3},{6,4},{7,5},{8,6},{9,7},{10,8},{11,9},{12,... | collective-permute-start | bytes 786440 | tf_op jit(solution)/shard_map/ppermute | solution.py:566
  20.7 11.7 %collective-permute-done.6.refs_2_ = bf16[2,256,128]{2,1,0:T(8,128)(2,1)S(1)} collective-permute-done((bf16[2,256,128]{2,1,0:T(8,128)(2,1)S(1)}, bf16[2,256,128]{2,1,0:T(8,128)(2,1)S(1)}, u32[]{:S(2)}, u32[]{:S(2)}) %collective-permute-start.6) | collective-permute-done | bytes 131104 | tf_op jit(solution)/shard_map/ppermute | solution.py:556
  32.5 0.0 collective-permute-done.7.refs_3_
  32.5 0.0 copy-start
  32.5 0.0 collective-permute-done.1.val_got_ref
  32.5 1.5 %near_window.1 = (f32[256,2048]{1,0:T(8,128)S(1)}, f32[256,2048]{1,0:T(8,128)S(1)}, f32[256,2048]{1,0:T(8,128)S(1)}) custom-call(s32[1]{0:T(128)} %bitcast.me_ref, bf16[128,2048]{1,0:T(8,128)(2,1)S(1)} %get-tuple-element.24.own_ref, bf16[128,2048]{1,0:T(8,128)(2,1)S(1)} %collective-permute-done.got_ref, bf16[128,2048]{1,0:T(8,128)(2,1)S(1)} %get-tuple-element.26.val_ref, ...), custom_call_target="tpu_custom_call" | custom-call | flops 1073741824 | bytes 8388608 | tf_op jit(solution)/shard_map/near_window/pallas_call | solution.py:251
  34.0 0.0 collective-permute-done.2.after_ref
  34.0 0.0 copy-done
  34.0 1.0 %tap_grad.2 = (f32[128,1024]{1,0:T(8,128)S(1)}, f32[256,1024]{1,0:T(8,128)S(1)}) custom-call(s32[1]{0:T(128)} %bitcast.me_ref, bf16[128,2048]{1,0:T(8,128)(2,1)S(1)} %get-tuple-element.24.own_ref, bf16[128,2048]{1,0:T(8,128)(2,1)S(1)} %collective-permute-done.got_ref, bf16[128,1024]{1,0:T(8,128)(2,1)S(1)} %collective-permute-done.2.after_ref, ...), custom_call_target="tpu_custom_call" | custom-call | flops 469762048 | bytes 3145728 | tf_op jit(solution)/shard_map/tap_grad/pallas_call | solution.py:299
  35.0 0.0 collective-permute-done.3.after_ref
  35.0 1.1 %tap_grad.3 = (f32[4,128,128]{2,1,0:T(8,128)S(1)}, bf16[4,128,128]{2,1,0:T(8,128)(2,1)S(1)}, bf16[4,128,128]{2,1,0:T(8,128)(2,1)S(1)}, bf16[4,128,128]{2,1,0:T(8,128)(2,1)S(1)}, f32[256,1024]{1,0:T(8,128)S(1)}) custom-call(s32[1]{0:T(128)} %bitcast.me_ref, bf16[128,2048]{1,0:T(8,128)(2,1)S(1)} %get-tuple-element.24.own_ref, ...), custom_call_target="tpu_custom_call" | custom-call | flops 469762048 | bytes 3145728 | tf_op jit(solution)/shard_map/tap_grad/pallas_call | solution.py:299
  36.2 2.3 %value_grad_pair.1 = (bf16[128,2048]{1,0:T(8,128)(2,1)S(1)}, bf16[128,2048]{1,0:T(8,128)(2,1)S(1)}) custom-call(s32[1]{0:T(128)} %bitcast.me_ref, f32[256,2048]{1,0:T(8,128)S(1)} %get-tuple-element.28.x_ref, f32[256,1024]{1,0:T(8,128)S(1)} %get-tuple-element.32.refs_0_, f32[256,1024]{1,0:T(8,128)S(1)} %get-tuple-element.35.refs_1_, ...), custom_call_target="tpu_custom_call" | custom-call | flops 1073741824 | bytes 6291456 | tf_op jit(solution)/shard_map/value_grad_pair/pallas_call | solution.py:492
  38.5 0.1 collective-permute-start.8
  38.5 1.6 %collective-permute-start.9 = (bf16[4,128,128]{2,1,0:T(8,128)(2,1)S(1)}, bf16[4,128,128]{2,1,0:T(8,128)(2,1)S(1)}, u32[]{:S(2)}, u32[]{:S(2)}) collective-permute-start(bf16[4,128,128]{2,1,0:T(8,128)(2,1)S(1)} %get-tuple-element.39), channel_id=1, source_target_pairs={{0,16},{1,17},{2,18},{3,19},{4,20},{5,21},{6,22},{7,23},{8,24},{9,... | collective-permute-start | bytes 393224 | tf_op jit(solution)/shard_map/ppermute | solution.py:556
  40.1 0.0 collective-permute-start.10
  40.1 2.0 %collective-permute-start.11 = (bf16[4,128,128]{2,1,0:T(8,128)(2,1)S(1)}, bf16[4,128,128]{2,1,0:T(8,128)(2,1)S(1)}, u32[]{:S(2)}, u32[]{:S(2)}) collective-permute-start(bf16[4,128,128]{2,1,0:T(8,128)(2,1)S(1)} %get-tuple-element.41), channel_id=1, source_target_pairs={{0,18},{1,19},{2,16},{3,17},{4,22},{5,23},{6,20},{7,21},{8,26},{9,... | collective-permute-start | bytes 393224 | tf_op jit(solution)/shard_map/ppermute | solution.py:556
  42.1 2.8 %collective-permute-done.9.refs_1_ = bf16[4,128,128]{2,1,0:T(8,128)(2,1)S(1)} collective-permute-done((bf16[4,128,128]{2,1,0:T(8,128)(2,1)S(1)}, bf16[4,128,128]{2,1,0:T(8,128)(2,1)S(1)}, u32[]{:S(2)}, u32[]{:S(2)}) %collective-permute-start.9) | collective-permute-done | bytes 131104 | tf_op jit(solution)/shard_map/ppermute | solution.py:556
  44.8 3.6 %collective-permute-done.10.refs_2_ = bf16[4,128,128]{2,1,0:T(8,128)(2,1)S(1)} collective-permute-done((bf16[4,128,128]{2,1,0:T(8,128)(2,1)S(1)}, bf16[4,128,128]{2,1,0:T(8,128)(2,1)S(1)}, u32[]{:S(2)}, u32[]{:S(2)}) %collective-permute-start.10) | collective-permute-done | bytes 131104 | tf_op jit(solution)/shard_map/ppermute | solution.py:556
  48.4 0.0 collective-permute-done.11.refs_3_
  48.5 0.1 along_line.1
  48.5 3.9 %collective-permute-start.12 = (bf16[128,128]{1,0:T(8,128)(2,1)S(1)}, bf16[128,128]{1,0:T(8,128)(2,1)S(1)}, u32[]{:S(2)}, u32[]{:S(2)}) collective-permute-start(bf16[128,128]{1,0:T(8,128)(2,1)S(1)} %get-tuple-element.43), channel_id=1, source_target_pairs={{0,4},{1,5},{2,6},{3,7},{4,0},{5,1},{6,2},{7,3},{8,12},{9,13},{10,... | collective-permute-start | bytes 98312 | tf_op jit(solution)/shard_map/ppermute | solution.py:556
  52.4 0.0 collective-permute-start.13
  52.4 2.4 %collective-permute-start.14 = (bf16[128,128]{1,0:T(8,128)(2,1)S(1)}, bf16[128,128]{1,0:T(8,128)(2,1)S(1)}, u32[]{:S(2)}, u32[]{:S(2)}) collective-permute-start(bf16[128,128]{1,0:T(8,128)(2,1)S(1)} %get-tuple-element.45), channel_id=1, source_target_pairs={{0,12},{1,13},{2,14},{3,15},{4,8},{5,9},{6,10},{7,11},{8,4},{9,5},... | collective-permute-start | bytes 98312 | tf_op jit(solution)/shard_map/ppermute | solution.py:556
  54.8 0.0 collective-permute-done.12.refs_0_
  54.8 2.4 %collective-permute-done.13.refs_1_ = bf16[128,128]{1,0:T(8,128)(2,1)S(1)} collective-permute-done((bf16[128,128]{1,0:T(8,128)(2,1)S(1)}, bf16[128,128]{1,0:T(8,128)(2,1)S(1)}, u32[]{:S(2)}, u32[]{:S(2)}) %collective-permute-start.13) | collective-permute-done | bytes 32800 | tf_op jit(solution)/shard_map/ppermute | solution.py:556
  57.2 0.9 %collective-permute-done.14.refs_2_ = bf16[128,128]{1,0:T(8,128)(2,1)S(1)} collective-permute-done((bf16[128,128]{1,0:T(8,128)(2,1)S(1)}, bf16[128,128]{1,0:T(8,128)(2,1)S(1)}, u32[]{:S(2)}, u32[]{:S(2)}) %collective-permute-start.14) | collective-permute-done | bytes 32800 | tf_op jit(solution)/shard_map/ppermute | solution.py:556
  58.1 0.1 finish.1.mine_ref
  58.2 1.5 %collective-permute-start.15 = (f32[128,128]{1,0:T(8,128)S(1)}, f32[128,128]{1,0:T(8,128)S(1)}, u32[]{:S(2)}, u32[]{:S(2)}) collective-permute-start(f32[128,128]{1,0:T(8,128)S(1)} %finish.1.mine_ref), channel_id=1, source_target_pairs={{0,16},{1,17},{2,18},{3,19},{4,20},{5,21},{6,22},{7,23},{8,24},{9,... | collective-permute-start | bytes 196616 | tf_op jit(solution)/shard_map/ppermute | solution.py:556
  59.7 2.8 %collective-permute-done.15.other_ref = f32[128,128]{1,0:T(8,128)S(1)} collective-permute-done((f32[128,128]{1,0:T(8,128)S(1)}, f32[128,128]{1,0:T(8,128)S(1)}, u32[]{:S(2)}, u32[]{:S(2)}) %collective-permute-start.15) | collective-permute-done | bytes 65568 | tf_op jit(solution)/shard_map/ppermute | solution.py:556
  62.6 0.7 %join.1 = f32[256,128]{1,0:T(8,128)} custom-call(s32[1]{0:T(128)} %bitcast.me_ref, f32[128,128]{1,0:T(8,128)S(1)} %finish.1.mine_ref, f32[128,128]{1,0:T(8,128)S(1)} %collective-permute-done.15.other_ref), custom_call_target="tpu_custom_call" | custom-call | flops 1 | bytes 262144 | tf_op jit(solution)/shard_map/join/pallas_call | solution.py:428
  63.2 0.0 collective-permute-done.8.got_ref
  63.2 1.1 %place.1 = bf16[128,4096]{1,0:T(8,128)(2,1)} custom-call(s32[1]{0:T(128)} %bitcast.me_ref, bf16[128,2048]{1,0:T(8,128)(2,1)S(1)} %get-tuple-element.36.own_ref, bf16[128,2048]{1,0:T(8,128)(2,1)S(1)} %collective-permute-done.8.got_ref), custom_call_target="tpu_custom_call" | custom-call | flops 1 | bytes 2097152 | tf_op jit(solution)/shard_map/place/pallas_call | solution.py:402
  (5 shorter events, 0.1 us)
Async XLA Ops:
  0.6 4.1 %copy-start.3 = (bf16[256,128]{1,0:T(8,128)(2,1)S(1)}, bf16[256,128]{1,0:T(8,128)(2,1)}, u32[]{:S(2)}) copy-start(bf16[256,128]{1,0:T(8,128)(2,1)} %refs_0_.1) | copy-start | bytes 196612
  2.6 29.9 %copy-start.1 = (bf16[512,256]{1,0:T(8,128)(2,1)S(1)}, bf16[512,256]{1,0:T(8,128)(2,1)}, u32[]{:S(2)}) copy-start(bf16[512,256]{1,0:T(8,128)(2,1)} %constant.17.clone.wx_ref) | copy-start | bytes 786436
  2.6 29.9 %copy-start.2 = (bf16[256,256]{1,0:T(8,128)(2,1)S(1)}, bf16[256,256]{1,0:T(8,128)(2,1)}, u32[]{:S(2)}) copy-start(bf16[256,256]{1,0:T(8,128)(2,1)} %constant.18.clone.wv_ref.refs_3_) | copy-start | bytes 393220
  2.6 9.4 %collective-permute-start = (bf16[128,2048]{1,0:T(8,128)(2,1)S(1)}, bf16[128,2048]{1,0:T(8,128)(2,1)S(1)}, u32[]{:S(2)}, u32[]{:S(2)}) collective-permute-start(bf16[128,2048]{1,0:T(8,128)(2,1)S(1)} %get-tuple-element.25), channel_id=1, source_target_pairs={{0,1},{1,0},{2,3},{3,2},{4,5},{5,4},{6,7},{7,6},{8,9},{9,8},{10,11... | collective-permute-start | bytes 1572872 | tf_op jit(solution)/shard_map/ppermute | solution.py:556
  4.6 28.0 %collective-permute-start.1 = (bf16[128,2048]{1,0:T(8,128)(2,1)S(1)}, bf16[128,2048]{1,0:T(8,128)(2,1)S(1)}, u32[]{:S(2)}, u32[]{:S(2)}) collective-permute-start(bf16[128,2048]{1,0:T(8,128)(2,1)S(1)} %get-tuple-element.27), channel_id=1, source_target_pairs={{0,1},{1,0},{2,3},{3,2},{4,5},{5,4},{6,7},{7,6},{8,9},{9,8},{10,11... | collective-permute-start | bytes 1572872 | tf_op jit(solution)/shard_map/ppermute | solution.py:556
  4.7 5.3 %collective-permute-start.4 = (bf16[256,128]{1,0:T(8,128)(2,1)S(1)}, bf16[256,128]{1,0:T(8,128)(2,1)S(1)}, u32[]{:S(2)}, u32[]{:S(2)}) collective-permute-start(bf16[256,128]{1,0:T(8,128)(2,1)S(1)} %copy-done.3), channel_id=1, source_target_pairs={{0,2},{1,3},{2,0},{3,1},{4,6},{5,7},{6,4},{7,5},{8,10},{9,11},{10,... | collective-permute-start | bytes 196616 | tf_op jit(solution)/shard_map/ppermute | solution.py:556
  10.0 9.4 %collective-permute-start.5 = (bf16[2,256,128]{2,1,0:T(8,128)(2,1)S(1)}, bf16[2,256,128]{2,1,0:T(8,128)(2,1)S(1)}, u32[]{:S(2)}, u32[]{:S(2)}) collective-permute-start(bf16[2,256,128]{2,1,0:T(8,128)(2,1)S(1)} %collect.2.refs_0_), channel_id=1, source_target_pairs={{0,4},{1,5},{2,6},{3,7},{4,0},{5,1},{6,2},{7,3},{8,12},{9,13},{10,... | collective-permute-start | bytes 393224 | tf_op jit(solution)/shard_map/ppermute | solution.py:556
  12.1 21.9 %collective-permute-start.2 = (bf16[128,1024]{1,0:T(8,128)(2,1)S(1)}, bf16[128,1024]{1,0:T(8,128)(2,1)S(1)}, u32[]{:S(2)}, u32[]{:S(2)}) collective-permute-start(bf16[128,1024]{1,0:T(8,128)(2,1)S(1)} %get-tuple-element.29), channel_id=1, source_target_pairs={{2,0},{3,1},{4,2},{5,3},{6,4},{7,5},{8,6},{9,7},{10,8},{11,9},{12,... | collective-permute-start | bytes 786440 | tf_op jit(solution)/shard_map/ppermute | solution.py:566
  13.4 19.0 %collective-permute-start.6 = (bf16[2,256,128]{2,1,0:T(8,128)(2,1)S(1)}, bf16[2,256,128]{2,1,0:T(8,128)(2,1)S(1)}, u32[]{:S(2)}, u32[]{:S(2)}) collective-permute-start(bf16[2,256,128]{2,1,0:T(8,128)(2,1)S(1)} %collect.2.refs_0_), channel_id=1, source_target_pairs={{0,8},{1,9},{2,10},{3,11},{4,12},{5,13},{6,14},{7,15},{8,0},{9,1},... | collective-permute-start | bytes 393224 | tf_op jit(solution)/shard_map/ppermute | solution.py:556
  17.0 15.5 %collective-permute-start.7 = (bf16[2,256,128]{2,1,0:T(8,128)(2,1)S(1)}, bf16[2,256,128]{2,1,0:T(8,128)(2,1)S(1)}, u32[]{:S(2)}, u32[]{:S(2)}) collective-permute-start(bf16[2,256,128]{2,1,0:T(8,128)(2,1)S(1)} %collect.2.refs_0_), channel_id=1, source_target_pairs={{0,12},{1,13},{2,14},{3,15},{4,8},{5,9},{6,10},{7,11},{8,4},{9,5},... | collective-permute-start | bytes 393224 | tf_op jit(solution)/shard_map/ppermute | solution.py:556
  19.4 15.6 %collective-permute-start.3 = (bf16[128,1024]{1,0:T(8,128)(2,1)S(1)}, bf16[128,1024]{1,0:T(8,128)(2,1)S(1)}, u32[]{:S(2)}, u32[]{:S(2)}) collective-permute-start(bf16[128,1024]{1,0:T(8,128)(2,1)S(1)} %get-tuple-element.33), channel_id=1, source_target_pairs={{2,0},{3,1},{4,2},{5,3},{6,4},{7,5},{8,6},{9,7},{10,8},{11,9},{12,... | collective-permute-start | bytes 786440 | tf_op jit(solution)/shard_map/ppermute | solution.py:566
  32.5 1.5 %copy-start = (bf16[256,256]{1,0:T(8,128)(2,1)S(1)}, bf16[256,256]{1,0:T(8,128)(2,1)}, u32[]{:S(2)}) copy-start(bf16[256,256]{1,0:T(8,128)(2,1)} %constant.19.clone.wi_ref.refs_4_) | copy-start | bytes 393220
  38.5 24.8 %collective-permute-start.8 = (bf16[128,2048]{1,0:T(8,128)(2,1)S(1)}, bf16[128,2048]{1,0:T(8,128)(2,1)S(1)}, u32[]{:S(2)}, u32[]{:S(2)}) collective-permute-start(bf16[128,2048]{1,0:T(8,128)(2,1)S(1)} %get-tuple-element.37), channel_id=1, source_target_pairs={{0,1},{1,0},{2,3},{3,2},{4,5},{5,4},{6,7},{7,6},{8,9},{9,8},{10,11... | collective-permute-start | bytes 1572872 | tf_op jit(solution)/shard_map/ppermute | solution.py:556
  38.5 6.3 %collective-permute-start.9 = (bf16[4,128,128]{2,1,0:T(8,128)(2,1)S(1)}, bf16[4,128,128]{2,1,0:T(8,128)(2,1)S(1)}, u32[]{:S(2)}, u32[]{:S(2)}) collective-permute-start(bf16[4,128,128]{2,1,0:T(8,128)(2,1)S(1)} %get-tuple-element.39), channel_id=1, source_target_pairs={{0,16},{1,17},{2,18},{3,19},{4,20},{5,21},{6,22},{7,23},{8,24},{9,... | collective-permute-start | bytes 393224 | tf_op jit(solution)/shard_map/ppermute | solution.py:556
  40.1 8.4 %collective-permute-start.10 = (bf16[4,128,128]{2,1,0:T(8,128)(2,1)S(1)}, bf16[4,128,128]{2,1,0:T(8,128)(2,1)S(1)}, u32[]{:S(2)}, u32[]{:S(2)}) collective-permute-start(bf16[4,128,128]{2,1,0:T(8,128)(2,1)S(1)} %get-tuple-element.40), channel_id=1, source_target_pairs={{0,2},{1,3},{2,0},{3,1},{4,6},{5,7},{6,4},{7,5},{8,10},{9,11},{10,... | collective-permute-start | bytes 393224 | tf_op jit(solution)/shard_map/ppermute | solution.py:556
  40.1 8.4 %collective-permute-start.11 = (bf16[4,128,128]{2,1,0:T(8,128)(2,1)S(1)}, bf16[4,128,128]{2,1,0:T(8,128)(2,1)S(1)}, u32[]{:S(2)}, u32[]{:S(2)}) collective-permute-start(bf16[4,128,128]{2,1,0:T(8,128)(2,1)S(1)} %get-tuple-element.41), channel_id=1, source_target_pairs={{0,18},{1,19},{2,16},{3,17},{4,22},{5,23},{6,20},{7,21},{8,26},{9,... | collective-permute-start | bytes 393224 | tf_op jit(solution)/shard_map/ppermute | solution.py:556
  48.5 6.3 %collective-permute-start.12 = (bf16[128,128]{1,0:T(8,128)(2,1)S(1)}, bf16[128,128]{1,0:T(8,128)(2,1)S(1)}, u32[]{:S(2)}, u32[]{:S(2)}) collective-permute-start(bf16[128,128]{1,0:T(8,128)(2,1)S(1)} %get-tuple-element.43), channel_id=1, source_target_pairs={{0,4},{1,5},{2,6},{3,7},{4,0},{5,1},{6,2},{7,3},{8,12},{9,13},{10,... | collective-permute-start | bytes 98312 | tf_op jit(solution)/shard_map/ppermute | solution.py:556
  52.4 4.8 %collective-permute-start.13 = (bf16[128,128]{1,0:T(8,128)(2,1)S(1)}, bf16[128,128]{1,0:T(8,128)(2,1)S(1)}, u32[]{:S(2)}, u32[]{:S(2)}) collective-permute-start(bf16[128,128]{1,0:T(8,128)(2,1)S(1)} %get-tuple-element.44), channel_id=1, source_target_pairs={{0,8},{1,9},{2,10},{3,11},{4,12},{5,13},{6,14},{7,15},{8,0},{9,1},... | collective-permute-start | bytes 98312 | tf_op jit(solution)/shard_map/ppermute | solution.py:556
  52.4 5.7 %collective-permute-start.14 = (bf16[128,128]{1,0:T(8,128)(2,1)S(1)}, bf16[128,128]{1,0:T(8,128)(2,1)S(1)}, u32[]{:S(2)}, u32[]{:S(2)}) collective-permute-start(bf16[128,128]{1,0:T(8,128)(2,1)S(1)} %get-tuple-element.45), channel_id=1, source_target_pairs={{0,12},{1,13},{2,14},{3,15},{4,8},{5,9},{6,10},{7,11},{8,4},{9,5},... | collective-permute-start | bytes 98312 | tf_op jit(solution)/shard_map/ppermute | solution.py:556
  58.2 4.3 %collective-permute-start.15 = (f32[128,128]{1,0:T(8,128)S(1)}, f32[128,128]{1,0:T(8,128)S(1)}, u32[]{:S(2)}, u32[]{:S(2)}) collective-permute-start(f32[128,128]{1,0:T(8,128)S(1)} %finish.1.mine_ref), channel_id=1, source_target_pairs={{0,16},{1,17},{2,18},{3,19},{4,20},{5,21},{6,22},{7,23},{8,24},{9,... | collective-permute-start | bytes 196616 | tf_op jit(solution)/shard_map/ppermute | solution.py:556

commit v7 on v6

--- a/solution.py
+++ b/solution.py
@@ -127,18 +127,19 @@
 
 
 def cotangent_pair_kernel(
-    pieces, shard, me_ref, ids_hbm, q_hbm, g_hbm, own_ref, other_ref, ids_ref, q_ref, g_ref, sems, ids_sem
+    piece, cuts, shard, me_ref, ids_hbm, q_hbm, g_hbm, own_ref, other_ref, ids_ref, q_ref, g_ref, sems, ids_sem
 ):
     core0 = me_ref[0] // 2 % 2 == 0
-    width = q_ref.shape[1] // pieces
+    width = q_ref.shape[1]
+    cut = width // cuts
     copies = []
     ids_copy = pltpu.make_async_copy(ids_hbm, ids_ref, ids_sem)
     ids_copy.start()
-    for i in range(pieces):
-        cols = pl.ds(i * width, width)
+    for i in range(cuts):
+        source, cols = pl.ds(piece * width + i * cut, cut), pl.ds(i * cut, cut)
         copies.append(
             [
-                pltpu.make_async_copy(src.at[:, cols], dst.at[:, cols], sems.at[n, i])
+                pltpu.make_async_copy(src.at[:, source], dst.at[:, cols], sems.at[n, i])
                 for n, (src, dst) in enumerate(((q_hbm, q_ref), (g_hbm, g_ref)))
             ]
         )
@@ -153,52 +154,49 @@
         cols = pl.ds(at, LANES)
         return (weight * g_ref[:, cols].astype(F32) * q_ref[:, cols].astype(F32)).astype(BF16)
 
-    for i in range(pieces):
+    for i in range(cuts):
         for copy in copies[i]:
             copy.wait()
-        for at in range(0, width // 2, LANES):
-            source = i * width + at // shard * 2 * shard + at % shard
+        for at in range(i * cut // 2, (i + 1) * cut // 2, LANES):
+            source = at // shard * 2 * shard + at % shard
             even, odd = cotangent(source), cotangent(source + shard)
-            cols = pl.ds(i * width // 2 + at, LANES)
+            cols = pl.ds(at, LANES)
             own_ref[:, cols] = jnp.where(core0, even, odd)
             other_ref[:, cols] = jnp.where(core0, odd, even)
 
 
-def cotangent_pair(me, token_ids, queries, out_grad, pieces, shard):
+def cotangent_pair(me, token_ids, queries, out_grad, piece, pieces, shard):
     positions, channels = queries.shape
-    half = jax.ShapeDtypeStruct((positions, channels // 2), BF16)
-    return pl.pallas_call(
-        functools.partial(cotangent_pair_kernel, pieces, shard),
+    width = channels // pieces
+    cuts = 2
+    half = jax.ShapeDtypeStruct((positions, width // 2), BF16)
+    return pl.pallas_call(
+        functools.partial(cotangent_pair_kernel, piece, cuts, shard),
         in_specs=[SMEM_SPEC] + [HBM_SPEC] * 3,
         out_specs=[VMEM_SPEC] * 2,
         out_shape=[half] * 2,
         scratch_shapes=[pltpu.VMEM(token_ids.shape, token_ids.dtype)]
-        + [pltpu.VMEM((positions, channels), BF16)] * 2
-        + [pltpu.SemaphoreType.DMA((2, pieces)), pltpu.SemaphoreType.DMA],
-        compiler_params=params(8),
-        cost_estimate=cost(2 * positions * channels, 8 * positions * channels),
+        + [pltpu.VMEM((positions, width), BF16)] * 2
+        + [pltpu.SemaphoreType.DMA((2, cuts)), pltpu.SemaphoreType.DMA],
+        compiler_params=params(8),
+        cost_estimate=cost(2 * positions * width, 6 * positions * width),
         name="cotangent_pair",
     )(me, *(pltpu.with_memory_space_constraint(x, pltpu.HBM) for x in (token_ids, queries, out_grad)))
 
 
-def heads_kernel(me_ref, own_ref, got_ref, *head_refs):
-    core0 = me_ref[0] // 2 % 2 == 0
-    for i, ref in enumerate(head_refs):
-        cols = pl.ds(i * ref.shape[1], ref.shape[1])
-        ref[...] = jnp.where(core0, own_ref[:, cols], got_ref[:, cols])
-
-
-def heads(me, own, got, pieces):
-    positions, width = own.shape
-    piece = jax.ShapeDtypeStruct((positions, width // pieces), own.dtype)
-    return pl.pallas_call(
-        heads_kernel,
+def head_kernel(me_ref, own_ref, got_ref, head_ref):
+    head_ref[...] = jnp.where(me_ref[0] // 2 % 2 == 0, own_ref[...], got_ref[...])
+
+
+def head(me, own, got):
+    return pl.pallas_call(
+        head_kernel,
         in_specs=[SMEM_SPEC] + [VMEM_SPEC] * 2,
-        out_specs=[VMEM_SPEC] * pieces,
-        out_shape=[piece] * pieces,
-        compiler_params=params(8),
-        cost_estimate=cost(1, 6 * positions * width),
-        name="heads",
+        out_specs=VMEM_SPEC,
+        out_shape=jax.ShapeDtypeStruct(own.shape, own.dtype),
+        compiler_params=params(8),
+        cost_estimate=cost(1, 6 * own.size),
+        name="head",
     )(me, own, got)
 
 
@@ -233,10 +231,12 @@
 
 
 def near_window_kernel(
-    me_ref, own_ref, got_ref, val_ref, val_got_ref, wx_ref, wv_ref, x_ref, product_ref, v_ref
+    pieces, me_ref, *refs
 ):
+    owns, gots = refs[:pieces], refs[pieces : 2 * pieces]
+    val_ref, val_got_ref, wx_ref, wv_ref, x_ref, product_ref, v_ref = refs[2 * pieces :]
     core0 = me_ref[0] // 2 % 2 == 0
-    own, got = own_ref[...], got_ref[...]
+    own, got = (jnp.concatenate([ref[...] for ref in refs], axis=1) for refs in (owns, gots))
     x = spectrum_of_window(wx_ref[...], jnp.where(core0, own, got), jnp.where(core0, got, own))
     x_ref[...] = x
     own, got = val_ref[...], val_got_ref[...]
@@ -245,67 +245,58 @@
 
 
 def near_window(me, own, got, values, values_got, taps):
-    positions, width = own.shape
+    positions, width = values.shape
     wx, wv, _, _, _ = transforms(positions, taps)
     spectrum = jax.ShapeDtypeStruct((wx.shape[1], width), F32)
     return pl.pallas_call(
-        near_window_kernel,
-        in_specs=[SMEM_SPEC] + [VMEM_SPEC] * 6,
+        functools.partial(near_window_kernel, len(own)),
+        in_specs=[SMEM_SPEC] + [VMEM_SPEC] * (2 * len(own) + 4),
         out_specs=[VMEM_SPEC] * 3,
         out_shape=[spectrum] * 3,
         compiler_params=params(24),
         cost_estimate=cost(2 * 8 * 128 * 256 * width, 32 * positions * width),
         name="near_window",
-    )(me, own, got, values, values_got, wx, wv)
+    )(me, *own, *got, values, values_got, wx, wv)
 
 
 def tap_grad_kernel(
-    piece, me_ref, own_ref, got_ref, after_ref, product_ref, v_ref, wx_ref, wi_ref, *refs
+    piece, last_chip, me_ref, own_ref, got_ref, after_ref, product_ref, v_ref, wx_ref, wi_ref, *refs
 ):
+    mine_ref, *send_refs, x_ref, tmp_ref = refs
     width = after_ref.shape[1]
     cols = pl.ds(piece * width, width)
     me = me_ref[0]
     core0, row, rank = me // 2 % 2 == 0, me // 4 % 2, me % 2
-    own = jnp.where(core0, got_ref[:, cols], own_ref[:, cols])
-    x = spectrum_of_window(wx_ref[...], own, after_ref[...])
+    own = jnp.where(core0, got_ref[...], own_ref[...])
+    after = jnp.where(me // 4 == last_chip, 0.0, after_ref[...]).astype(BF16)
+    x = spectrum_of_window(wx_ref[...], own, after)
+    x_ref[...] = x
     out = inverted(product_ref[:, cols] + cross(x, v_ref[:, cols]), wi_ref[...])
-    if len(refs) == 2:
-        out_ref, x_ref = refs
-        out_ref[...], x_ref[...] = out, x
-        return
-    before_refs, (mine_ref, *send_refs, x_ref, tmp_ref) = refs[:piece], refs[piece:]
-    x_ref[...] = x
-    per_piece = width // LANES
-    for block in range((piece + 1) * per_piece):
+    for block in range(width // LANES):
         half, y, z = block % 2, block // 2 % 2, block // 4
-        at = block % per_piece * LANES
-        source = before_refs[block // per_piece] if block < piece * per_piece else out
-        tmp_ref[(half ^ rank) + 2 * (y ^ row), z] = source[:, at : at + LANES]
+        tmp_ref[(half ^ rank) + 2 * (y ^ row), z] = out[:, block * LANES : (block + 1) * LANES]
     mine_ref[...] = tmp_ref[0]
     for k, ref in enumerate(send_refs, 1):
         ref[...] = tmp_ref[k].astype(BF16)
 
 
-def tap_grad(me, own, got, after, product, v, taps, piece, pieces, before):
+def tap_grad(me, own, got, after, product, v, taps, piece, last_chip):
     positions, width = after.shape
     wx, _, _, wi, _ = transforms(positions, taps)
-    block = (pieces * width // (4 * LANES), taps, LANES)
-    last = piece == pieces - 1
-    out_shape = [jax.ShapeDtypeStruct((taps, width), F32)]
-    if last:
-        out_shape = [jax.ShapeDtypeStruct(block, F32)] + [jax.ShapeDtypeStruct(block, BF16)] * 3
-    out_shape.append(jax.ShapeDtypeStruct((wx.shape[1], width), F32))
-    before = list(before) if last else []
-    return pl.pallas_call(
-        functools.partial(tap_grad_kernel, piece),
-        in_specs=[SMEM_SPEC] + [VMEM_SPEC] * (7 + len(before)),
-        out_specs=[VMEM_SPEC] * len(out_shape),
-        out_shape=out_shape,
-        scratch_shapes=[pltpu.VMEM((4, *block), F32)] if last else [],
+    depth = width // (4 * LANES)
+    block = (depth, taps, LANES)
+    return pl.pallas_call(
+        functools.partial(tap_grad_kernel, piece, last_chip),
+        in_specs=[SMEM_SPEC] + [VMEM_SPEC] * 7,
+        out_specs=[VMEM_SPEC] * 5,
+        out_shape=[jax.ShapeDtypeStruct(block, F32)]
+        + [jax.ShapeDtypeStruct(block, BF16)] * 3
+        + [jax.ShapeDtypeStruct((wx.shape[1], width), F32)],
+        scratch_shapes=[pltpu.VMEM((4, *block), F32)],
         compiler_params=params(24),
         cost_estimate=cost(2 * 7 * 128 * 256 * width, 24 * positions * width),
         name="tap_grad",
-    )(me, own, got, after, product, v, wx, wi, *before)
+    )(me, own, got, after, product, v, wx, wi)
 
 
 def collect_kernel(*refs):
@@ -555,27 +546,32 @@
     def swap(x, bits):
         return lax.ppermute(x, AXES, [(i, i ^ bits) for i in range(devices)])
 
-    back = [(seq * parts + i, seq * parts + i - 2) for seq in range(seqs) for i in range(2, parts)]
+    back = [
+        (seq * parts + i, seq * parts + (i - 2) % parts) for seq in range(seqs) for i in range(parts)
+    ]
+    back_open = [pair for pair in back if pair[1] % parts < parts - 2]
+    last_chip = parts // 2 - 1
     hops = (parts, 2, parts + 2)
     filters_y = swap(filters, 2)
 
-    own, other = cotangent_pair(me, token_ids, queries, out_grad, 2 * pieces, shard)
-    got = swap(other, 1)
-    afters = []
-    for head in heads(me, own, got, pieces):
-        afters.append(lax.ppermute(head, AXES, back))
+    own, got, afters = [], [], []
+    for i in range(pieces):
+        mine, other = cotangent_pair(me, token_ids, queries, out_grad, i, pieces, shard)
+        own.append(mine)
+        got.append(swap(other, 1))
+    for i in range(pieces):
+        first = head(me, own[i], got[i])
+        afters.append(lax.ppermute(first, AXES, back_open if i else back))
     values, other = split(me, gated_values, shard)
     values_got = swap(other, 1)
     near, product, v = near_window(me, own, got, values, values_got, taps)
 
-    shares, far = [], []
+    sums, far = [], []
     for i in range(pieces):
-        *shares, x = tap_grad(
-            me, own, got, afters[i], product, v, taps, i, pieces, shares
-        )
+        mine, *sends, x = tap_grad(me, own[i], got[i], afters[i], product, v, taps, i, last_chip)
+        got_sends = [swap(x, hops[k]) for k, x in enumerate(sends)]
+        sums.append([mine] + got_sends)
         far.append(x)
-    mine, *sends = shares
-    sums = [[mine] + [swap(x, bits) for x, bits in zip(sends, hops)]]
 
     filters = collect([filters, filters_y])
     filters = [filters] + [swap(filters, 4 * k) for k in range(1, depth)]

time: 64.6 us -> 67.1 us (1.039)
  starting transfers between devices: 25.7 us -> 26.8 us
  Pallas kernels: 11.2 us -> 12.1 us
    ppermute x2, starting transfers between devices: 2.57 us -> 4.78 us  [body(): afters.append(lax.ppermute(first, AXES, back_open if i else back))]
    ppermute x14 -> x18, starting transfers between devices: 23.2 us -> 22 us  [swap(): return lax.ppermute(x, AXES, [(i, i ^ bits) for i in range(devices)])]
    pallas_call x5 -> x7, Pallas kernels: 5.56 us -> 6.39 us  [the longest x2 2.81 us: cotangent_pair(): pl.pallas_call(functools.partial(cotangent_pair_kernel, piece, cuts, shar...]
    ppermute x14 -> x18, waiting for transfers between devices: 26.5 us -> 27.1 us  [swap(): return lax.ppermute(x, AXES, [(i, i ^ bits) for i in range(devices)])]
  transfers between devices with their start and end apart: 16 -> 20, of which waited for: 7 -> 10; matrix products, arithmetic and copies ran while one was open for 0% -> 0% of each run, Pallas kernels for 7% -> 9%
where the time goes in v7:
time: 67.1 us; the launch traced here: 66.8 us
  waiting for transfers between devices  27.1 us (40%)
  starting transfers between devices  26.8 us (40%)
  Pallas kernels  12.1 us (18%)
  between operations  0.85 us (1%)
    ppermute x18, waiting for transfers between devices, swap(): return lax.ppermute(x, AXES, [(i, i ^ bits) for i in range(devices)])  27.1 us
    ppermute x18, starting transfers between devices, swap(): return lax.ppermute(x, AXES, [(i, i ^ bits) for i in range(devices)])  22 us
    ppermute x2, starting transfers between devices, body(): afters.append(lax.ppermute(first, AXES, back_open if i else back))  4.78 us
    pallas_call x2, Pallas kernels, cotangent_pair(): pl.pallas_call(functools.partial(cotangent_pair_kernel, piece, cuts, shar...  2.81 us
    pallas_call x1, Pallas kernels, value_grad_pair(): pl.pallas_call(functools.partial(value_grad_kernel, len(far)), in_specs=[...  2.28 us
    pallas_call x2, Pallas kernels, tap_grad(): pl.pallas_call(functools.partial(tap_grad_kernel, piece, last_chip), in_s...  2.06 us
    pallas_call x1, Pallas kernels, near_window(): pl.pallas_call(functools.partial(near_window_kernel, len(own)), in_specs=...  1.47 us
    pallas_call x1, Pallas kernels, split(): pl.pallas_call(functools.partial(split_kernel, shard), in_specs=[SMEM_SPE...  1.41 us
  transfers between devices with their start and end apart: 20, of which 10 were waited for; matrix products, arithmetic and copies ran while one was open for 0% of the time, Pallas kernels for 9%

profile of v7, /device:TPU:0, one launch (start us, length us, event | category | flops | bytes accessed | tf_op | source)
XLA Modules:
  0.0 66.8 jit_solution(1164518819777563095)
XLA Ops:
  0.6 1.4 %split.1 = (bf16[128,2048]{1,0:T(8,128)(2,1)S(1)}, bf16[128,2048]{1,0:T(8,128)(2,1)S(1)}) custom-call(s32[1]{0:T(128)} %bitcast.me_ref, bf16[128,4096]{1,0:T(8,128)(2,1)} %bitcast.10), custom_call_target="tpu_custom_call" | custom-call | flops 1 | bytes 2097152 | tf_op jit(solution)/shard_map/split/pallas_call | solution.py:221
  2.0 0.6 collective-permute-start.2
  2.6 1.4 %cotangent_pair.2 = (bf16[128,1024]{1,0:T(8,128)(2,1)S(1)}, bf16[128,1024]{1,0:T(8,128)(2,1)S(1)}) custom-call(s32[1]{0:T(128)} %bitcast.me_ref, s32[1,128]{1,0:T(1,128)} %ids_hbm.3, bf16[128,4096]{1,0:T(8,128)(2,1)} %bitcast.5, bf16[128,4096]{1,0:T(8,128)(2,1)} %bitcast.7), custom_call_target="tpu_custom_call" | custom-call | flops 524288 | bytes 1572864 | tf_op jit(solution)/shard_map/cotangent_pair/pallas_call | solution.py:173
  4.0 0.0 copy-start.1
  4.0 0.0 copy-start.2
  4.0 0.1 collective-permute-start
  4.1 1.4 %cotangent_pair.3 = (bf16[128,1024]{1,0:T(8,128)(2,1)S(1)}, bf16[128,1024]{1,0:T(8,128)(2,1)S(1)}) custom-call(s32[1]{0:T(128)} %bitcast.me_ref, s32[1,128]{1,0:T(1,128)} %ids_hbm.3, bf16[128,4096]{1,0:T(8,128)(2,1)} %bitcast.6, bf16[128,4096]{1,0:T(8,128)(2,1)} %bitcast.8), custom_call_target="tpu_custom_call" | custom-call | flops 524288 | bytes 1572864 | tf_op jit(solution)/shard_map/cotangent_pair/pallas_call | solution.py:173
  5.5 0.5 collective-permute-start.1
  6.1 2.6 %collective-permute-start.5 = (bf16[256,128]{1,0:T(8,128)(2,1)S(1)}, bf16[256,128]{1,0:T(8,128)(2,1)S(1)}, u32[]{:S(2)}, u32[]{:S(2)}) collective-permute-start(bf16[256,128]{1,0:T(8,128)(2,1)S(1)} %copy-done.3), channel_id=1, source_target_pairs={{0,2},{1,3},{2,0},{3,1},{4,6},{5,7},{6,4},{7,5},{8,10},{9,11},{10,... | collective-permute-start | bytes 196616 | tf_op jit(solution)/shard_map/ppermute | solution.py:547
  8.7 2.7 %collective-permute-done.5.refs_1_ = bf16[256,128]{1,0:T(8,128)(2,1)S(1)} collective-permute-done((bf16[256,128]{1,0:T(8,128)(2,1)S(1)}, bf16[256,128]{1,0:T(8,128)(2,1)S(1)}, u32[]{:S(2)}, u32[]{:S(2)}) %collective-permute-start.5) | collective-permute-done | bytes 65568 | tf_op jit(solution)/shard_map/ppermute | solution.py:547
  11.3 1.9 %collective-permute-start.6 = (bf16[2,256,128]{2,1,0:T(8,128)(2,1)S(1)}, bf16[2,256,128]{2,1,0:T(8,128)(2,1)S(1)}, u32[]{:S(2)}, u32[]{:S(2)}) collective-permute-start(bf16[2,256,128]{2,1,0:T(8,128)(2,1)S(1)} %collect.2.refs_0_), channel_id=1, source_target_pairs={{0,4},{1,5},{2,6},{3,7},{4,0},{5,1},{6,2},{7,3},{8,12},{9,13},{10,... | collective-permute-start | bytes 393224 | tf_op jit(solution)/shard_map/ppermute | solution.py:547
  13.2 0.0 collective-permute-done.refs_2_.got_ref
  13.3 3.5 %collective-permute-start.3 = (bf16[128,1024]{1,0:T(8,128)(2,1)S(1)}, bf16[128,1024]{1,0:T(8,128)(2,1)S(1)}, u32[]{:S(2)}, u32[]{:S(2)}) collective-permute-start(bf16[128,1024]{1,0:T(8,128)(2,1)S(1)} %head.2), channel_id=1, source_target_pairs={{0,14},{1,15},{2,0},{3,1},{4,2},{5,3},{6,4},{7,5},{8,6},{9,7},{10,... | collective-permute-start | bytes 786440 | tf_op jit(solution)/shard_map/ppermute | solution.py:564
  16.7 1.9 %collective-permute-start.8 = (bf16[2,256,128]{2,1,0:T(8,128)(2,1)S(1)}, bf16[2,256,128]{2,1,0:T(8,128)(2,1)S(1)}, u32[]{:S(2)}, u32[]{:S(2)}) collective-permute-start(bf16[2,256,128]{2,1,0:T(8,128)(2,1)S(1)} %collect.2.refs_0_), channel_id=1, source_target_pairs={{0,12},{1,13},{2,14},{3,15},{4,8},{5,9},{6,10},{7,11},{8,4},{9,5},... | collective-permute-start | bytes 393224 | tf_op jit(solution)/shard_map/ppermute | solution.py:547
  18.7 0.0 collective-permute-done.6.refs_1_
  18.7 1.3 %collective-permute-start.4 = (bf16[128,1024]{1,0:T(8,128)(2,1)S(1)}, bf16[128,1024]{1,0:T(8,128)(2,1)S(1)}, u32[]{:S(2)}, u32[]{:S(2)}) collective-permute-start(bf16[128,1024]{1,0:T(8,128)(2,1)S(1)} %head.3), channel_id=1, source_target_pairs={{2,0},{3,1},{4,2},{5,3},{6,4},{7,5},{8,6},{9,7},{10,8},{11,9},{12,... | collective-permute-start | bytes 786440 | tf_op jit(solution)/shard_map/ppermute | solution.py:564
  20.0 11.8 %collective-permute-done.7.refs_2_ = bf16[2,256,128]{2,1,0:T(8,128)(2,1)S(1)} collective-permute-done((bf16[2,256,128]{2,1,0:T(8,128)(2,1)S(1)}, bf16[2,256,128]{2,1,0:T(8,128)(2,1)S(1)}, u32[]{:S(2)}, u32[]{:S(2)}) %collective-permute-start.7) | collective-permute-done | bytes 131104 | tf_op jit(solution)/shard_map/ppermute | solution.py:547
  31.8 0.0 copy-start
  31.8 0.0 collective-permute-done.2.refs_5_
  31.8 1.5 %near_window.1 = (f32[256,2048]{1,0:T(8,128)S(1)}, f32[256,2048]{1,0:T(8,128)S(1)}, f32[256,2048]{1,0:T(8,128)S(1)}) custom-call(s32[1]{0:T(128)} %bitcast.me_ref, bf16[128,1024]{1,0:T(8,128)(2,1)S(1)} %get-tuple-element.27.refs_0_.own_ref, bf16[128,1024]{1,0:T(8,128)(2,1)S(1)} %get-tuple-element.28.refs_1_.own_ref, ...), custom_call_target="tpu_custom_call" | custom-call | flops 1073741824 | bytes 8388608 | tf_op jit(solution)/shard_map/near_window/pallas_call | solution.py:251
  33.3 0.0 collective-permute-done.3.after_ref
  33.3 1.0 %tap_grad.2 = (f32[2,128,128]{2,1,0:T(8,128)S(1)}, bf16[2,128,128]{2,1,0:T(8,128)(2,1)S(1)}, bf16[2,128,128]{2,1,0:T(8,128)(2,1)S(1)}, bf16[2,128,128]{2,1,0:T(8,128)(2,1)S(1)}, f32[256,1024]{1,0:T(8,128)S(1)}) custom-call(s32[1]{0:T(128)} %bitcast.me_ref, bf16[128,1024]{1,0:T(8,128)(2,1)S(1)} %get-tuple-element.27.refs_0_.own_ref, ...), custom_call_target="tpu_custom_call" | custom-call | flops 469762048 | bytes 3145728 | tf_op jit(solution)/shard_map/tap_grad/pallas_call | solution.py:288
  34.4 0.0 collective-permute-done.4.after_ref
  34.4 1.0 %tap_grad.3 = (f32[2,128,128]{2,1,0:T(8,128)S(1)}, bf16[2,128,128]{2,1,0:T(8,128)(2,1)S(1)}, bf16[2,128,128]{2,1,0:T(8,128)(2,1)S(1)}, bf16[2,128,128]{2,1,0:T(8,128)(2,1)S(1)}, f32[256,1024]{1,0:T(8,128)S(1)}) custom-call(s32[1]{0:T(128)} %bitcast.me_ref, bf16[128,1024]{1,0:T(8,128)(2,1)S(1)} %get-tuple-element.28.refs_1_.own_ref, ...), custom_call_target="tpu_custom_call" | custom-call | flops 469762048 | bytes 3145728 | tf_op jit(solution)/shard_map/tap_grad/pallas_call | solution.py:288
  35.4 2.3 %value_grad_pair.1 = (bf16[128,2048]{1,0:T(8,128)(2,1)S(1)}, bf16[128,2048]{1,0:T(8,128)(2,1)S(1)}) custom-call(s32[1]{0:T(128)} %bitcast.me_ref, f32[256,2048]{1,0:T(8,128)S(1)} %get-tuple-element.33.x_ref, f32[256,1024]{1,0:T(8,128)S(1)} %get-tuple-element.36.refs_0_, f32[256,1024]{1,0:T(8,128)S(1)} %get-tuple-element.37.refs_1_, ...), custom_call_target="tpu_custom_call" | custom-call | flops 1073741824 | bytes 6291456 | tf_op jit(solution)/shard_map/value_grad_pair/pallas_call | solution.py:483
  37.7 0.1 collective-permute-start.9
  37.8 1.6 %collective-permute-start.10 = (bf16[2,128,128]{2,1,0:T(8,128)(2,1)S(1)}, bf16[2,128,128]{2,1,0:T(8,128)(2,1)S(1)}, u32[]{:S(2)}, u32[]{:S(2)}) collective-permute-start(bf16[2,128,128]{2,1,0:T(8,128)(2,1)S(1)} %get-tuple-element.41), channel_id=1, source_target_pairs={{0,16},{1,17},{2,18},{3,19},{4,20},{5,21},{6,22},{7,23},{8,24},{9,... | collective-permute-start | bytes 196616 | tf_op jit(solution)/shard_map/ppermute | solution.py:547
  39.3 0.5 collective-permute-start.11
  39.9 1.5 %collective-permute-start.12 = (bf16[2,128,128]{2,1,0:T(8,128)(2,1)S(1)}, bf16[2,128,128]{2,1,0:T(8,128)(2,1)S(1)}, u32[]{:S(2)}, u32[]{:S(2)}) collective-permute-start(bf16[2,128,128]{2,1,0:T(8,128)(2,1)S(1)} %get-tuple-element.43), channel_id=1, source_target_pairs={{0,18},{1,19},{2,16},{3,17},{4,22},{5,23},{6,20},{7,21},{8,26},{9,... | collective-permute-start | bytes 196616 | tf_op jit(solution)/shard_map/ppermute | solution.py:547
  41.3 1.5 %collective-permute-start.13 = (bf16[2,128,128]{2,1,0:T(8,128)(2,1)S(1)}, bf16[2,128,128]{2,1,0:T(8,128)(2,1)S(1)}, u32[]{:S(2)}, u32[]{:S(2)}) collective-permute-start(bf16[2,128,128]{2,1,0:T(8,128)(2,1)S(1)} %get-tuple-element.45), channel_id=1, source_target_pairs={{0,16},{1,17},{2,18},{3,19},{4,20},{5,21},{6,22},{7,23},{8,24},{9,... | collective-permute-start | bytes 196616 | tf_op jit(solution)/shard_map/ppermute | solution.py:547
  42.8 0.5 collective-permute-start.14
  43.4 0.9 %collective-permute-done.11.refs_2_ = bf16[2,128,128]{2,1,0:T(8,128)(2,1)S(1)} collective-permute-done((bf16[2,128,128]{2,1,0:T(8,128)(2,1)S(1)}, bf16[2,128,128]{2,1,0:T(8,128)(2,1)S(1)}, u32[]{:S(2)}, u32[]{:S(2)}) %collective-permute-start.11) | collective-permute-done | bytes 65568 | tf_op jit(solution)/shard_map/ppermute | solution.py:547
  44.3 0.9 %collective-permute-start.15 = (bf16[2,128,128]{2,1,0:T(8,128)(2,1)S(1)}, bf16[2,128,128]{2,1,0:T(8,128)(2,1)S(1)}, u32[]{:S(2)}, u32[]{:S(2)}) collective-permute-start(bf16[2,128,128]{2,1,0:T(8,128)(2,1)S(1)} %get-tuple-element.47), channel_id=1, source_target_pairs={{0,18},{1,19},{2,16},{3,17},{4,22},{5,23},{6,20},{7,21},{8,26},{9,... | collective-permute-start | bytes 196616 | tf_op jit(solution)/shard_map/ppermute | solution.py:547
  45.2 0.1 collective-permute-done.12.refs_3_
  45.3 0.9 %collective-permute-done.13.refs_5_ = bf16[2,128,128]{2,1,0:T(8,128)(2,1)S(1)} collective-permute-done((bf16[2,128,128]{2,1,0:T(8,128)(2,1)S(1)}, bf16[2,128,128]{2,1,0:T(8,128)(2,1)S(1)}, u32[]{:S(2)}, u32[]{:S(2)}) %collective-permute-start.13) | collective-permute-done | bytes 65568 | tf_op jit(solution)/shard_map/ppermute | solution.py:547
  46.2 1.3 %collective-permute-done.14.refs_6_ = bf16[2,128,128]{2,1,0:T(8,128)(2,1)S(1)} collective-permute-done((bf16[2,128,128]{2,1,0:T(8,128)(2,1)S(1)}, bf16[2,128,128]{2,1,0:T(8,128)(2,1)S(1)}, u32[]{:S(2)}, u32[]{:S(2)}) %collective-permute-start.14) | collective-permute-done | bytes 65568 | tf_op jit(solution)/shard_map/ppermute | solution.py:547
  47.5 2.0 %collective-permute-done.15.refs_7_ = bf16[2,128,128]{2,1,0:T(8,128)(2,1)S(1)} collective-permute-done((bf16[2,128,128]{2,1,0:T(8,128)(2,1)S(1)}, bf16[2,128,128]{2,1,0:T(8,128)(2,1)S(1)}, u32[]{:S(2)}, u32[]{:S(2)}) %collective-permute-start.15) | collective-permute-done | bytes 65568 | tf_op jit(solution)/shard_map/ppermute | solution.py:547
  49.5 0.1 along_line.1
  49.6 4.7 %collective-permute-start.16 = (bf16[128,128]{1,0:T(8,128)(2,1)S(1)}, bf16[128,128]{1,0:T(8,128)(2,1)S(1)}, u32[]{:S(2)}, u32[]{:S(2)}) collective-permute-start(bf16[128,128]{1,0:T(8,128)(2,1)S(1)} %get-tuple-element.49), channel_id=1, source_target_pairs={{0,4},{1,5},{2,6},{3,7},{4,0},{5,1},{6,2},{7,3},{8,12},{9,13},{10,... | collective-permute-start | bytes 98312 | tf_op jit(solution)/shard_map/ppermute | solution.py:547
  54.3 0.6 collective-permute-start.17
  54.9 1.9 %collective-permute-start.18 = (bf16[128,128]{1,0:T(8,128)(2,1)S(1)}, bf16[128,128]{1,0:T(8,128)(2,1)S(1)}, u32[]{:S(2)}, u32[]{:S(2)}) collective-permute-start(bf16[128,128]{1,0:T(8,128)(2,1)S(1)} %get-tuple-element.51), channel_id=1, source_target_pairs={{0,12},{1,13},{2,14},{3,15},{4,8},{5,9},{6,10},{7,11},{8,4},{9,5},... | collective-permute-start | bytes 98312 | tf_op jit(solution)/shard_map/ppermute | solution.py:547
  56.7 2.4 %collective-permute-done.17.refs_1_ = bf16[128,128]{1,0:T(8,128)(2,1)S(1)} collective-permute-done((bf16[128,128]{1,0:T(8,128)(2,1)S(1)}, bf16[128,128]{1,0:T(8,128)(2,1)S(1)}, u32[]{:S(2)}, u32[]{:S(2)}) %collective-permute-start.17) | collective-permute-done | bytes 32800 | tf_op jit(solution)/shard_map/ppermute | solution.py:547
  59.1 1.5 %collective-permute-done.18.refs_2_ = bf16[128,128]{1,0:T(8,128)(2,1)S(1)} collective-permute-done((bf16[128,128]{1,0:T(8,128)(2,1)S(1)}, bf16[128,128]{1,0:T(8,128)(2,1)S(1)}, u32[]{:S(2)}, u32[]{:S(2)}) %collective-permute-start.18) | collective-permute-done | bytes 32800 | tf_op jit(solution)/shard_map/ppermute | solution.py:547
  60.6 0.1 finish.1.mine_ref
  60.7 0.8 %collective-permute-start.19 = (f32[128,128]{1,0:T(8,128)S(1)}, f32[128,128]{1,0:T(8,128)S(1)}, u32[]{:S(2)}, u32[]{:S(2)}) collective-permute-start(f32[128,128]{1,0:T(8,128)S(1)} %finish.1.mine_ref), channel_id=1, source_target_pairs={{0,16},{1,17},{2,18},{3,19},{4,20},{5,21},{6,22},{7,23},{8,24},{9,... | collective-permute-start | bytes 196616 | tf_op jit(solution)/shard_map/ppermute | solution.py:547
  61.4 3.6 %collective-permute-done.19.other_ref = f32[128,128]{1,0:T(8,128)S(1)} collective-permute-done((f32[128,128]{1,0:T(8,128)S(1)}, f32[128,128]{1,0:T(8,128)S(1)}, u32[]{:S(2)}, u32[]{:S(2)}) %collective-permute-start.19) | collective-permute-done | bytes 65568 | tf_op jit(solution)/shard_map/ppermute | solution.py:547
  65.0 0.7 join.1
  65.7 1.1 %place.1 = bf16[128,4096]{1,0:T(8,128)(2,1)} custom-call(s32[1]{0:T(128)} %bitcast.me_ref, bf16[128,2048]{1,0:T(8,128)(2,1)S(1)} %get-tuple-element.38.own_ref, bf16[128,2048]{1,0:T(8,128)(2,1)S(1)} %collective-permute-done.9.got_ref), custom_call_target="tpu_custom_call" | custom-call | flops 1 | bytes 2097152 | tf_op jit(solution)/shard_map/place/pallas_call | solution.py:393
  (15 shorter events, 0.1 us)
Async XLA Ops:
  2.0 29.8 %collective-permute-start.2 = (bf16[128,2048]{1,0:T(8,128)(2,1)S(1)}, bf16[128,2048]{1,0:T(8,128)(2,1)S(1)}, u32[]{:S(2)}, u32[]{:S(2)}) collective-permute-start(bf16[128,2048]{1,0:T(8,128)(2,1)S(1)} %get-tuple-element.32), channel_id=1, source_target_pairs={{0,1},{1,0},{2,3},{3,2},{4,5},{5,4},{6,7},{7,6},{8,9},{9,8},{10,11... | collective-permute-start | bytes 1572872 | tf_op jit(solution)/shard_map/ppermute | solution.py:547
  2.6 3.5 %copy-start.3 = (bf16[256,128]{1,0:T(8,128)(2,1)S(1)}, bf16[256,128]{1,0:T(8,128)(2,1)}, u32[]{:S(2)}) copy-start(bf16[256,128]{1,0:T(8,128)(2,1)} %refs_0_.1) | copy-start | bytes 196612
  4.0 27.8 %copy-start.1 = (bf16[512,256]{1,0:T(8,128)(2,1)S(1)}, bf16[512,256]{1,0:T(8,128)(2,1)}, u32[]{:S(2)}) copy-start(bf16[512,256]{1,0:T(8,128)(2,1)} %constant.17.clone.refs_6_.wx_ref) | copy-start | bytes 786436
  4.0 27.8 %copy-start.2 = (bf16[256,256]{1,0:T(8,128)(2,1)S(1)}, bf16[256,256]{1,0:T(8,128)(2,1)}, u32[]{:S(2)}) copy-start(bf16[256,256]{1,0:T(8,128)(2,1)} %constant.18.clone.refs_7_.refs_3_) | copy-start | bytes 393220
  4.0 9.2 %collective-permute-start = (bf16[128,1024]{1,0:T(8,128)(2,1)S(1)}, bf16[128,1024]{1,0:T(8,128)(2,1)S(1)}, u32[]{:S(2)}, u32[]{:S(2)}) collective-permute-start(bf16[128,1024]{1,0:T(8,128)(2,1)S(1)} %get-tuple-element.29), channel_id=1, source_target_pairs={{0,1},{1,0},{2,3},{3,2},{4,5},{5,4},{6,7},{7,6},{8,9},{9,8},{10,11... | collective-permute-start | bytes 786440 | tf_op jit(solution)/shard_map/ppermute | solution.py:547
  5.5 11.2 %collective-permute-start.1 = (bf16[128,1024]{1,0:T(8,128)(2,1)S(1)}, bf16[128,1024]{1,0:T(8,128)(2,1)S(1)}, u32[]{:S(2)}, u32[]{:S(2)}) collective-permute-start(bf16[128,1024]{1,0:T(8,128)(2,1)S(1)} %get-tuple-element.30), channel_id=1, source_target_pairs={{0,1},{1,0},{2,3},{3,2},{4,5},{5,4},{6,7},{7,6},{8,9},{9,8},{10,11... | collective-permute-start | bytes 786440 | tf_op jit(solution)/shard_map/ppermute | solution.py:547
  6.1 5.3 %collective-permute-start.5 = (bf16[256,128]{1,0:T(8,128)(2,1)S(1)}, bf16[256,128]{1,0:T(8,128)(2,1)S(1)}, u32[]{:S(2)}, u32[]{:S(2)}) collective-permute-start(bf16[256,128]{1,0:T(8,128)(2,1)S(1)} %copy-done.3), channel_id=1, source_target_pairs={{0,2},{1,3},{2,0},{3,1},{4,6},{5,7},{6,4},{7,5},{8,10},{9,11},{10,... | collective-permute-start | bytes 196616 | tf_op jit(solution)/shard_map/ppermute | solution.py:547
  11.3 7.3 %collective-permute-start.6 = (bf16[2,256,128]{2,1,0:T(8,128)(2,1)S(1)}, bf16[2,256,128]{2,1,0:T(8,128)(2,1)S(1)}, u32[]{:S(2)}, u32[]{:S(2)}) collective-permute-start(bf16[2,256,128]{2,1,0:T(8,128)(2,1)S(1)} %collect.2.refs_0_), channel_id=1, source_target_pairs={{0,4},{1,5},{2,6},{3,7},{4,0},{5,1},{6,2},{7,3},{8,12},{9,13},{10,... | collective-permute-start | bytes 393224 | tf_op jit(solution)/shard_map/ppermute | solution.py:547
  13.3 20.1 %collective-permute-start.3 = (bf16[128,1024]{1,0:T(8,128)(2,1)S(1)}, bf16[128,1024]{1,0:T(8,128)(2,1)S(1)}, u32[]{:S(2)}, u32[]{:S(2)}) collective-permute-start(bf16[128,1024]{1,0:T(8,128)(2,1)S(1)} %head.2), channel_id=1, source_target_pairs={{0,14},{1,15},{2,0},{3,1},{4,2},{5,3},{6,4},{7,5},{8,6},{9,7},{10,... | collective-permute-start | bytes 786440 | tf_op jit(solution)/shard_map/ppermute | solution.py:564
  16.7 15.0 %collective-permute-start.7 = (bf16[2,256,128]{2,1,0:T(8,128)(2,1)S(1)}, bf16[2,256,128]{2,1,0:T(8,128)(2,1)S(1)}, u32[]{:S(2)}, u32[]{:S(2)}) collective-permute-start(bf16[2,256,128]{2,1,0:T(8,128)(2,1)S(1)} %collect.2.refs_0_), channel_id=1, source_target_pairs={{0,8},{1,9},{2,10},{3,11},{4,12},{5,13},{6,14},{7,15},{8,0},{9,1},... | collective-permute-start | bytes 393224 | tf_op jit(solution)/shard_map/ppermute | solution.py:547
  16.7 15.0 %collective-permute-start.8 = (bf16[2,256,128]{2,1,0:T(8,128)(2,1)S(1)}, bf16[2,256,128]{2,1,0:T(8,128)(2,1)S(1)}, u32[]{:S(2)}, u32[]{:S(2)}) collective-permute-start(bf16[2,256,128]{2,1,0:T(8,128)(2,1)S(1)} %collect.2.refs_0_), channel_id=1, source_target_pairs={{0,12},{1,13},{2,14},{3,15},{4,8},{5,9},{6,10},{7,11},{8,4},{9,5},... | collective-permute-start | bytes 393224 | tf_op jit(solution)/shard_map/ppermute | solution.py:547
  18.7 15.7 %collective-permute-start.4 = (bf16[128,1024]{1,0:T(8,128)(2,1)S(1)}, bf16[128,1024]{1,0:T(8,128)(2,1)S(1)}, u32[]{:S(2)}, u32[]{:S(2)}) collective-permute-start(bf16[128,1024]{1,0:T(8,128)(2,1)S(1)} %head.3), channel_id=1, source_target_pairs={{2,0},{3,1},{4,2},{5,3},{6,4},{7,5},{8,6},{9,7},{10,8},{11,9},{12,... | collective-permute-start | bytes 786440 | tf_op jit(solution)/shard_map/ppermute | solution.py:564
  31.8 1.5 %copy-start = (bf16[256,256]{1,0:T(8,128)(2,1)S(1)}, bf16[256,256]{1,0:T(8,128)(2,1)}, u32[]{:S(2)}) copy-start(bf16[256,256]{1,0:T(8,128)(2,1)} %constant.19.clone.wi_ref.refs_4_) | copy-start | bytes 393220
  37.7 28.0 %collective-permute-start.9 = (bf16[128,2048]{1,0:T(8,128)(2,1)S(1)}, bf16[128,2048]{1,0:T(8,128)(2,1)S(1)}, u32[]{:S(2)}, u32[]{:S(2)}) collective-permute-start(bf16[128,2048]{1,0:T(8,128)(2,1)S(1)} %get-tuple-element.39), channel_id=1, source_target_pairs={{0,1},{1,0},{2,3},{3,2},{4,5},{5,4},{6,7},{7,6},{8,9},{9,8},{10,11... | collective-permute-start | bytes 1572872 | tf_op jit(solution)/shard_map/ppermute | solution.py:547
  37.8 5.0 %collective-permute-start.10 = (bf16[2,128,128]{2,1,0:T(8,128)(2,1)S(1)}, bf16[2,128,128]{2,1,0:T(8,128)(2,1)S(1)}, u32[]{:S(2)}, u32[]{:S(2)}) collective-permute-start(bf16[2,128,128]{2,1,0:T(8,128)(2,1)S(1)} %get-tuple-element.41), channel_id=1, source_target_pairs={{0,16},{1,17},{2,18},{3,19},{4,20},{5,21},{6,22},{7,23},{8,24},{9,... | collective-permute-start | bytes 196616 | tf_op jit(solution)/shard_map/ppermute | solution.py:547
  39.3 5.0 %collective-permute-start.11 = (bf16[2,128,128]{2,1,0:T(8,128)(2,1)S(1)}, bf16[2,128,128]{2,1,0:T(8,128)(2,1)S(1)}, u32[]{:S(2)}, u32[]{:S(2)}) collective-permute-start(bf16[2,128,128]{2,1,0:T(8,128)(2,1)S(1)} %get-tuple-element.42), channel_id=1, source_target_pairs={{0,2},{1,3},{2,0},{3,1},{4,6},{5,7},{6,4},{7,5},{8,10},{9,11},{10,... | collective-permute-start | bytes 196616 | tf_op jit(solution)/shard_map/ppermute | solution.py:547
  39.9 5.5 %collective-permute-start.12 = (bf16[2,128,128]{2,1,0:T(8,128)(2,1)S(1)}, bf16[2,128,128]{2,1,0:T(8,128)(2,1)S(1)}, u32[]{:S(2)}, u32[]{:S(2)}) collective-permute-start(bf16[2,128,128]{2,1,0:T(8,128)(2,1)S(1)} %get-tuple-element.43), channel_id=1, source_target_pairs={{0,18},{1,19},{2,16},{3,17},{4,22},{5,23},{6,20},{7,21},{8,26},{9,... | collective-permute-start | bytes 196616 | tf_op jit(solution)/shard_map/ppermute | solution.py:547
  41.3 4.9 %collective-permute-start.13 = (bf16[2,128,128]{2,1,0:T(8,128)(2,1)S(1)}, bf16[2,128,128]{2,1,0:T(8,128)(2,1)S(1)}, u32[]{:S(2)}, u32[]{:S(2)}) collective-permute-start(bf16[2,128,128]{2,1,0:T(8,128)(2,1)S(1)} %get-tuple-element.45), channel_id=1, source_target_pairs={{0,16},{1,17},{2,18},{3,19},{4,20},{5,21},{6,22},{7,23},{8,24},{9,... | collective-permute-start | bytes 196616 | tf_op jit(solution)/shard_map/ppermute | solution.py:547
  42.8 4.7 %collective-permute-start.14 = (bf16[2,128,128]{2,1,0:T(8,128)(2,1)S(1)}, bf16[2,128,128]{2,1,0:T(8,128)(2,1)S(1)}, u32[]{:S(2)}, u32[]{:S(2)}) collective-permute-start(bf16[2,128,128]{2,1,0:T(8,128)(2,1)S(1)} %get-tuple-element.46), channel_id=1, source_target_pairs={{0,2},{1,3},{2,0},{3,1},{4,6},{5,7},{6,4},{7,5},{8,10},{9,11},{10,... | collective-permute-start | bytes 196616 | tf_op jit(solution)/shard_map/ppermute | solution.py:547
  44.3 5.2 %collective-permute-start.15 = (bf16[2,128,128]{2,1,0:T(8,128)(2,1)S(1)}, bf16[2,128,128]{2,1,0:T(8,128)(2,1)S(1)}, u32[]{:S(2)}, u32[]{:S(2)}) collective-permute-start(bf16[2,128,128]{2,1,0:T(8,128)(2,1)S(1)} %get-tuple-element.47), channel_id=1, source_target_pairs={{0,18},{1,19},{2,16},{3,17},{4,22},{5,23},{6,20},{7,21},{8,26},{9,... | collective-permute-start | bytes 196616 | tf_op jit(solution)/shard_map/ppermute | solution.py:547
  49.6 7.2 %collective-permute-start.16 = (bf16[128,128]{1,0:T(8,128)(2,1)S(1)}, bf16[128,128]{1,0:T(8,128)(2,1)S(1)}, u32[]{:S(2)}, u32[]{:S(2)}) collective-permute-start(bf16[128,128]{1,0:T(8,128)(2,1)S(1)} %get-tuple-element.49), channel_id=1, source_target_pairs={{0,4},{1,5},{2,6},{3,7},{4,0},{5,1},{6,2},{7,3},{8,12},{9,13},{10,... | collective-permute-start | bytes 98312 | tf_op jit(solution)/shard_map/ppermute | solution.py:547
  54.3 4.8 %collective-permute-start.17 = (bf16[128,128]{1,0:T(8,128)(2,1)S(1)}, bf16[128,128]{1,0:T(8,128)(2,1)S(1)}, u32[]{:S(2)}, u32[]{:S(2)}) collective-permute-start(bf16[128,128]{1,0:T(8,128)(2,1)S(1)} %get-tuple-element.50), channel_id=1, source_target_pairs={{0,8},{1,9},{2,10},{3,11},{4,12},{5,13},{6,14},{7,15},{8,0},{9,1},... | collective-permute-start | bytes 98312 | tf_op jit(solution)/shard_map/ppermute | solution.py:547
  54.9 5.7 %collective-permute-start.18 = (bf16[128,128]{1,0:T(8,128)(2,1)S(1)}, bf16[128,128]{1,0:T(8,128)(2,1)S(1)}, u32[]{:S(2)}, u32[]{:S(2)}) collective-permute-start(bf16[128,128]{1,0:T(8,128)(2,1)S(1)} %get-tuple-element.51), channel_id=1, source_target_pairs={{0,12},{1,13},{2,14},{3,15},{4,8},{5,9},{6,10},{7,11},{8,4},{9,5},... | collective-permute-start | bytes 98312 | tf_op jit(solution)/shard_map/ppermute | solution.py:547
  60.7 4.3 %collective-permute-start.19 = (f32[128,128]{1,0:T(8,128)S(1)}, f32[128,128]{1,0:T(8,128)S(1)}, u32[]{:S(2)}, u32[]{:S(2)}) collective-permute-start(f32[128,128]{1,0:T(8,128)S(1)} %finish.1.mine_ref), channel_id=1, source_target_pairs={{0,16},{1,17},{2,18},{3,19},{4,20},{5,21},{6,22},{7,23},{8,24},{9,... | collective-permute-start | bytes 196616 | tf_op jit(solution)/shard_map/ppermute | solution.py:547

commit v8 on v7

--- a/solution.py
+++ b/solution.py
@@ -200,56 +200,34 @@
     )(me, own, got)
 
 
-def split_kernel(shard, me_ref, src_hbm, own_ref, other_ref, sems):
-    core = me_ref[0] // 2 % 2
-    copies = []
-    for n, (parity, ref) in enumerate(((core, own_ref), (1 - core, other_ref))):
-        for at in range(0, own_ref.shape[1], shard):
-            cols = pl.ds(pl.multiple_of(2 * at + parity * shard, shard), shard)
-            copy = pltpu.make_async_copy(
-                src_hbm.at[:, cols], ref.at[:, pl.ds(at, shard)], sems.at[n, at // shard]
-            )
-            copy.start()
-            copies.append(copy)
-    for copy in copies:
-        copy.wait()
-
-
-def split(me, values, shard):
-    positions, channels = values.shape
-    half = jax.ShapeDtypeStruct((positions, channels // 2), values.dtype)
-    return pl.pallas_call(
-        functools.partial(split_kernel, shard),
-        in_specs=[SMEM_SPEC, HBM_SPEC],
-        out_specs=[VMEM_SPEC] * 2,
-        out_shape=[half] * 2,
-        scratch_shapes=[pltpu.SemaphoreType.DMA((2, channels // 2 // shard))],
-        compiler_params=params(8),
-        cost_estimate=cost(1, 4 * positions * channels),
-        name="split",
-    )(me, pltpu.with_memory_space_constraint(values, pltpu.HBM))
-
-
-def near_window_kernel(
-    pieces, me_ref, *refs
-):
+def near_window_kernel(pieces, shard, me_ref, *refs):
     owns, gots = refs[:pieces], refs[pieces : 2 * pieces]
     val_ref, val_got_ref, wx_ref, wv_ref, x_ref, product_ref, v_ref = refs[2 * pieces :]
-    core0 = me_ref[0] // 2 % 2 == 0
+    core = me_ref[0] // 2 % 2
+    core0 = core == 0
     own, got = (jnp.concatenate([ref[...] for ref in refs], axis=1) for refs in (owns, gots))
     x = spectrum_of_window(wx_ref[...], jnp.where(core0, own, got), jnp.where(core0, got, own))
     x_ref[...] = x
-    own, got = val_ref[...], val_got_ref[...]
+    own, got = (
+        jnp.concatenate(
+            [
+                ref[:, pl.ds(pl.multiple_of(at + core * shard, shard), shard)]
+                for at in range(0, ref.shape[1], 2 * shard)
+            ],
+            axis=1,
+        )
+        for ref in (val_ref, val_got_ref)
+    )
     v_ref[...] = spectrum_of_values(wv_ref[...], jnp.where(core0, got, own))
     product_ref[...] = cross(x, spectrum_of_values(wv_ref[...], jnp.where(core0, own, got)))
 
 
-def near_window(me, own, got, values, values_got, taps):
-    positions, width = values.shape
+def near_window(me, own, got, values, values_got, shard, taps):
+    positions, width = values.shape[0], values.shape[1] // 2
     wx, wv, _, _, _ = transforms(positions, taps)
     spectrum = jax.ShapeDtypeStruct((wx.shape[1], width), F32)
     return pl.pallas_call(
-        functools.partial(near_window_kernel, len(own)),
+        functools.partial(near_window_kernel, len(own), shard),
         in_specs=[SMEM_SPEC] + [VMEM_SPEC] * (2 * len(own) + 4),
         out_specs=[VMEM_SPEC] * 3,
         out_shape=[spectrum] * 3,
@@ -562,9 +540,10 @@
     for i in range(pieces):
         first = head(me, own[i], got[i])
         afters.append(lax.ppermute(first, AXES, back_open if i else back))
-    values, other = split(me, gated_values, shard)
-    values_got = swap(other, 1)
-    near, product, v = near_window(me, own, got, values, values_got, taps)
+    values_got = swap(gated_values, 1)
+    near, product, v = near_window(
+        me, own, got, gated_values, values_got, shard, taps
+    )
 
     sums, far = [], []
     for i in range(pieces):

time: 67.1 us -> 65.6 us (0.978)
  Pallas kernels: 12.1 us -> 10.7 us
    pallas_call x2 -> x1, Pallas kernels: 2.88 us -> 1.48 us  [near_window(): pl.pallas_call(functools.partial(near_window_kernel, len(own), shard), in...]
  transfers between devices with their start and end apart: 20 -> 20, of which waited for: 10 -> 10; matrix products, arithmetic and copies ran while one was open for 0% -> 0% of each run, Pallas kernels for 9% -> 10%
where the time goes in v8:
time: 65.6 us; the launch traced here: 65.4 us
  waiting for transfers between devices  27.1 us (41%)
  starting transfers between devices  26.7 us (41%)
  Pallas kernels  10.7 us (16%)
  between operations  0.85 us (1%)
    ppermute x18, waiting for transfers between devices, swap(): return lax.ppermute(x, AXES, [(i, i ^ bits) for i in range(devices)])  27.1 us
    ppermute x18, starting transfers between devices, swap(): return lax.ppermute(x, AXES, [(i, i ^ bits) for i in range(devices)])  21.9 us
    ppermute x2, starting transfers between devices, body(): afters.append(lax.ppermute(first, AXES, back_open if i else back))  4.78 us
    pallas_call x2, Pallas kernels, cotangent_pair(): pl.pallas_call(functools.partial(cotangent_pair_kernel, piece, cuts, shar...  2.86 us
    pallas_call x1, Pallas kernels, value_grad_pair(): pl.pallas_call(functools.partial(value_grad_kernel, len(far)), in_specs=[...  2.27 us
    pallas_call x2, Pallas kernels, tap_grad(): pl.pallas_call(functools.partial(tap_grad_kernel, piece, last_chip), in_s...  2.07 us
    pallas_call x1, Pallas kernels, near_window(): pl.pallas_call(functools.partial(near_window_kernel, len(own), shard), in...  1.48 us
  transfers between devices with their start and end apart: 20, of which 10 were waited for; matrix products, arithmetic and copies ran while one was open for 0% of the time, Pallas kernels for 10%

profile of v8, /device:TPU:0, one launch (start us, length us, event | category | flops | bytes accessed | tf_op | source)
XLA Modules:
  0.0 65.4 jit_solution(4761029116764382557)
XLA Ops:
  0.6 0.6 collective-permute-start.2
  1.2 1.4 %cotangent_pair.2 = (bf16[128,1024]{1,0:T(8,128)(2,1)S(1)}, bf16[128,1024]{1,0:T(8,128)(2,1)S(1)}) custom-call(s32[1]{0:T(128)} %bitcast.me_ref, s32[1,128]{1,0:T(1,128)} %ids_hbm.3, bf16[128,4096]{1,0:T(8,128)(2,1)} %bitcast.7, bf16[128,4096]{1,0:T(8,128)(2,1)} %bitcast.9), custom_call_target="tpu_custom_call" | custom-call | flops 524288 | bytes 1572864 | tf_op jit(solution)/shard_map/cotangent_pair/pallas_call | solution.py:173
  2.6 0.0 copy-start.1
  2.6 0.0 copy-start.2
  2.6 0.0 copy-start.4
  2.6 0.1 collective-permute-start
  2.7 1.5 %cotangent_pair.3 = (bf16[128,1024]{1,0:T(8,128)(2,1)S(1)}, bf16[128,1024]{1,0:T(8,128)(2,1)S(1)}) custom-call(s32[1]{0:T(128)} %bitcast.me_ref, s32[1,128]{1,0:T(1,128)} %ids_hbm.3, bf16[128,4096]{1,0:T(8,128)(2,1)} %bitcast.8, bf16[128,4096]{1,0:T(8,128)(2,1)} %bitcast.10), custom_call_target="tpu_custom_call" | custom-call | flops 524288 | bytes 1572864 | tf_op jit(solution)/shard_map/cotangent_pair/pallas_call | solution.py:173
  4.2 0.5 collective-permute-start.1
  4.7 2.6 %collective-permute-start.5 = (bf16[256,128]{1,0:T(8,128)(2,1)S(1)}, bf16[256,128]{1,0:T(8,128)(2,1)S(1)}, u32[]{:S(2)}, u32[]{:S(2)}) collective-permute-start(bf16[256,128]{1,0:T(8,128)(2,1)S(1)} %copy-done.3), channel_id=1, source_target_pairs={{0,2},{1,3},{2,0},{3,1},{4,6},{5,7},{6,4},{7,5},{8,10},{9,11},{10,... | collective-permute-start | bytes 196616 | tf_op jit(solution)/shard_map/ppermute | solution.py:525
  7.3 2.6 %collective-permute-done.5.refs_1_ = bf16[256,128]{1,0:T(8,128)(2,1)S(1)} collective-permute-done((bf16[256,128]{1,0:T(8,128)(2,1)S(1)}, bf16[256,128]{1,0:T(8,128)(2,1)S(1)}, u32[]{:S(2)}, u32[]{:S(2)}) %collective-permute-start.5) | collective-permute-done | bytes 65568 | tf_op jit(solution)/shard_map/ppermute | solution.py:525
  9.9 1.9 %collective-permute-start.6 = (bf16[2,256,128]{2,1,0:T(8,128)(2,1)S(1)}, bf16[2,256,128]{2,1,0:T(8,128)(2,1)S(1)}, u32[]{:S(2)}, u32[]{:S(2)}) collective-permute-start(bf16[2,256,128]{2,1,0:T(8,128)(2,1)S(1)} %collect.2.refs_0_), channel_id=1, source_target_pairs={{0,4},{1,5},{2,6},{3,7},{4,0},{5,1},{6,2},{7,3},{8,12},{9,13},{10,... | collective-permute-start | bytes 393224 | tf_op jit(solution)/shard_map/ppermute | solution.py:525
  11.8 0.0 collective-permute-done.refs_2_.got_ref
  11.8 3.5 %collective-permute-start.3 = (bf16[128,1024]{1,0:T(8,128)(2,1)S(1)}, bf16[128,1024]{1,0:T(8,128)(2,1)S(1)}, u32[]{:S(2)}, u32[]{:S(2)}) collective-permute-start(bf16[128,1024]{1,0:T(8,128)(2,1)S(1)} %head.2), channel_id=1, source_target_pairs={{0,14},{1,15},{2,0},{3,1},{4,2},{5,3},{6,4},{7,5},{8,6},{9,7},{10,... | collective-permute-start | bytes 786440 | tf_op jit(solution)/shard_map/ppermute | solution.py:542
  15.3 0.0 collective-permute-start.7
  15.3 0.0 collective-permute-done.1.refs_3_.got_ref
  15.3 1.9 %collective-permute-start.8 = (bf16[2,256,128]{2,1,0:T(8,128)(2,1)S(1)}, bf16[2,256,128]{2,1,0:T(8,128)(2,1)S(1)}, u32[]{:S(2)}, u32[]{:S(2)}) collective-permute-start(bf16[2,256,128]{2,1,0:T(8,128)(2,1)S(1)} %collect.2.refs_0_), channel_id=1, source_target_pairs={{0,12},{1,13},{2,14},{3,15},{4,8},{5,9},{6,10},{7,11},{8,4},{9,5},... | collective-permute-start | bytes 393224 | tf_op jit(solution)/shard_map/ppermute | solution.py:525
  17.3 0.0 collective-permute-done.6.refs_1_
  17.3 1.3 %collective-permute-start.4 = (bf16[128,1024]{1,0:T(8,128)(2,1)S(1)}, bf16[128,1024]{1,0:T(8,128)(2,1)S(1)}, u32[]{:S(2)}, u32[]{:S(2)}) collective-permute-start(bf16[128,1024]{1,0:T(8,128)(2,1)S(1)} %head.3), channel_id=1, source_target_pairs={{2,0},{3,1},{4,2},{5,3},{6,4},{7,5},{8,6},{9,7},{10,8},{11,9},{12,... | collective-permute-start | bytes 786440 | tf_op jit(solution)/shard_map/ppermute | solution.py:542
  18.6 11.8 %collective-permute-done.7.refs_2_ = bf16[2,256,128]{2,1,0:T(8,128)(2,1)S(1)} collective-permute-done((bf16[2,256,128]{2,1,0:T(8,128)(2,1)S(1)}, bf16[2,256,128]{2,1,0:T(8,128)(2,1)S(1)}, u32[]{:S(2)}, u32[]{:S(2)}) %collective-permute-start.7) | collective-permute-done | bytes 131104 | tf_op jit(solution)/shard_map/ppermute | solution.py:525
  30.4 0.0 collective-permute-done.8.refs_3_
  30.4 0.0 copy-start
  30.4 1.5 %near_window.1 = (f32[256,2048]{1,0:T(8,128)S(1)}, f32[256,2048]{1,0:T(8,128)S(1)}, f32[256,2048]{1,0:T(8,128)S(1)}) custom-call(s32[1]{0:T(128)} %bitcast.me_ref, bf16[128,1024]{1,0:T(8,128)(2,1)S(1)} %get-tuple-element.25.refs_0_.own_ref, bf16[128,1024]{1,0:T(8,128)(2,1)S(1)} %get-tuple-element.26.refs_1_.own_ref, ...), custom_call_target="tpu_custom_call" | custom-call | flops 1073741824 | bytes 8388608 | tf_op jit(solution)/shard_map/near_window/pallas_call | solution.py:229
  32.0 1.0 %tap_grad.2 = (f32[2,128,128]{2,1,0:T(8,128)S(1)}, bf16[2,128,128]{2,1,0:T(8,128)(2,1)S(1)}, bf16[2,128,128]{2,1,0:T(8,128)(2,1)S(1)}, bf16[2,128,128]{2,1,0:T(8,128)(2,1)S(1)}, f32[256,1024]{1,0:T(8,128)S(1)}) custom-call(s32[1]{0:T(128)} %bitcast.me_ref, bf16[128,1024]{1,0:T(8,128)(2,1)S(1)} %get-tuple-element.25.refs_0_.own_ref, ...), custom_call_target="tpu_custom_call" | custom-call | flops 469762048 | bytes 3145728 | tf_op jit(solution)/shard_map/tap_grad/pallas_call | solution.py:266
  33.0 1.0 %tap_grad.3 = (f32[2,128,128]{2,1,0:T(8,128)S(1)}, bf16[2,128,128]{2,1,0:T(8,128)(2,1)S(1)}, bf16[2,128,128]{2,1,0:T(8,128)(2,1)S(1)}, bf16[2,128,128]{2,1,0:T(8,128)(2,1)S(1)}, f32[256,1024]{1,0:T(8,128)S(1)}) custom-call(s32[1]{0:T(128)} %bitcast.me_ref, bf16[128,1024]{1,0:T(8,128)(2,1)S(1)} %get-tuple-element.26.refs_1_.own_ref, ...), custom_call_target="tpu_custom_call" | custom-call | flops 469762048 | bytes 3145728 | tf_op jit(solution)/shard_map/tap_grad/pallas_call | solution.py:266
  34.1 2.3 %value_grad_pair.1 = (bf16[128,2048]{1,0:T(8,128)(2,1)S(1)}, bf16[128,2048]{1,0:T(8,128)(2,1)S(1)}) custom-call(s32[1]{0:T(128)} %bitcast.me_ref, f32[256,2048]{1,0:T(8,128)S(1)} %get-tuple-element.29.x_ref, f32[256,1024]{1,0:T(8,128)S(1)} %get-tuple-element.32.refs_0_, f32[256,1024]{1,0:T(8,128)S(1)} %get-tuple-element.33.refs_1_, ...), custom_call_target="tpu_custom_call" | custom-call | flops 1073741824 | bytes 6291456 | tf_op jit(solution)/shard_map/value_grad_pair/pallas_call | solution.py:461
  36.3 0.1 collective-permute-start.9
  36.4 1.6 %collective-permute-start.10 = (bf16[2,128,128]{2,1,0:T(8,128)(2,1)S(1)}, bf16[2,128,128]{2,1,0:T(8,128)(2,1)S(1)}, u32[]{:S(2)}, u32[]{:S(2)}) collective-permute-start(bf16[2,128,128]{2,1,0:T(8,128)(2,1)S(1)} %get-tuple-element.37), channel_id=1, source_target_pairs={{0,16},{1,17},{2,18},{3,19},{4,20},{5,21},{6,22},{7,23},{8,24},{9,... | collective-permute-start | bytes 196616 | tf_op jit(solution)/shard_map/ppermute | solution.py:525
  38.0 0.5 collective-permute-start.11
  38.5 1.5 %collective-permute-start.12 = (bf16[2,128,128]{2,1,0:T(8,128)(2,1)S(1)}, bf16[2,128,128]{2,1,0:T(8,128)(2,1)S(1)}, u32[]{:S(2)}, u32[]{:S(2)}) collective-permute-start(bf16[2,128,128]{2,1,0:T(8,128)(2,1)S(1)} %get-tuple-element.39), channel_id=1, source_target_pairs={{0,18},{1,19},{2,16},{3,17},{4,22},{5,23},{6,20},{7,21},{8,26},{9,... | collective-permute-start | bytes 196616 | tf_op jit(solution)/shard_map/ppermute | solution.py:525
  40.0 1.5 %collective-permute-start.13 = (bf16[2,128,128]{2,1,0:T(8,128)(2,1)S(1)}, bf16[2,128,128]{2,1,0:T(8,128)(2,1)S(1)}, u32[]{:S(2)}, u32[]{:S(2)}) collective-permute-start(bf16[2,128,128]{2,1,0:T(8,128)(2,1)S(1)} %get-tuple-element.41), channel_id=1, source_target_pairs={{0,16},{1,17},{2,18},{3,19},{4,20},{5,21},{6,22},{7,23},{8,24},{9,... | collective-permute-start | bytes 196616 | tf_op jit(solution)/shard_map/ppermute | solution.py:525
  41.5 0.5 collective-permute-start.14
  42.0 1.0 %collective-permute-done.11.refs_2_ = bf16[2,128,128]{2,1,0:T(8,128)(2,1)S(1)} collective-permute-done((bf16[2,128,128]{2,1,0:T(8,128)(2,1)S(1)}, bf16[2,128,128]{2,1,0:T(8,128)(2,1)S(1)}, u32[]{:S(2)}, u32[]{:S(2)}) %collective-permute-start.11) | collective-permute-done | bytes 65568 | tf_op jit(solution)/shard_map/ppermute | solution.py:525
  42.9 0.9 %collective-permute-start.15 = (bf16[2,128,128]{2,1,0:T(8,128)(2,1)S(1)}, bf16[2,128,128]{2,1,0:T(8,128)(2,1)S(1)}, u32[]{:S(2)}, u32[]{:S(2)}) collective-permute-start(bf16[2,128,128]{2,1,0:T(8,128)(2,1)S(1)} %get-tuple-element.43), channel_id=1, source_target_pairs={{0,18},{1,19},{2,16},{3,17},{4,22},{5,23},{6,20},{7,21},{8,26},{9,... | collective-permute-start | bytes 196616 | tf_op jit(solution)/shard_map/ppermute | solution.py:525
  43.9 0.1 collective-permute-done.12.refs_3_
  43.9 0.9 %collective-permute-done.13.refs_5_ = bf16[2,128,128]{2,1,0:T(8,128)(2,1)S(1)} collective-permute-done((bf16[2,128,128]{2,1,0:T(8,128)(2,1)S(1)}, bf16[2,128,128]{2,1,0:T(8,128)(2,1)S(1)}, u32[]{:S(2)}, u32[]{:S(2)}) %collective-permute-start.13) | collective-permute-done | bytes 65568 | tf_op jit(solution)/shard_map/ppermute | solution.py:525
  44.9 1.3 %collective-permute-done.14.refs_6_ = bf16[2,128,128]{2,1,0:T(8,128)(2,1)S(1)} collective-permute-done((bf16[2,128,128]{2,1,0:T(8,128)(2,1)S(1)}, bf16[2,128,128]{2,1,0:T(8,128)(2,1)S(1)}, u32[]{:S(2)}, u32[]{:S(2)}) %collective-permute-start.14) | collective-permute-done | bytes 65568 | tf_op jit(solution)/shard_map/ppermute | solution.py:525
  46.1 2.0 %collective-permute-done.15.refs_7_ = bf16[2,128,128]{2,1,0:T(8,128)(2,1)S(1)} collective-permute-done((bf16[2,128,128]{2,1,0:T(8,128)(2,1)S(1)}, bf16[2,128,128]{2,1,0:T(8,128)(2,1)S(1)}, u32[]{:S(2)}, u32[]{:S(2)}) %collective-permute-start.15) | collective-permute-done | bytes 65568 | tf_op jit(solution)/shard_map/ppermute | solution.py:525
  48.1 0.1 along_line.1
  48.2 4.7 %collective-permute-start.16 = (bf16[128,128]{1,0:T(8,128)(2,1)S(1)}, bf16[128,128]{1,0:T(8,128)(2,1)S(1)}, u32[]{:S(2)}, u32[]{:S(2)}) collective-permute-start(bf16[128,128]{1,0:T(8,128)(2,1)S(1)} %get-tuple-element.45), channel_id=1, source_target_pairs={{0,4},{1,5},{2,6},{3,7},{4,0},{5,1},{6,2},{7,3},{8,12},{9,13},{10,... | collective-permute-start | bytes 98312 | tf_op jit(solution)/shard_map/ppermute | solution.py:525
  52.8 0.6 collective-permute-start.17
  53.5 1.8 %collective-permute-start.18 = (bf16[128,128]{1,0:T(8,128)(2,1)S(1)}, bf16[128,128]{1,0:T(8,128)(2,1)S(1)}, u32[]{:S(2)}, u32[]{:S(2)}) collective-permute-start(bf16[128,128]{1,0:T(8,128)(2,1)S(1)} %get-tuple-element.47), channel_id=1, source_target_pairs={{0,12},{1,13},{2,14},{3,15},{4,8},{5,9},{6,10},{7,11},{8,4},{9,5},... | collective-permute-start | bytes 98312 | tf_op jit(solution)/shard_map/ppermute | solution.py:525
  55.3 2.4 %collective-permute-done.17.refs_1_ = bf16[128,128]{1,0:T(8,128)(2,1)S(1)} collective-permute-done((bf16[128,128]{1,0:T(8,128)(2,1)S(1)}, bf16[128,128]{1,0:T(8,128)(2,1)S(1)}, u32[]{:S(2)}, u32[]{:S(2)}) %collective-permute-start.17) | collective-permute-done | bytes 32800 | tf_op jit(solution)/shard_map/ppermute | solution.py:525
  57.7 1.5 %collective-permute-done.18.refs_2_ = bf16[128,128]{1,0:T(8,128)(2,1)S(1)} collective-permute-done((bf16[128,128]{1,0:T(8,128)(2,1)S(1)}, bf16[128,128]{1,0:T(8,128)(2,1)S(1)}, u32[]{:S(2)}, u32[]{:S(2)}) %collective-permute-start.18) | collective-permute-done | bytes 32800 | tf_op jit(solution)/shard_map/ppermute | solution.py:525
  59.2 0.1 finish.1.mine_ref
  59.3 0.7 %collective-permute-start.19 = (f32[128,128]{1,0:T(8,128)S(1)}, f32[128,128]{1,0:T(8,128)S(1)}, u32[]{:S(2)}, u32[]{:S(2)}) collective-permute-start(f32[128,128]{1,0:T(8,128)S(1)} %finish.1.mine_ref), channel_id=1, source_target_pairs={{0,16},{1,17},{2,18},{3,19},{4,20},{5,21},{6,22},{7,23},{8,24},{9,... | collective-permute-start | bytes 196616 | tf_op jit(solution)/shard_map/ppermute | solution.py:525
  60.0 3.6 %collective-permute-done.19.other_ref = f32[128,128]{1,0:T(8,128)S(1)} collective-permute-done((f32[128,128]{1,0:T(8,128)S(1)}, f32[128,128]{1,0:T(8,128)S(1)}, u32[]{:S(2)}, u32[]{:S(2)}) %collective-permute-start.19) | collective-permute-done | bytes 65568 | tf_op jit(solution)/shard_map/ppermute | solution.py:525
  63.6 0.7 %join.1 = f32[256,128]{1,0:T(8,128)} custom-call(s32[1]{0:T(128)} %bitcast.me_ref, f32[128,128]{1,0:T(8,128)S(1)} %finish.1.mine_ref, f32[128,128]{1,0:T(8,128)S(1)} %collective-permute-done.19.other_ref), custom_call_target="tpu_custom_call" | custom-call | flops 1 | bytes 262144 | tf_op jit(solution)/shard_map/join/pallas_call | solution.py:397
  64.3 1.1 %place.1 = bf16[128,4096]{1,0:T(8,128)(2,1)} custom-call(s32[1]{0:T(128)} %bitcast.me_ref, bf16[128,2048]{1,0:T(8,128)(2,1)S(1)} %get-tuple-element.34.own_ref, bf16[128,2048]{1,0:T(8,128)(2,1)S(1)} %collective-permute-done.9.got_ref), custom_call_target="tpu_custom_call" | custom-call | flops 1 | bytes 2097152 | tf_op jit(solution)/shard_map/place/pallas_call | solution.py:371
  (16 shorter events, 0.1 us)
Async XLA Ops:
  0.6 29.8 %collective-permute-start.2 = (bf16[128,4096]{1,0:T(8,128)(2,1)}, bf16[128,4096]{1,0:T(8,128)(2,1)S(1)}, u32[]{:S(2)}, u32[]{:S(2)}) collective-permute-start(bf16[128,4096]{1,0:T(8,128)(2,1)} %bitcast.5), channel_id=1, source_target_pairs={{0,1},{1,0},{2,3},{3,2},{4,5},{5,4},{6,7},{7,6},{8,9},{9,8},{10,11... | collective-permute-start | bytes 3145736 | tf_op jit(solution)/shard_map/ppermute | solution.py:525
  1.2 3.5 %copy-start.3 = (bf16[256,128]{1,0:T(8,128)(2,1)S(1)}, bf16[256,128]{1,0:T(8,128)(2,1)}, u32[]{:S(2)}) copy-start(bf16[256,128]{1,0:T(8,128)(2,1)} %refs_0_.1) | copy-start | bytes 196612
  2.6 27.8 %copy-start.1 = (bf16[512,256]{1,0:T(8,128)(2,1)S(1)}, bf16[512,256]{1,0:T(8,128)(2,1)}, u32[]{:S(2)}) copy-start(bf16[512,256]{1,0:T(8,128)(2,1)} %constant.17.clone.refs_6_.wx_ref) | copy-start | bytes 786436
  2.6 27.8 %copy-start.2 = (bf16[256,256]{1,0:T(8,128)(2,1)S(1)}, bf16[256,256]{1,0:T(8,128)(2,1)}, u32[]{:S(2)}) copy-start(bf16[256,256]{1,0:T(8,128)(2,1)} %constant.18.clone.refs_7_.refs_3_) | copy-start | bytes 393220
  2.6 27.8 %copy-start.4 = (bf16[1,128,4096]{2,1,0:T(8,128)(2,1)S(1)}, bf16[1,128,4096]{2,1,0:T(8,128)(2,1)}, u32[]{:S(2)}) copy-start(bf16[1,128,4096]{2,1,0:T(8,128)(2,1)} %param.12) | copy-start | bytes 3145732
  2.6 9.2 %collective-permute-start = (bf16[128,1024]{1,0:T(8,128)(2,1)S(1)}, bf16[128,1024]{1,0:T(8,128)(2,1)S(1)}, u32[]{:S(2)}, u32[]{:S(2)}) collective-permute-start(bf16[128,1024]{1,0:T(8,128)(2,1)S(1)} %get-tuple-element.27), channel_id=1, source_target_pairs={{0,1},{1,0},{2,3},{3,2},{4,5},{5,4},{6,7},{7,6},{8,9},{9,8},{10,11... | collective-permute-start | bytes 786440 | tf_op jit(solution)/shard_map/ppermute | solution.py:525
  4.2 11.1 %collective-permute-start.1 = (bf16[128,1024]{1,0:T(8,128)(2,1)S(1)}, bf16[128,1024]{1,0:T(8,128)(2,1)S(1)}, u32[]{:S(2)}, u32[]{:S(2)}) collective-permute-start(bf16[128,1024]{1,0:T(8,128)(2,1)S(1)} %get-tuple-element.28), channel_id=1, source_target_pairs={{0,1},{1,0},{2,3},{3,2},{4,5},{5,4},{6,7},{7,6},{8,9},{9,8},{10,11... | collective-permute-start | bytes 786440 | tf_op jit(solution)/shard_map/ppermute | solution.py:525
  4.7 5.3 %collective-permute-start.5 = (bf16[256,128]{1,0:T(8,128)(2,1)S(1)}, bf16[256,128]{1,0:T(8,128)(2,1)S(1)}, u32[]{:S(2)}, u32[]{:S(2)}) collective-permute-start(bf16[256,128]{1,0:T(8,128)(2,1)S(1)} %copy-done.3), channel_id=1, source_target_pairs={{0,2},{1,3},{2,0},{3,1},{4,6},{5,7},{6,4},{7,5},{8,10},{9,11},{10,... | collective-permute-start | bytes 196616 | tf_op jit(solution)/shard_map/ppermute | solution.py:525
  9.9 7.3 %collective-permute-start.6 = (bf16[2,256,128]{2,1,0:T(8,128)(2,1)S(1)}, bf16[2,256,128]{2,1,0:T(8,128)(2,1)S(1)}, u32[]{:S(2)}, u32[]{:S(2)}) collective-permute-start(bf16[2,256,128]{2,1,0:T(8,128)(2,1)S(1)} %collect.2.refs_0_), channel_id=1, source_target_pairs={{0,4},{1,5},{2,6},{3,7},{4,0},{5,1},{6,2},{7,3},{8,12},{9,13},{10,... | collective-permute-start | bytes 393224 | tf_op jit(solution)/shard_map/ppermute | solution.py:525
  11.8 20.1 %collective-permute-start.3 = (bf16[128,1024]{1,0:T(8,128)(2,1)S(1)}, bf16[128,1024]{1,0:T(8,128)(2,1)S(1)}, u32[]{:S(2)}, u32[]{:S(2)}) collective-permute-start(bf16[128,1024]{1,0:T(8,128)(2,1)S(1)} %head.2), channel_id=1, source_target_pairs={{0,14},{1,15},{2,0},{3,1},{4,2},{5,3},{6,4},{7,5},{8,6},{9,7},{10,... | collective-permute-start | bytes 786440 | tf_op jit(solution)/shard_map/ppermute | solution.py:542
  15.3 15.0 %collective-permute-start.7 = (bf16[2,256,128]{2,1,0:T(8,128)(2,1)S(1)}, bf16[2,256,128]{2,1,0:T(8,128)(2,1)S(1)}, u32[]{:S(2)}, u32[]{:S(2)}) collective-permute-start(bf16[2,256,128]{2,1,0:T(8,128)(2,1)S(1)} %collect.2.refs_0_), channel_id=1, source_target_pairs={{0,8},{1,9},{2,10},{3,11},{4,12},{5,13},{6,14},{7,15},{8,0},{9,1},... | collective-permute-start | bytes 393224 | tf_op jit(solution)/shard_map/ppermute | solution.py:525
  15.3 15.0 %collective-permute-start.8 = (bf16[2,256,128]{2,1,0:T(8,128)(2,1)S(1)}, bf16[2,256,128]{2,1,0:T(8,128)(2,1)S(1)}, u32[]{:S(2)}, u32[]{:S(2)}) collective-permute-start(bf16[2,256,128]{2,1,0:T(8,128)(2,1)S(1)} %collect.2.refs_0_), channel_id=1, source_target_pairs={{0,12},{1,13},{2,14},{3,15},{4,8},{5,9},{6,10},{7,11},{8,4},{9,5},... | collective-permute-start | bytes 393224 | tf_op jit(solution)/shard_map/ppermute | solution.py:525
  17.3 15.7 %collective-permute-start.4 = (bf16[128,1024]{1,0:T(8,128)(2,1)S(1)}, bf16[128,1024]{1,0:T(8,128)(2,1)S(1)}, u32[]{:S(2)}, u32[]{:S(2)}) collective-permute-start(bf16[128,1024]{1,0:T(8,128)(2,1)S(1)} %head.3), channel_id=1, source_target_pairs={{2,0},{3,1},{4,2},{5,3},{6,4},{7,5},{8,6},{9,7},{10,8},{11,9},{12,... | collective-permute-start | bytes 786440 | tf_op jit(solution)/shard_map/ppermute | solution.py:542
  30.4 1.6 %copy-start = (bf16[256,256]{1,0:T(8,128)(2,1)S(1)}, bf16[256,256]{1,0:T(8,128)(2,1)}, u32[]{:S(2)}) copy-start(bf16[256,256]{1,0:T(8,128)(2,1)} %constant.19.clone.wi_ref.refs_4_) | copy-start | bytes 393220
  36.3 27.9 %collective-permute-start.9 = (bf16[128,2048]{1,0:T(8,128)(2,1)S(1)}, bf16[128,2048]{1,0:T(8,128)(2,1)S(1)}, u32[]{:S(2)}, u32[]{:S(2)}) collective-permute-start(bf16[128,2048]{1,0:T(8,128)(2,1)S(1)} %get-tuple-element.35), channel_id=1, source_target_pairs={{0,1},{1,0},{2,3},{3,2},{4,5},{5,4},{6,7},{7,6},{8,9},{9,8},{10,11... | collective-permute-start | bytes 1572872 | tf_op jit(solution)/shard_map/ppermute | solution.py:525
  36.4 5.0 %collective-permute-start.10 = (bf16[2,128,128]{2,1,0:T(8,128)(2,1)S(1)}, bf16[2,128,128]{2,1,0:T(8,128)(2,1)S(1)}, u32[]{:S(2)}, u32[]{:S(2)}) collective-permute-start(bf16[2,128,128]{2,1,0:T(8,128)(2,1)S(1)} %get-tuple-element.37), channel_id=1, source_target_pairs={{0,16},{1,17},{2,18},{3,19},{4,20},{5,21},{6,22},{7,23},{8,24},{9,... | collective-permute-start | bytes 196616 | tf_op jit(solution)/shard_map/ppermute | solution.py:525
  38.0 5.0 %collective-permute-start.11 = (bf16[2,128,128]{2,1,0:T(8,128)(2,1)S(1)}, bf16[2,128,128]{2,1,0:T(8,128)(2,1)S(1)}, u32[]{:S(2)}, u32[]{:S(2)}) collective-permute-start(bf16[2,128,128]{2,1,0:T(8,128)(2,1)S(1)} %get-tuple-element.38), channel_id=1, source_target_pairs={{0,2},{1,3},{2,0},{3,1},{4,6},{5,7},{6,4},{7,5},{8,10},{9,11},{10,... | collective-permute-start | bytes 196616 | tf_op jit(solution)/shard_map/ppermute | solution.py:525
  38.5 5.5 %collective-permute-start.12 = (bf16[2,128,128]{2,1,0:T(8,128)(2,1)S(1)}, bf16[2,128,128]{2,1,0:T(8,128)(2,1)S(1)}, u32[]{:S(2)}, u32[]{:S(2)}) collective-permute-start(bf16[2,128,128]{2,1,0:T(8,128)(2,1)S(1)} %get-tuple-element.39), channel_id=1, source_target_pairs={{0,18},{1,19},{2,16},{3,17},{4,22},{5,23},{6,20},{7,21},{8,26},{9,... | collective-permute-start | bytes 196616 | tf_op jit(solution)/shard_map/ppermute | solution.py:525
  40.0 4.9 %collective-permute-start.13 = (bf16[2,128,128]{2,1,0:T(8,128)(2,1)S(1)}, bf16[2,128,128]{2,1,0:T(8,128)(2,1)S(1)}, u32[]{:S(2)}, u32[]{:S(2)}) collective-permute-start(bf16[2,128,128]{2,1,0:T(8,128)(2,1)S(1)} %get-tuple-element.41), channel_id=1, source_target_pairs={{0,16},{1,17},{2,18},{3,19},{4,20},{5,21},{6,22},{7,23},{8,24},{9,... | collective-permute-start | bytes 196616 | tf_op jit(solution)/shard_map/ppermute | solution.py:525
  41.5 4.7 %collective-permute-start.14 = (bf16[2,128,128]{2,1,0:T(8,128)(2,1)S(1)}, bf16[2,128,128]{2,1,0:T(8,128)(2,1)S(1)}, u32[]{:S(2)}, u32[]{:S(2)}) collective-permute-start(bf16[2,128,128]{2,1,0:T(8,128)(2,1)S(1)} %get-tuple-element.42), channel_id=1, source_target_pairs={{0,2},{1,3},{2,0},{3,1},{4,6},{5,7},{6,4},{7,5},{8,10},{9,11},{10,... | collective-permute-start | bytes 196616 | tf_op jit(solution)/shard_map/ppermute | solution.py:525
  42.9 5.2 %collective-permute-start.15 = (bf16[2,128,128]{2,1,0:T(8,128)(2,1)S(1)}, bf16[2,128,128]{2,1,0:T(8,128)(2,1)S(1)}, u32[]{:S(2)}, u32[]{:S(2)}) collective-permute-start(bf16[2,128,128]{2,1,0:T(8,128)(2,1)S(1)} %get-tuple-element.43), channel_id=1, source_target_pairs={{0,18},{1,19},{2,16},{3,17},{4,22},{5,23},{6,20},{7,21},{8,26},{9,... | collective-permute-start | bytes 196616 | tf_op jit(solution)/shard_map/ppermute | solution.py:525
  48.2 7.1 %collective-permute-start.16 = (bf16[128,128]{1,0:T(8,128)(2,1)S(1)}, bf16[128,128]{1,0:T(8,128)(2,1)S(1)}, u32[]{:S(2)}, u32[]{:S(2)}) collective-permute-start(bf16[128,128]{1,0:T(8,128)(2,1)S(1)} %get-tuple-element.45), channel_id=1, source_target_pairs={{0,4},{1,5},{2,6},{3,7},{4,0},{5,1},{6,2},{7,3},{8,12},{9,13},{10,... | collective-permute-start | bytes 98312 | tf_op jit(solution)/shard_map/ppermute | solution.py:525
  52.8 4.8 %collective-permute-start.17 = (bf16[128,128]{1,0:T(8,128)(2,1)S(1)}, bf16[128,128]{1,0:T(8,128)(2,1)S(1)}, u32[]{:S(2)}, u32[]{:S(2)}) collective-permute-start(bf16[128,128]{1,0:T(8,128)(2,1)S(1)} %get-tuple-element.46), channel_id=1, source_target_pairs={{0,8},{1,9},{2,10},{3,11},{4,12},{5,13},{6,14},{7,15},{8,0},{9,1},... | collective-permute-start | bytes 98312 | tf_op jit(solution)/shard_map/ppermute | solution.py:525
  53.5 5.7 %collective-permute-start.18 = (bf16[128,128]{1,0:T(8,128)(2,1)S(1)}, bf16[128,128]{1,0:T(8,128)(2,1)S(1)}, u32[]{:S(2)}, u32[]{:S(2)}) collective-permute-start(bf16[128,128]{1,0:T(8,128)(2,1)S(1)} %get-tuple-element.47), channel_id=1, source_target_pairs={{0,12},{1,13},{2,14},{3,15},{4,8},{5,9},{6,10},{7,11},{8,4},{9,5},... | collective-permute-start | bytes 98312 | tf_op jit(solution)/shard_map/ppermute | solution.py:525
  59.3 4.3 %collective-permute-start.19 = (f32[128,128]{1,0:T(8,128)S(1)}, f32[128,128]{1,0:T(8,128)S(1)}, u32[]{:S(2)}, u32[]{:S(2)}) collective-permute-start(f32[128,128]{1,0:T(8,128)S(1)} %finish.1.mine_ref), channel_id=1, source_target_pairs={{0,16},{1,17},{2,18},{3,19},{4,20},{5,21},{6,22},{7,23},{8,24},{9,... | collective-permute-start | bytes 196616 | tf_op jit(solution)/shard_map/ppermute | solution.py:525
